TPU v7x, 128 devices: a whole 4x4x4 slice. The times are simulated.
128 devices in a mesh: layer: 2 (over y_hi), row: 8 (over y_lo, x), col: 8 (over z, core).
Axes of the slice: x: 4, y: 4 (y_hi: 2, y_lo: 2; y = y_hi * 2 + y_lo), z: 4, core: 2. Of those that a mesh axis runs over, the one named last changes fastest.
Arguments:
- weights: bfloat16 [16, 8192, 8192], P('layer', 'row', 'col'), may hold values from -6 to 6
- col_factor: bfloat16 [8192, 256], P('col'), may hold values from -0.0625 to 0.0625
- layer_factor: float32 [16, 4], P('layer'), may hold values from -1.5 to 1.5
- row_factor: float32 [8192, 256], P('row'), may hold values from -0.0625 to 0.0625
Outputs:
- row_update: float32 [8192, 256], P('row')
- core_out: float32 [256, 1024], replicated
All inputs are finite; a program needn't handle non-finite values.
Results may differ from a plain program's by a relative error of at most 0.0003.
Values sent between devices are 32-bit elements; how exact they have to be, the bound alone decides.
No kernel may reach another device: no remote copies, remote signals or barrier semaphores. Data moves between devices by JAX's collectives and lax.ppermute only.
A program may use at most 128 MiB of HBM per device.

v0:
```python
import jax
import jax.numpy as jnp
from jax import lax
from jax.sharding import PartitionSpec as P

R = 8192
RC = 256
RL = 4


highest = lax.Precision.HIGHEST


def inner(left, right):
    return lax.dot_general(
        left, right, (((0,), (0,)), ((), ())), precision=highest, preferred_element_type=jnp.float32
    )


def body(weights, col_factor, layer_factor, row_factor):
    width_scale = 1.0 / jnp.sqrt(jnp.float32(RL * RC))
    row_scale = 1.0 / jnp.sqrt(jnp.float32(R))
    rows_here = weights.shape[1]
    share = rows_here // lax.axis_size(("layer", "col"))
    projected = jnp.einsum("lrc,ck->lrk", weights, col_factor, preferred_element_type=jnp.float32)
    contracted = jnp.einsum("lrk,lm->rmk", projected, layer_factor, precision=highest)
    y_block = lax.psum_scatter(
        contracted.reshape(lax.axis_size(("layer", "col")) * share, RL * RC),
        ("layer", "col"),
        scatter_dimension=0,
        tiled=True,
    )
    position = lax.axis_index(("layer", "col"))
    local_rows = lax.dynamic_slice_in_dim(row_factor, position * share, share, 0)
    cross = lax.psum(inner(y_block, local_rows), ("layer", "row", "col"))
    z_rows = (
        jnp.dot(y_block, cross, precision=highest, preferred_element_type=jnp.float32) * width_scale
    )
    core_out = lax.psum(inner(z_rows, y_block) * row_scale, ("layer", "row", "col"))
    row_update = lax.all_gather(z_rows, ("layer", "col"), axis=0, tiled=True)
    return (row_update, core_out)


def solution(mesh):
    return jax.shard_map(
        body,
        mesh=mesh,
        in_specs=(P("layer", "row", "col"), P("col", None), P("layer", None), P("row", None)),
        out_specs=(P("row", None), P()),
        check_vma=False,
    )
```

profile of v0, /device:TPU:1, one launch (start us, length us, event | category | flops | bytes accessed | tf_op | source)
XLA Modules:
  0.0 485.6 jit_solution(18117699378010569194)
XLA Ops:
  7.2 0.0 copy-start
  7.2 0.0 copy-start.1
  7.2 0.0 reduce-scatter.2.cloned.1.call-start
  7.2 19.4 %fusion = f32[8,1024,256]{2,0,1:T(8,128)} fusion(bf16[8,1024,1024]{2,1,0:T(8,128)(2,1)} %param.4, bf16[1024,256]{1,0:T(8,128)(2,1)} %param.5), kind=kOutput, calls=%fused_computation | convolution fusion | flops 4294967296 | bytes 25690112 | tf_op jit(solution)/shard_map/lrc,ck->lrk/dot_general | solution.py:25
  26.6 0.0 copy-done.1
  26.6 9.4 %fusion.5 = f32[1024,256,4]{1,2,0:T(4,128)S(1)} fusion(f32[8,1024,256]{2,0,1:T(8,128)} %fusion, f32[8,4]{0,1:T(4,128)S(1)} %copy-done.1), kind=kOutput, calls=%fused_computation.7 | convolution fusion | flops 100663296 | bytes 12583040 | tf_op jit(solution)/shard_map/lrk,lm->rmk/dot_general | solution.py:26
  36.0 2.9 copy.7
  39.0 0.0 reduce-scatter.2.cloned.1.call-update
  39.0 0.0 all-reduce.3.cloned.1.call-start
  39.1 82.7 %reduce-scatter.2.cloned.1.call-done = f32[64,1024]{1,0:T(8,128)} async-done(((f32[1024,1024]{1,0:T(8,128)}), f32[64,1024]{1,0:T(8,128)}) %reduce-scatter.2.cloned.1.call-update) | async-done | bytes 262160 | tf_op jit(solution)/shard_map/reduce_scatter | solution.py:27
  121.8 0.0 copy-done
  121.8 2.9 fusion.3
  124.7 0.0 all-reduce.3.cloned.1.call-update
  124.7 0.0 all-gather.2.cloned.1.call-start
  124.8 150.9 %all-reduce.3.cloned.1.call-done = f32[1024,256]{1,0:T(8,128)} async-done(((f32[1024,256]{1,0:T(8,128)}), f32[1024,256]{1,0:T(8,128)}) %all-reduce.3.cloned.1.call-update) | async-done | bytes 1048592 | tf_op jit(solution)/shard_map/psum | solution.py:35
  275.7 2.6 convolution_multiply_fusion.1
  278.3 0.0 all-gather.2.cloned.1.call-update
  278.3 0.0 all-reduce.5.cloned.1.call-start
  278.3 3.0 convolution_multiply_fusion
  281.3 0.0 all-reduce.5.cloned.1.call-update
  281.4 41.2 %all-gather.2.cloned.1.call-done = f32[1024,256]{1,0:T(8,128)} async-done(((f32[64,256]{1,0:T(8,128)}), f32[1024,256]{1,0:T(8,128)}) %all-gather.2.cloned.1.call-update) | async-done | bytes 1048592 | tf_op jit(solution)/shard_map/all_gather | solution.py:40
  322.5 152.0 %all-reduce.5.cloned.1.call-done = f32[256,1024]{1,0:T(8,128)} async-done(((f32[256,1024]{1,0:T(8,128)}), f32[256,1024]{1,0:T(8,128)}) %all-reduce.5.cloned.1.call-update) | async-done | bytes 1048592 | tf_op jit(solution)/shard_map/psum | solution.py:39
  474.5 2.3 copy.13
  476.8 2.3 copy.14
Async XLA Ops:
  7.2 114.6 %copy-start = (f32[1024,256]{1,0:T(8,128)S(1)}, f32[1024,256]{1,0:T(8,128)}, u32[]{:S(2)}) copy-start(f32[1024,256]{1,0:T(8,128)} %param.7) | copy-start | bytes 3145732
  7.2 19.4 %copy-start.1 = (f32[8,4]{0,1:T(4,128)S(1)}, f32[8,4]{0,1:T(4,128)}, u32[]{:S(2)}) copy-start(f32[8,4]{0,1:T(4,128)} %param.6) | copy-start | bytes 388
  7.2 114.6 %reduce-scatter.2.cloned.1.call-start = ((), (), s32[]{:S(2)}) async-start(), calls=%async_computation.1 | async-start | bytes 4456448 | tf_op jit(solution)/shard_map/reduce_scatter | solution.py:27
  39.0 236.7 %all-reduce.3.cloned.1.call-start = ((), (), s32[]{:S(2)}) async-start(), calls=%async_computation.2 | async-start | bytes 2097152 | tf_op jit(solution)/shard_map/psum | solution.py:35
  124.7 197.8 %all-gather.2.cloned.1.call-start = ((), (), s32[]{:S(2)}) async-start(), calls=%async_computation.3 | async-start | bytes 1114112 | tf_op jit(solution)/shard_map/all_gather | solution.py:40
  278.3 196.3 %all-reduce.5.cloned.1.call-start = ((), (), s32[]{:S(2)}) async-start(), calls=%async_computation.4 | async-start | bytes 2097152 | tf_op jit(solution)/shard_map/psum | solution.py:39
Sparse Core Ops, SparseCore 0:
  39.1 82.5 reduce-scatter.1
  127.1 148.5 all-reduce.2
  278.7 43.7 all-gather.1
  327.7 146.7 all-reduce.4
where the time goes:
time: 486 us
  waiting for transfers between devices  427 us (88%)
  matrix products  37.3 us (8%)
  between operations  13.8 us (3%)
  local copies, waits for them, and re-layouts  7.52 us (2%)
    psum x1, waiting for transfers between devices, body(): lax.psum(inner(z_rows, y_block) * row_scale, ('layer', 'row', 'col'))  152 us
    psum x1, waiting for transfers between devices, body(): cross = lax.psum(inner(y_block, local_rows), ('layer', 'row', 'col'))  151 us
    reduce_scatter x1, waiting for transfers between devices, body(): lax.psum_scatter(contracted.reshape(lax.axis_size(('layer', 'col')) * sha...  82.7 us
    all_gather x1, waiting for transfers between devices, body(): row_update = lax.all_gather(z_rows, ('layer', 'col'), axis=0, tiled=True)  41.2 us
    dot_general x1, matrix products, body(): jnp.einsum('lrc,ck->lrk', weights, col_factor, preferred_element_type=jnp...  19.4 us
  transfers between devices with their start and end apart: 4, of which 4 were waited for; matrix products, arithmetic and copies ran while one was open for 1% of the time, Pallas kernels for 0%

commit v1 on v0

v1 whole, which is shorter than its diff:
```python
import jax
import jax.numpy as jnp
from jax import lax
from jax.experimental import pallas as pl
from jax.experimental.pallas import tpu as pltpu
from jax.sharding import Mesh, PartitionSpec as P

R = 8192
RC = 256
RL = 4

AXES = ("yhi", "ylo", "x", "z", "core")
CHIPS = AXES[:4]
TILE = 128
HALF = RL * RC // 2
f32 = jnp.float32
bf16 = jnp.bfloat16


def parts_of(v):
    hi = v.astype(bf16)
    return hi, (v - hi.astype(f32)).astype(bf16)


def dot3(a, b, dims):
    ah, al = parts_of(a)
    bh, bl = parts_of(b)

    def dot(p, q):
        return lax.dot_general(p, q, (dims, ((), ())), preferred_element_type=f32)

    return dot(ah, bh) + (dot(ah, bl) + dot(al, bh))


def to_tiles(ref, value):
    cols = value.shape[1] // 128
    for a in range(value.shape[0] // 8):
        for b in range(cols):
            ref[a * cols + b] = value[8 * a : 8 * a + 8, 128 * b : 128 * b + 128]


def contract_kernel(order, lf, w, c, send, keep, d):
    layers = w.shape[0]
    for l in range(layers):
        d[l] = jnp.dot(w[l], c[...], preferred_element_type=f32)
    for half, out in ((0, send), (1, keep)):
        for j in range(RL // 2):
            m = half * (RL // 2) + j
            acc = d[0] * lf[0, m]
            for l in range(1, layers):
                acc = acc + d[l] * lf[l, m]
            out[:, j * RC : (j + 1) * RC] = acc


def contract(order, lf, w, c, first, count):
    layers, _, cols = w.shape
    out = jax.ShapeDtypeStruct((count * TILE, HALF), f32)
    spec = pl.BlockSpec((TILE, HALF), lambda i, order: (i, 0))
    return pl.pallas_call(
        contract_kernel,
        out_shape=(out, out),
        grid_spec=pltpu.PrefetchScalarGridSpec(
            num_scalar_prefetch=1,
            grid=(count,),
            in_specs=[
                pl.BlockSpec(memory_space=pltpu.SMEM),
                pl.BlockSpec((layers, TILE, cols), lambda i, order: (0, order[first + i], 0)),
                pl.BlockSpec((cols, RC), lambda i, order: (0, 0)),
            ],
            out_specs=(spec, spec),
            scratch_shapes=[pltpu.VMEM((layers, TILE, RC), f32)],
        ),
        cost_estimate=pl.CostEstimate(
            flops=2 * layers * count * TILE * cols * RC,
            bytes_accessed=2 * layers * count * TILE * cols + 8 * count * TILE * HALF,
            transcendentals=0,
        ),
        name="contract",
    )(order, lf, w, c)


def cross_kernel(first, order, keep, recv, rf, *refs):
    prior = refs[0] if len(refs) == 4 else None
    va, vb, ct = refs[-3:]
    rows = [rf[pl.ds(pl.multiple_of(order[first + i] * TILE, TILE), TILE), :] for i in range(4)]
    total = None
    for out, at in ((va, 0), (vb, 1)):
        v = keep[at * 256 : at * 256 + 256] + recv[at * 256 : at * 256 + 256]
        out[...] = v
        f = jnp.concatenate(rows[2 * at : 2 * at + 2], axis=0)
        term = dot3(f, v, ((0,), (0,)))
        total = term if total is None else total + term
    cols = HALF // 128
    for a in range(RC // 8):
        for b in range(cols):
            t = total[8 * a : 8 * a + 8, 128 * b : 128 * b + 128]
            if prior is not None:
                t = t + prior[a * cols + b]
            ct[a * cols + b] = t


def cross_part(order, keep, recv, rf, first, prior):
    vmem = pl.BlockSpec(memory_space=pltpu.VMEM)
    ops = [keep, recv, rf] + ([] if prior is None else [prior])
    v = jax.ShapeDtypeStruct((256, HALF), f32)
    ct = jax.ShapeDtypeStruct((RC * HALF // 1024, 8, 128), f32)

    def kernel(*refs):
        cross_kernel(first, *refs)

    return pl.pallas_call(
        kernel,
        out_shape=(v, v, ct),
        in_specs=[pl.BlockSpec(memory_space=pltpu.SMEM)] + [vmem] * len(ops),
        out_specs=(vmem, vmem, vmem),
        cost_estimate=pl.CostEstimate(
            flops=6 * 512 * RC * HALF, bytes_accessed=8 << 20, transcendentals=0
        ),
        name="cross_part",
    )(order, *ops)


def rows_kernel(ct, ka, kb, zp, u, full):
    cols = HALF // 128
    for a in range(RC // 8):
        for b in range(cols):
            full[8 * a : 8 * a + 8, 128 * b : 128 * b + 128] = ct[a * cols + b]
    v = ka[...] + kb[...]
    u[...] = v
    zp[...] = dot3(v, full[...], ((1,), (1,)))


def core_kernel(zp, zr, u, z, ct):
    width_scale = 1.0 / jnp.sqrt(f32(RL * RC))
    row_scale = 1.0 / jnp.sqrt(f32(R))
    rows = (zp[...] + zr[...]) * width_scale
    z[...] = rows
    to_tiles(ct, dot3(rows, u[...], ((0,), (0,))) * row_scale)


def finish_kernel(core, mine, other, out):
    cols = HALF // 128
    for ref, at in ((mine, core[0]), (other, 1 - core[0])):
        base = at * HALF
        for b in range(cols):
            lane = pl.ds(pl.multiple_of(base + 128 * b, 128), 128)
            for a in range(RC // 8):
                out[8 * a : 8 * a + 8, lane] = ref[a * cols + b]


def whole(kernel, outs, n_in, scratch=(), smem=0, name=None):
    vmem = pl.BlockSpec(memory_space=pltpu.VMEM)
    return pl.pallas_call(
        kernel,
        out_shape=outs,
        in_specs=[pl.BlockSpec(memory_space=pltpu.SMEM)] * smem + [vmem] * n_in,
        out_specs=jax.tree.map(lambda _: vmem, outs),
        scratch_shapes=list(scratch),
        name=name,
    )


def shift(v, axis, size, by):
    return lax.ppermute(v, axis, [(i, (i + by) % size) for i in range(size)])


def sum_over_chips(tiles):
    n = lax.axis_size(CHIPS)
    v = tiles.reshape(n, -1, 128)
    v = lax.all_to_all(v, CHIPS, 0, 0, tiled=True)
    s = jnp.sum(v, axis=0)
    g = lax.all_to_all(jnp.broadcast_to(s, v.shape), CHIPS, 0, 0, tiled=True)
    return g.reshape(tiles.shape)


def body(weights, col_factor, layer_factor, row_factor):
    yhi, z, core = lax.axis_index("yhi"), lax.axis_index("z"), lax.axis_index("core")
    away = jnp.array([2, 2, 1, 1, 3, 3, 0, 0], jnp.int32)
    flip = jnp.array([1, 0] * 4, jnp.int32)
    order = ((z + away) % 4) * 2 + (yhi ^ flip)
    swapped = jnp.concatenate([layer_factor[:, RL // 2 :], layer_factor[:, : RL // 2]], axis=1)
    lf = jnp.where(core == 0, swapped, layer_factor)

    send1, keep1 = contract(order, lf, weights, col_factor, 0, 4)
    recv1 = shift(send1, "core", 2, 1)
    send2, keep2 = contract(order, lf, weights, col_factor, 4, 4)
    recv2 = shift(send2, "core", 2, 1)
    v2, v1, ct1 = cross_part(order, keep1, recv1, row_factor, 0, None)
    v3, v0, ct = cross_part(order, keep2, recv2, row_factor, 4, ct1)

    r2 = shift(v2, "z", 4, 2)
    r1 = shift(v1, "z", 4, 1)
    r3 = shift(v3, "z", 4, 3)
    cross = sum_over_chips(ct)
    block = v0 + r1 + r2 + r3
    ka = block[TILE:]
    kb = shift(block[:TILE], "yhi", 2, 1)

    out = jax.ShapeDtypeStruct
    zp, u = whole(
        rows_kernel,
        (out((TILE, RC), f32), out((TILE, HALF), f32)),
        3,
        [pltpu.VMEM((RC, HALF), f32)],
        name="rows_part",
    )(cross, ka, kb)
    zr = shift(zp, "core", 2, 1)
    zrows, ct = whole(
        core_kernel, (out((TILE, RC), f32), out(ct.shape, f32)), 3, name="core_part"
    )(zp, zr, u)

    mine = sum_over_chips(ct)
    other = shift(mine, "core", 2, 1)
    core_out = whole(
        finish_kernel, out((RC, 2 * HALF), f32), 2, smem=1, name="finish_core"
    )(core[None], mine, other)

    n = lax.axis_size(("z", "yhi"))
    part = lax.dynamic_slice_in_dim(zrows, core * (TILE // 2), TILE // 2, 0)
    got = lax.all_to_all(
        jnp.broadcast_to(part, (n,) + part.shape), ("z", "yhi"), 0, 0, tiled=True
    )
    more = shift(got, "core", 2, 1)
    pair = jnp.where(core == 0, jnp.stack([got, more], 1), jnp.stack([more, got], 1))
    return pair.reshape(n * TILE, RC), core_out


def solution(mesh):
    fine = Mesh(mesh.devices.reshape(2, 2, 4, 4, 2), AXES)
    return jax.shard_map(
        body,
        mesh=fine,
        in_specs=(
            P("yhi", ("ylo", "x"), ("z", "core")),
            P(("z", "core"), None),
            P("yhi", None),
            P(("ylo", "x"), None),
        ),
        out_specs=(P(("ylo", "x"), None), P()),
        check_vma=False,
    )
```

time: 486 us -> 156 us (0.32)
  waiting for transfers between devices: 427 us -> 41 us
  starting transfers between devices: 0.16 us -> 40.4 us
  matrix products: 37.3 us -> 0 us
  blocking collectives: 0 us -> 29.7 us
  Pallas kernels: 0 us -> 29.4 us
  between operations: 13.8 us -> 0.73 us
    psum x2 -> x0, waiting for transfers between devices: 303 us -> none  [the longest x1 152 us: body(): lax.psum(inner(z_rows, y_block) * row_scale, ('layer', 'row', 'col'))]
    reduce_scatter x1 -> x0, waiting for transfers between devices: 82.7 us -> none  [body(): lax.psum_scatter(contracted.reshape(lax.axis_size(('layer', 'col')) * sha...]
    all_gather x1 -> x0, waiting for transfers between devices: 41.2 us -> none  [body(): row_update = lax.all_gather(z_rows, ('layer', 'col'), axis=0, tiled=True)]
    dot_general x5 -> x0, matrix products: 37.3 us -> none  [the longest x1 19.4 us: body(): jnp.einsum('lrc,ck->lrk', weights, col_factor, preferred_element_type=jnp...]
    all_to_all x0 -> x1, blocking collectives: none -> 29.7 us  [sum_over_chips(): v = lax.all_to_all(v, CHIPS, 0, 0, tiled=True)]
    pallas_call x0 -> x7, Pallas kernels: none -> 29.4 us  [the longest x2 15.8 us: contract(): pl.pallas_call(contract_kernel, out_shape=(out, out), grid_spec=pltpu.Pre...]
    all_to_all x0 -> x4, waiting for transfers between devices: none -> 28.3 us  [the longest x1 11.4 us: sum_over_chips(): v = lax.all_to_all(v, CHIPS, 0, 0, tiled=True)]
    all_to_all x0 -> x4, starting transfers between devices: none -> 22.8 us  [the longest x2 12.6 us: sum_over_chips(): g = lax.all_to_all(jnp.broadcast_to(s, v.shape), CHIPS, 0, 0, tiled=True)]
  transfers between devices with their start and end apart: 4 -> 13, of which waited for: 4 -> 6; matrix products, arithmetic and copies ran while one was open for 1% -> 3% of each run, Pallas kernels for 0% -> 7%
where the time goes in v1:
time: 156 us; the launch traced here: 155 us
  waiting for transfers between devices  41 us (26%)
  starting transfers between devices  40.4 us (26%)
  blocking collectives  29.7 us (19%)
  Pallas kernels  29.4 us (19%)
  local copies, waits for them, and re-layouts  9.18 us (6%)
  other arithmetic  4.39 us (3%)
    all_to_all x1, blocking collectives, sum_over_chips(): v = lax.all_to_all(v, CHIPS, 0, 0, tiled=True)  29.7 us
    ppermute x9, starting transfers between devices, shift(): return lax.ppermute(v, axis, [(i, (i + by) % size) for i in range(size)])  17.6 us
    pallas_call x2, Pallas kernels, contract(): pl.pallas_call(contract_kernel, out_shape=(out, out), grid_spec=pltpu.Pre...  15.8 us
    ppermute x9, waiting for transfers between devices, shift(): return lax.ppermute(v, axis, [(i, (i + by) % size) for i in range(size)])  12.7 us
    all_to_all x2, starting transfers between devices, sum_over_chips(): g = lax.all_to_all(jnp.broadcast_to(s, v.shape), CHIPS, 0, 0, tiled=True)  12.6 us
    all_to_all x1, waiting for transfers between devices, sum_over_chips(): v = lax.all_to_all(v, CHIPS, 0, 0, tiled=True)  11.4 us
    all_to_all x1, waiting for transfers between devices, body(): lax.all_to_all(jnp.broadcast_to(part, (n,) + part.shape), ('z', 'yhi'), 0...  9.28 us
    all_to_all x2, waiting for transfers between devices, sum_over_chips(): g = lax.all_to_all(jnp.broadcast_to(s, v.shape), CHIPS, 0, 0, tiled=True)  7.64 us
  transfers between devices with their start and end apart: 13, of which 6 were waited for; matrix products, arithmetic and copies ran while one was open for 3% of the time, Pallas kernels for 7%

profile of v1, /device:TPU:1, one launch (start us, length us, event | category | flops | bytes accessed | tf_op | source)
XLA Modules:
  0.0 154.7 jit_solution(15327477952263960938)
XLA Ops:
  2.1 1.2 fusion.2.order.refs_0_
  3.4 7.9 %contract.3 = (f32[512,512]{1,0:T(8,128)}, f32[512,512]{1,0:T(8,128)}) custom-call(s32[8]{0:T(128)} %fusion.2.order.refs_0_, f32[8,4]{1,0:T(8,128)} %maximum_select_fusion.1.lf, bf16[8,1024,1024]{2,1,0:T(8,128)(2,1)} %w.3, bf16[1024,256]{1,0:T(8,128)(2,1)} %c.3), custom_call_target="tpu_custom_call" | custom-call | flops 2147483648 | bytes 10485760 | tf_op jit(solution)/shard_map/contract/pallas_call | solution.py:59
  11.3 1.4 collective-permute-start.1
  12.7 7.9 %contract.2 = (f32[512,512]{1,0:T(8,128)}, f32[512,512]{1,0:T(8,128)}) custom-call(s32[8]{0:T(128)} %fusion.2.order.refs_0_, f32[8,4]{1,0:T(8,128)} %maximum_select_fusion.1.lf, bf16[8,1024,1024]{2,1,0:T(8,128)(2,1)} %w.3, bf16[1024,256]{1,0:T(8,128)(2,1)} %c.3), custom_call_target="tpu_custom_call" | custom-call | flops 2147483648 | bytes 10485760 | tf_op jit(solution)/shard_map/contract/pallas_call | solution.py:59
  21.5 3.3 %cross_part.2 = (f32[256,512]{1,0:T(8,128)}, f32[256,512]{1,0:T(8,128)}, f32[128,8,128]{2,1,0:T(8,128)}) custom-call(s32[8]{0:T(128)} %fusion.2.order.refs_0_, f32[512,512]{1,0:T(8,128)} %get-tuple-element.18.refs_1_, f32[512,512]{1,0:T(8,128)} %copy-done.2, f32[1024,256]{1,0:T(8,128)} %refs_3_.3), custom_call_target="tpu_custom_call" | custom-call | flops 402653184 | bytes 8388608 | tf_op jit(solution)/shard_map/cross_part/pallas_call | solution.py:111
  25.8 3.5 %cross_part.3 = (f32[256,512]{1,0:T(8,128)}, f32[256,512]{1,0:T(8,128)}, f32[128,8,128]{2,1,0:T(8,128)}) custom-call(s32[8]{0:T(128)} %fusion.2.order.refs_0_, f32[512,512]{1,0:T(8,128)} %get-tuple-element.16.refs_1_, f32[512,512]{1,0:T(8,128)} %copy-done.3, f32[1024,256]{1,0:T(8,128)} %refs_3_.3, f32[128,8,128]{2,1,0:T(8,128)} %get-tuple-element.20.refs_4_), custom_call_target="tpu_custom_call" | custom-call | flops 402653184 | bytes 8388608 | tf_op jit(solution)/shard_map/cross_part/pallas_call | solution.py:111
  29.3 3.9 %collective-permute-start.4 = (f32[256,512]{1,0:T(8,128)}, f32[256,512]{1,0:T(8,128)S(1)}, u32[]{:S(2)}, u32[]{:S(2)}) collective-permute-start(f32[256,512]{1,0:T(8,128)} %get-tuple-element.25), channel_id=1, source_target_pairs={{0,6},{2,0},{4,2},{6,4},{1,7},{3,1},{5,3},{7,5},{8,14},{10,8},{12,... | collective-permute-start | bytes 1572872 | tf_op jit(solution)/shard_map/ppermute | solution.py:164
  33.1 1.3 collective-permute-start.3
  34.4 29.7 %all_to_all.25 = f32[64,16,128]{2,1,0:T(8,128)S(1)} all-to-all(f32[64,16,128]{2,1,0:T(8,128)} %bitcast.15), channel_id=1, replica_groups=mesh['yhi'=2,'ylo'=2,'x'=4,'z'=4,'core'=2] {'yhi','ylo','x','z'}, dimensions={0} | all-to-all | bytes 1048576 | tf_op jit(solution)/shard_map/all_to_all | solution.py:170
  65.0 8.0 %all-to-all-start.1 = ((f32[64,16,128]{2,1,0:T(8,128)}), f32[64,16,128]{2,1,0:T(8,128)S(1)}, u32[]{:S(2)}, u32[]{:S(2)}) async-start(f32[64,16,128]{2,1,0:T(8,128)} %broadcast_in_dim.12), calls=%async_computation.1 | async-start | bytes 1048576 | tf_op jit(solution)/shard_map/all_to_all | solution.py:172
  73.0 1.3 add_add_fusion
  75.0 2.6 %collective-permute-start.5 = (f32[128,512]{1,0:T(8,128)S(1)}, f32[128,512]{1,0:T(8,128)S(1)}, u32[]{:S(2)}, u32[]{:S(2)}) collective-permute-start(f32[128,512]{1,0:T(8,128)S(1)} %get-tuple-element.30), channel_id=1, source_target_pairs={{0,64},{64,0},{1,65},{65,1},{2,66},{66,2},{3,67},{67,3},{4,68},{68... | collective-permute-start | bytes 786440 | tf_op jit(solution)/shard_map/ppermute | solution.py:164
  77.6 11.0 %collective-permute-done.5.kb = f32[128,512]{1,0:T(8,128)S(1)} collective-permute-done((f32[128,512]{1,0:T(8,128)S(1)}, f32[128,512]{1,0:T(8,128)S(1)}, u32[]{:S(2)}, u32[]{:S(2)}) %collective-permute-start.5) | collective-permute-done | bytes 262176 | tf_op jit(solution)/shard_map/ppermute | solution.py:164
  89.5 2.2 %rows_part.1 = (f32[128,256]{1,0:T(8,128)}, f32[128,512]{1,0:T(8,128)}) custom-call(f32[128,8,128]{2,1,0:T(8,128)} %bitcast.11, f32[128,512]{1,0:T(8,128)} %get-tuple-element.31.ka, f32[128,512]{1,0:T(8,128)} %copy-done.5), custom_call_target="tpu_custom_call" | custom-call | tf_op jit(solution)/shard_map/rows_part/pallas_call | solution.py:200
  94.6 2.3 %core_part.1 = (f32[128,256]{1,0:T(8,128)}, f32[128,8,128]{2,1,0:T(8,128)}) custom-call(f32[128,256]{1,0:T(8,128)} %get-tuple-element.26.zp, f32[128,256]{1,0:T(8,128)} %copy-done.6, f32[128,512]{1,0:T(8,128)} %get-tuple-element.27.u), custom_call_target="tpu_custom_call" | custom-call | tf_op jit(solution)/shard_map/core_part/pallas_call | solution.py:208
  96.9 6.7 %all-to-all-start.3 = ((f32[64,16,128]{2,1,0:T(8,128)}), f32[64,16,128]{2,1,0:T(8,128)S(1)}, u32[]{:S(2)}, u32[]{:S(2)}) async-start(f32[64,16,128]{2,1,0:T(8,128)} %bitcast.14), calls=%async_computation.3 | async-start | bytes 1048576 | tf_op jit(solution)/shard_map/all_to_all | solution.py:170
  104.5 11.4 %all-to-all-done.3 = f32[64,16,128]{2,1,0:T(8,128)S(1)} async-done(((f32[64,16,128]{2,1,0:T(8,128)}), f32[64,16,128]{2,1,0:T(8,128)S(1)}, u32[]{:S(2)}, u32[]{:S(2)}) %all-to-all-start.3) | async-done | bytes 524320 | tf_op jit(solution)/shard_map/all_to_all | solution.py:170
  116.8 3.5 %all-to-all-start.2 = ((f32[8,64,256]{2,1,0:T(8,128)}), f32[8,64,256]{2,1,0:T(8,128)S(1)}, u32[]{:S(2)}, u32[]{:S(2)}) async-start(f32[8,64,256]{2,1,0:T(8,128)} %broadcast_in_dim.13), calls=%async_computation.2 | async-start | bytes 1048576 | tf_op jit(solution)/shard_map/all_to_all | solution.py:220
  120.4 9.3 %all-to-all-done.2 = f32[8,64,256]{2,1,0:T(8,128)S(1)} async-done(((f32[8,64,256]{2,1,0:T(8,128)}), f32[8,64,256]{2,1,0:T(8,128)S(1)}, u32[]{:S(2)}, u32[]{:S(2)}) %all-to-all-start.2) | async-done | bytes 524320 | tf_op jit(solution)/shard_map/all_to_all | solution.py:220
  130.5 4.6 %all-to-all-start.4 = ((f32[64,16,128]{2,1,0:T(8,128)}), f32[64,16,128]{2,1,0:T(8,128)S(1)}, u32[]{:S(2)}, u32[]{:S(2)}) async-start(f32[64,16,128]{2,1,0:T(8,128)} %broadcast_in_dim.15), calls=%async_computation.4 | async-start | bytes 1048576 | tf_op jit(solution)/shard_map/all_to_all | solution.py:172
  135.1 3.2 %collective-permute-start.7 = (f32[8,64,256]{2,1,0:T(8,128)S(1)}, f32[8,64,256]{2,1,0:T(8,128)S(1)}, u32[]{:S(2)}, u32[]{:S(2)}) collective-permute-start(f32[8,64,256]{2,1,0:T(8,128)S(1)} %all-to-all-done.2), channel_id=1, source_target_pairs={{0,1},{1,0},{2,3},{3,2},{4,5},{5,4},{6,7},{7,6},{8,9},{9,8},{10,11... | collective-permute-start | bytes 1572872 | tf_op jit(solution)/shard_map/ppermute | solution.py:164
  138.3 7.6 %all-to-all-done.4 = f32[64,16,128]{2,1,0:T(8,128)S(1)} async-done(((f32[64,16,128]{2,1,0:T(8,128)}), f32[64,16,128]{2,1,0:T(8,128)S(1)}, u32[]{:S(2)}, u32[]{:S(2)}) %all-to-all-start.4) | async-done | bytes 524320 | tf_op jit(solution)/shard_map/all_to_all | solution.py:172
  145.9 4.2 %collective-permute-start.8 = (f32[128,8,128]{2,1,0:T(8,128)S(1)}, f32[128,8,128]{2,1,0:T(8,128)S(1)}, u32[]{:S(2)}, u32[]{:S(2)}) collective-permute-start(f32[128,8,128]{2,1,0:T(8,128)S(1)} %bitcast.9), channel_id=1, source_target_pairs={{0,1},{1,0},{2,3},{3,2},{4,5},{5,4},{6,7},{7,6},{8,9},{9,8},{10,11... | collective-permute-start | bytes 1572872 | tf_op jit(solution)/shard_map/ppermute | solution.py:164
  152.4 2.3 %finish_core.1 = f32[256,1024]{1,0:T(8,128)} custom-call(s32[1]{0:T(128)} %bitcast.5.core, f32[128,8,128]{2,1,0:T(8,128)} %bitcast.10, f32[128,8,128]{2,1,0:T(8,128)} %copy-done.4), custom_call_target="tpu_custom_call" | custom-call | tf_op jit(solution)/shard_map/finish_core/pallas_call | solution.py:214
  (37 shorter events, 13.8 us)
Async XLA Ops:
  11.3 9.3 %collective-permute-start.1 = (f32[512,512]{1,0:T(8,128)}, f32[512,512]{1,0:T(8,128)S(1)}, u32[]{:S(2)}, u32[]{:S(2)}) collective-permute-start(f32[512,512]{1,0:T(8,128)} %get-tuple-element.19), channel_id=1, source_target_pairs={{0,1},{1,0},{2,3},{3,2},{4,5},{5,4},{6,7},{7,6},{8,9},{9,8},{10,11... | collective-permute-start | bytes 3145736 | tf_op jit(solution)/shard_map/ppermute | solution.py:164
  20.5 4.3 %collective-permute-start = (f32[512,512]{1,0:T(8,128)}, f32[512,512]{1,0:T(8,128)S(1)}, u32[]{:S(2)}, u32[]{:S(2)}) collective-permute-start(f32[512,512]{1,0:T(8,128)} %get-tuple-element.17), channel_id=1, source_target_pairs={{0,1},{1,0},{2,3},{3,2},{4,5},{5,4},{6,7},{7,6},{8,9},{9,8},{10,11... | collective-permute-start | bytes 3145736 | tf_op jit(solution)/shard_map/ppermute | solution.py:164
  20.5 1.0 copy-start.2
  24.8 1.0 copy-start.3
  29.3 43.7 %collective-permute-start.4 = (f32[256,512]{1,0:T(8,128)}, f32[256,512]{1,0:T(8,128)S(1)}, u32[]{:S(2)}, u32[]{:S(2)}) collective-permute-start(f32[256,512]{1,0:T(8,128)} %get-tuple-element.25), channel_id=1, source_target_pairs={{0,6},{2,0},{4,2},{6,4},{1,7},{3,1},{5,3},{7,5},{8,14},{10,8},{12,... | collective-permute-start | bytes 1572872 | tf_op jit(solution)/shard_map/ppermute | solution.py:164
  33.1 39.9 %collective-permute-start.2 = (f32[256,512]{1,0:T(8,128)}, f32[256,512]{1,0:T(8,128)S(1)}, u32[]{:S(2)}, u32[]{:S(2)}) collective-permute-start(f32[256,512]{1,0:T(8,128)} %get-tuple-element.23), channel_id=1, source_target_pairs={{0,2},{2,4},{4,6},{6,0},{1,3},{3,5},{5,7},{7,1},{8,10},{10,12},{12... | collective-permute-start | bytes 1572872 | tf_op jit(solution)/shard_map/ppermute | solution.py:164
  33.1 39.9 %collective-permute-start.3 = (f32[256,512]{1,0:T(8,128)}, f32[256,512]{1,0:T(8,128)S(1)}, u32[]{:S(2)}, u32[]{:S(2)}) collective-permute-start(f32[256,512]{1,0:T(8,128)} %get-tuple-element.24), channel_id=1, source_target_pairs={{0,4},{2,6},{4,0},{6,2},{1,5},{3,7},{5,1},{7,3},{8,12},{10,14},{12... | collective-permute-start | bytes 1572872 | tf_op jit(solution)/shard_map/ppermute | solution.py:164
  65.0 23.6 %all-to-all-start.1 = ((f32[64,16,128]{2,1,0:T(8,128)}), f32[64,16,128]{2,1,0:T(8,128)S(1)}, u32[]{:S(2)}, u32[]{:S(2)}) async-start(f32[64,16,128]{2,1,0:T(8,128)} %broadcast_in_dim.12), calls=%async_computation.1 | async-start | bytes 1048576 | tf_op jit(solution)/shard_map/all_to_all | solution.py:172
  75.0 13.6 %collective-permute-start.5 = (f32[128,512]{1,0:T(8,128)S(1)}, f32[128,512]{1,0:T(8,128)S(1)}, u32[]{:S(2)}, u32[]{:S(2)}) collective-permute-start(f32[128,512]{1,0:T(8,128)S(1)} %get-tuple-element.30), channel_id=1, source_target_pairs={{0,64},{64,0},{1,65},{65,1},{2,66},{66,2},{3,67},{67,3},{4,68},{68... | collective-permute-start | bytes 786440 | tf_op jit(solution)/shard_map/ppermute | solution.py:164
  88.6 0.7 copy-start.5
  88.6 0.9 copy-start.1
  91.8 2.2 %collective-permute-start.6 = (f32[128,256]{1,0:T(8,128)}, f32[128,256]{1,0:T(8,128)S(1)}, u32[]{:S(2)}, u32[]{:S(2)}) collective-permute-start(f32[128,256]{1,0:T(8,128)} %get-tuple-element.26.zp), channel_id=1, source_target_pairs={{0,1},{1,0},{2,3},{3,2},{4,5},{5,4},{6,7},{7,6},{8,9},{9,8},{10,11... | collective-permute-start | bytes 393224 | tf_op jit(solution)/shard_map/ppermute | solution.py:164
  94.0 0.7 copy-start.6
  96.9 19.0 %all-to-all-start.3 = ((f32[64,16,128]{2,1,0:T(8,128)}), f32[64,16,128]{2,1,0:T(8,128)S(1)}, u32[]{:S(2)}, u32[]{:S(2)}) async-start(f32[64,16,128]{2,1,0:T(8,128)} %bitcast.14), calls=%async_computation.3 | async-start | bytes 1048576 | tf_op jit(solution)/shard_map/all_to_all | solution.py:170
  116.8 12.9 %all-to-all-start.2 = ((f32[8,64,256]{2,1,0:T(8,128)}), f32[8,64,256]{2,1,0:T(8,128)S(1)}, u32[]{:S(2)}, u32[]{:S(2)}) async-start(f32[8,64,256]{2,1,0:T(8,128)} %broadcast_in_dim.13), calls=%async_computation.2 | async-start | bytes 1048576 | tf_op jit(solution)/shard_map/all_to_all | solution.py:220
  130.5 15.5 %all-to-all-start.4 = ((f32[64,16,128]{2,1,0:T(8,128)}), f32[64,16,128]{2,1,0:T(8,128)S(1)}, u32[]{:S(2)}, u32[]{:S(2)}) async-start(f32[64,16,128]{2,1,0:T(8,128)} %broadcast_in_dim.15), calls=%async_computation.4 | async-start | bytes 1048576 | tf_op jit(solution)/shard_map/all_to_all | solution.py:172
  135.1 15.0 %collective-permute-start.7 = (f32[8,64,256]{2,1,0:T(8,128)S(1)}, f32[8,64,256]{2,1,0:T(8,128)S(1)}, u32[]{:S(2)}, u32[]{:S(2)}) collective-permute-start(f32[8,64,256]{2,1,0:T(8,128)S(1)} %all-to-all-done.2), channel_id=1, source_target_pairs={{0,1},{1,0},{2,3},{3,2},{4,5},{5,4},{6,7},{7,6},{8,9},{9,8},{10,11... | collective-permute-start | bytes 1572872 | tf_op jit(solution)/shard_map/ppermute | solution.py:164
  145.9 5.7 %copy-start = (f32[64,16,128]{2,1,0:T(8,128)}, f32[64,16,128]{2,1,0:T(8,128)S(1)}, u32[]{:S(2)}) copy-start(f32[64,16,128]{2,1,0:T(8,128)S(1)} %all-to-all-done.4) | copy-start | bytes 1572868
  145.9 5.7 %collective-permute-start.8 = (f32[128,8,128]{2,1,0:T(8,128)S(1)}, f32[128,8,128]{2,1,0:T(8,128)S(1)}, u32[]{:S(2)}, u32[]{:S(2)}) collective-permute-start(f32[128,8,128]{2,1,0:T(8,128)S(1)} %bitcast.9), channel_id=1, source_target_pairs={{0,1},{1,0},{2,3},{3,2},{4,5},{5,4},{6,7},{7,6},{8,9},{9,8},{10,11... | collective-permute-start | bytes 1572872 | tf_op jit(solution)/shard_map/ppermute | solution.py:164
  151.6 0.8 copy-start.4

commit v2 on v0

v2 whole, which is shorter than its diff:
```python
import functools

import jax
import jax.numpy as jnp
from jax import lax
from jax.experimental import pallas as pl
from jax.experimental.pallas import tpu as pltpu
from jax.sharding import Mesh, PartitionSpec as P


R = 8192
RC = 256
RL = 4

AXES = ("yhi", "ylo", "x", "z", "core")
PLANE = AXES[:3]
CHIPS = AXES[:4]
SUB = 64
BLOCK = 256
HALF = RL * RC // 2
COLS = HALF // 128
f32 = jnp.float32
bf16 = jnp.bfloat16
SMEM = pl.BlockSpec(memory_space=pltpu.SMEM)
VMEM = pl.BlockSpec(memory_space=pltpu.VMEM)
MIB = 1 << 20


def parts_of(v):
    hi = v.astype(bf16)
    return hi, (v - hi.astype(f32)).astype(bf16)


def dot3(a, b, dims):
    ah, al = parts_of(a)
    bh, bl = parts_of(b)

    def dot(p, q):
        return lax.dot_general(p, q, (dims, ((), ())), preferred_element_type=f32)

    return dot(ah, bh) + (dot(ah, bl) + dot(al, bh))


def call(kernel, outs, ops, smem=0, scratch=(), vmem=16, cost=None):
    return pl.pallas_call(
        kernel,
        out_shape=outs,
        in_specs=[SMEM] * smem + [VMEM] * (len(ops) - smem),
        out_specs=jax.tree.map(lambda _: VMEM, outs),
        scratch_shapes=list(scratch),
        compiler_params=pltpu.CompilerParams(vmem_limit_bytes=vmem * MIB),
        cost_estimate=cost,
    )(*ops)


def shape(*dims):
    return jax.ShapeDtypeStruct(dims, f32)


def half_block(i, where):
    k = i // 2
    away = jnp.where(k == 0, 2, jnp.where(k == 1, 1, jnp.where(k == 2, 3, 0)))
    flip = 1 - i % 2
    return ((where[0] + away) % 4) * 2 + (where[1] + flip) % 2


def contract_kernel(where, lf, w_a, w_b, c, send, keep, d):
    layers, rows, cols = w_a.shape
    per = rows // SUB
    for s in range(2 * per):
        w = (w_a, w_b)[s // per]
        at = (s % per) * SUB
        part = w[:, at : at + SUB, :].reshape(layers * SUB, cols)
        d[s] = jnp.dot(part, c[...], preferred_element_type=f32).reshape(layers, SUB, RC)
    theirs = (1 - where[2]) * (RL // 2)
    step = 16
    for s in range(2 * per):
        for r in range(0, SUB, step):
            v = [d[s, l, r : r + step, :] for l in range(layers)]
            for base, out in ((theirs, send), (RL // 2 - theirs, keep)):
                for j in range(RL // 2):
                    acc = v[0] * lf[base + j, 0]
                    for l in range(1, layers):
                        acc = acc + v[l] * lf[base + j, l]
                    out[s * SUB + r : s * SUB + r + step, j * RC : (j + 1) * RC] = acc


def contract(where, lf, w, c, first, count):
    layers, _, cols = w.shape
    out = shape(count * BLOCK, HALF)
    spec = pl.BlockSpec((BLOCK, HALF), lambda i, where: (i, 0))

    def half(n):
        return pl.BlockSpec(
            (layers, BLOCK // 2, cols),
            lambda i, where: (0, half_block(2 * (first + i) + n, where), 0),
        )

    return pl.pallas_call(
        contract_kernel,
        out_shape=(out, out),
        grid_spec=pltpu.PrefetchScalarGridSpec(
            num_scalar_prefetch=1,
            grid=(count,),
            in_specs=[SMEM, half(0), half(1), pl.BlockSpec((cols, RC), lambda i, where: (0, 0))],
            out_specs=(spec, spec),
            scratch_shapes=[pltpu.VMEM((BLOCK // SUB, layers, SUB, RC), f32)],
        ),
        compiler_params=pltpu.CompilerParams(vmem_limit_bytes=50 * MIB),
        cost_estimate=pl.CostEstimate(
            flops=2 * layers * count * BLOCK * cols * RC,
            bytes_accessed=2 * layers * count * BLOCK * cols + 8 * count * BLOCK * HALF,
            transcendentals=0,
        ),
        name="contract",
    )(where, lf, w, w, c)


def cross_kernel(first, count, where, keep, recv, rf, *refs):
    prior = refs[0] if len(refs) > count + 1 else None
    blocks, ct = refs[-count - 1 : -1], refs[-1]
    half = BLOCK // 2
    total = None
    for n, out in enumerate(blocks):
        v = keep[n * BLOCK : (n + 1) * BLOCK] + recv[n * BLOCK : (n + 1) * BLOCK]
        out[...] = v
        f = jnp.concatenate(
            [
                rf[pl.ds(pl.multiple_of(half_block(2 * (first + n) + h, where) * half, half), half), :]
                for h in range(2)
            ],
            axis=0,
        )
        term = dot3(f, v, ((0,), (0,)))
        total = term if total is None else total + term
    for a in range(RC // 8):
        for b in range(COLS):
            t = total[8 * a : 8 * a + 8, 128 * b : 128 * b + 128]
            if prior is not None:
                t = t + prior[a * COLS + b]
            ct[a * COLS + b] = t


def cross_part(where, keep, recv, rf, first, count, prior):
    ops = [where, keep, recv, rf] + ([] if prior is None else [prior])
    return call(
        functools.partial(cross_kernel, first, count),
        [shape(BLOCK, HALF)] * count + [shape(RC * HALF // 1024, 8, 128)],
        ops,
        smem=1,
        vmem=20,
        cost=pl.CostEstimate(
            flops=6 * count * BLOCK * RC * HALF, bytes_accessed=4 * MIB, transcendentals=0
        ),
    )


def rows_kernel(ct, ka, kb, zp, u, full):
    for a in range(RC // 8):
        for b in range(COLS):
            full[8 * a : 8 * a + 8, 128 * b : 128 * b + 128] = ct[a * COLS + b]
    v = ka[...] + kb[...]
    u[...] = v
    zp[...] = dot3(v, full[...], ((1,), (1,)))


def core_kernel(where, zp, zr, u, z, ct):
    width_scale = 1.0 / jnp.sqrt(f32(RL * RC))
    row_scale = 1.0 / jnp.sqrt(f32(R))
    rows = (zp[...] + zr[...]) * width_scale
    half = rows.shape[0] // 2
    mine = pl.ds(pl.multiple_of(where[2] * half, half), half)
    z[...] = (zp[mine] + zr[mine]) * width_scale
    core = dot3(rows, u[...], ((0,), (0,))) * row_scale
    for a in range(RC // 8):
        for b in range(COLS):
            ct[a * COLS + b] = core[8 * a : 8 * a + 8, 128 * b : 128 * b + 128]


def finish_core_kernel(where, mine, other, out):
    for ref, at in ((mine, where[2]), (other, 1 - where[2])):
        for b in range(COLS):
            lane = pl.ds(pl.multiple_of(at * HALF + 128 * b, 128), 128)
            for a in range(RC // 8):
                out[8 * a : 8 * a + 8, lane] = ref[a * COLS + b]


def finish_rows_kernel(where, mine, other, out):
    quarter = BLOCK // 4
    for ref, at in ((mine, where[2]), (other, 1 - where[2])):
        for k in range(4):
            base = ((where[0] + 4 - k) % 4) * BLOCK + at * quarter
            for n in range(2):
                row = base + (where[1] + n) % 2 * (BLOCK // 2)
                rows = pl.ds(pl.multiple_of(row, quarter), quarter)
                i = (2 * k + n) * quarter
                out[rows, :] = ref[i : i + quarter, :]


def block_kernel(v0, r2, r1, r3, away, keep):
    half = BLOCK // 2
    for out, at in ((away, 0), (keep, half)):
        at = pl.ds(at, half)
        out[...] = (v0[at] + r2[at]) + (r1[at] + r3[at])


def gathered_kernel(v, out):
    total = v[0]
    for i in range(1, v.shape[0]):
        total = total + v[i]
    out[...] = total


def spread_kernel(*refs):
    out = refs[-1]
    if len(refs) == 2:
        v = refs[0][0]
        for i in range(1, out.shape[0]):
            v = v + refs[0][i]
    else:
        s, s1, s2, s3 = (ref[...] for ref in refs[:-1])
        v = (s + s2) + (s1 + s3)
    for i in range(out.shape[0]):
        out[i] = v


def join_kernel(*refs):
    out = refs[-1]
    rows = refs[0].shape[0]
    for i, ref in enumerate(refs[:-1]):
        out[i * rows : (i + 1) * rows] = ref[...]


def shift(v, axis, size, by):
    return lax.ppermute(v, axis, [(i, (i + by) % size) for i in range(size)])


def exchange(v, axes):
    return lax.all_to_all(v, axes, 0, 0, tiled=True)


def sum_over_planes(tiles):
    n = lax.axis_size(PLANE)
    v = exchange(tiles.reshape(n, -1, 128), PLANE)
    s = call(gathered_kernel, shape(*v.shape[1:]), [v])
    s1, s2, s3 = (shift(s, "z", 4, k) for k in (1, 2, 3))
    b = call(spread_kernel, shape(*v.shape), [s, s1, s2, s3])
    return exchange(b, PLANE).reshape(tiles.shape)


def sum_over_chips(tiles):
    n = lax.axis_size(CHIPS)
    v = exchange(tiles.reshape(n, -1, 128), CHIPS)
    b = call(spread_kernel, shape(*v.shape), [v])
    return exchange(b, CHIPS).reshape(tiles.shape)


def body(weights, col_factor, layer_factor, row_factor):
    weights, col_factor = (pltpu.with_memory_space_constraint(v, pltpu.HBM) for v in (weights, col_factor))
    where = jnp.stack([lax.axis_index(a) for a in ("z", "yhi", "core")])
    lf = pltpu.with_memory_space_constraint(layer_factor.T, pltpu.HBM)

    send1, keep1 = contract(where, lf, weights, col_factor, 0, 3)
    recv1 = shift(send1, "core", 2, 1)
    send2, keep2 = contract(where, lf, weights, col_factor, 3, 1)
    recv2 = shift(send2, "core", 2, 1)
    v2, v1, v3, ct = cross_part(where, keep1, recv1, row_factor, 0, 3, None)
    r2 = shift(v2, "z", 4, 2)
    r1 = shift(v1, "z", 4, 1)
    r3 = shift(v3, "z", 4, 3)
    v0, ct = cross_part(where, keep2, recv2, row_factor, 3, 1, ct)
    cross = sum_over_planes(ct)

    rows = BLOCK // 2
    away, ka = call(block_kernel, [shape(rows, HALF)] * 2, [v0, r2, r1, r3])
    kb = shift(away, "yhi", 2, 1)

    zp, u = call(
        rows_kernel,
        [shape(rows, RC), shape(rows, HALF)],
        [cross, ka, kb],
        scratch=[pltpu.VMEM((RC, HALF), f32)],
    )
    zr = shift(zp, "core", 2, 1)
    z, ct = call(core_kernel, [shape(rows // 2, RC), shape(*ct.shape)], [where, zp, zr, u], smem=1)

    zy = shift(z, "yhi", 2, 1)
    both = call(join_kernel, shape(rows, RC), [z, zy])
    gathered = [both] + [shift(both, "z", 4, k) for k in (1, 2, 3)]
    four = call(join_kernel, shape(4 * rows, RC), gathered)
    other = shift(four, "core", 2, 1)
    row_update = call(finish_rows_kernel, shape(8 * rows, RC), [where, four, other], smem=1)

    mine = sum_over_chips(ct)
    other = shift(mine, "core", 2, 1)
    core_out = call(finish_core_kernel, shape(RC, 2 * HALF), [where, mine, other], smem=1)
    return row_update, core_out


def solution(mesh):
    fine = Mesh(mesh.devices.reshape(2, 2, 4, 4, 2), AXES)
    return jax.shard_map(
        body,
        mesh=fine,
        in_specs=(
            P("yhi", ("ylo", "x"), ("z", "core")),
            P(("z", "core"), None),
            P("yhi", None),
            P(("ylo", "x"), None),
        ),
        out_specs=(P(("ylo", "x"), None), P()),
        check_vma=False,
    )
```

time: 486 us -> 134 us (0.28)
  waiting for transfers between devices: 427 us -> 40.7 us
  starting transfers between devices: 0.16 us -> 49.1 us
  matrix products: 37.3 us -> 0 us
  Pallas kernels: 0 us -> 23.5 us
  blocking collectives: 0 us -> 19.8 us
  between operations: 13.8 us -> 0.76 us
  local copies, waits for them, and re-layouts: 7.52 us -> 0.01 us
    psum x2 -> x0, waiting for transfers between devices: 303 us -> none  [the longest x1 152 us: body(): lax.psum(inner(z_rows, y_block) * row_scale, ('layer', 'row', 'col'))]
    reduce_scatter x1 -> x0, waiting for transfers between devices: 82.7 us -> none  [body(): lax.psum_scatter(contracted.reshape(lax.axis_size(('layer', 'col')) * sha...]
    all_gather x1 -> x0, waiting for transfers between devices: 41.2 us -> none  [body(): row_update = lax.all_gather(z_rows, ('layer', 'col'), axis=0, tiled=True)]
    dot_general x5 -> x0, matrix products: 37.3 us -> none  [the longest x1 19.4 us: body(): jnp.einsum('lrc,ck->lrk', weights, col_factor, preferred_element_type=jnp...]
    ppermute x0 -> x16, waiting for transfers between devices: none -> 36.5 us  [shift(): return lax.ppermute(v, axis, [(i, (i + by) % size) for i in range(size)])]
    ppermute x0 -> x16, starting transfers between devices: none -> 31 us  [shift(): return lax.ppermute(v, axis, [(i, (i + by) % size) for i in range(size)])]
    pallas_call x0 -> x14, Pallas kernels: none -> 23.5 us  [the longest x2 13.2 us: contract(): pl.pallas_call(contract_kernel, out_shape=(out, out), grid_spec=pltpu.Pre...]
    all_to_all x0 -> x1, blocking collectives: none -> 19.8 us  [exchange(): return lax.all_to_all(v, axes, 0, 0, tiled=True)]
  transfers between devices with their start and end apart: 4 -> 19, of which waited for: 4 -> 9; matrix products, arithmetic and copies ran while one was open for 1% -> 0% of each run, Pallas kernels for 0% -> 7%
where the time goes in v2:
time: 134 us
  starting transfers between devices  49.1 us (37%)
  waiting for transfers between devices  40.7 us (30%)
  Pallas kernels  23.5 us (18%)
  blocking collectives  19.8 us (15%)
    ppermute x16, waiting for transfers between devices, shift(): return lax.ppermute(v, axis, [(i, (i + by) % size) for i in range(size)])  36.5 us
    ppermute x16, starting transfers between devices, shift(): return lax.ppermute(v, axis, [(i, (i + by) % size) for i in range(size)])  31 us
    all_to_all x1, blocking collectives, exchange(): return lax.all_to_all(v, axes, 0, 0, tiled=True)  19.8 us
    all_to_all x3, starting transfers between devices, exchange(): return lax.all_to_all(v, axes, 0, 0, tiled=True)  18.1 us
    pallas_call x2, Pallas kernels, contract(): pl.pallas_call(contract_kernel, out_shape=(out, out), grid_spec=pltpu.Pre...  13.2 us
    pallas_call x12, Pallas kernels, call(): pl.pallas_call(kernel, out_shape=outs, in_specs=[SMEM] * smem + [VMEM] *...  10.3 us
    all_to_all x3, waiting for transfers between devices, exchange(): return lax.all_to_all(v, axes, 0, 0, tiled=True)  4.28 us
  transfers between devices with their start and end apart: 19, of which 9 were waited for; matrix products, arithmetic and copies ran while one was open for 0% of the time, Pallas kernels for 7%

profile of v2, /device:TPU:1, one launch (start us, length us, event | category | flops | bytes accessed | tf_op | source)
XLA Modules:
  0.0 134.0 jit_solution(6015190891576381236)
XLA Ops:
  0.7 8.7 %contract.3 = (f32[768,512]{1,0:T(8,128)S(1)}, f32[768,512]{1,0:T(8,128)S(1)}) custom-call(s32[3]{0:T(128)S(1)} %pad_add_fusion.where, f32[4,8]{1,0:T(4,128)} %bitcast.12, bf16[8,1024,1024]{2,1,0:T(8,128)(2,1)} %w_b.3, bf16[8,1024,1024]{2,1,0:T(8,128)(2,1)} %w_b.3, bf16[1024,256]{1,0:T(8,128)(2,1)} %c.3), custom_call_target="tpu_custom_call" | custom-call | flops 3221225472 | bytes 15728640 | tf_op jit(solution)/shard_map/contract/pallas_call | solution.py:99
  10.9 4.5 %contract.2 = (f32[256,512]{1,0:T(8,128)S(1)}, f32[256,512]{1,0:T(8,128)S(1)}) custom-call(s32[3]{0:T(128)S(1)} %pad_add_fusion.where, f32[4,8]{1,0:T(4,128)} %bitcast.13, bf16[8,1024,1024]{2,1,0:T(8,128)(2,1)} %w_b.3, bf16[8,1024,1024]{2,1,0:T(8,128)(2,1)} %w_b.3, bf16[1024,256]{1,0:T(8,128)(2,1)} %c.3), custom_call_target="tpu_custom_call" | custom-call | flops 1073741824 | bytes 5242880 | tf_op jit(solution)/shard_map/contract/pallas_call | solution.py:99
  15.6 2.0 %shard_map.59 = (f32[256,512]{1,0:T(8,128)}, f32[256,512]{1,0:T(8,128)}, f32[256,512]{1,0:T(8,128)S(1)}, f32[128,8,128]{2,1,0:T(8,128)S(1)}) custom-call(s32[3]{0:T(128)S(1)} %pad_add_fusion.where, f32[768,512]{1,0:T(8,128)S(1)} %get-tuple-element.20.keep, f32[768,512]{1,0:T(8,128)S(1)} %collective-permute-done.1.recv, f32[1024,256]{1,0:T(8,128)S(1)} %copy-done), custom_call_target="tpu_custom_call" | custom-call | flops 603979776 | bytes 4194304 | tf_op jit(solution)/shard_map/pallas_call | solution.py:45
  17.6 1.8 %shard_map.60 = (f32[256,512]{1,0:T(8,128)S(1)}, f32[128,8,128]{2,1,0:T(8,128)}) custom-call(s32[3]{0:T(128)S(1)} %pad_add_fusion.where, f32[256,512]{1,0:T(8,128)S(1)} %get-tuple-element.18.keep, f32[256,512]{1,0:T(8,128)S(1)} %collective-permute-done.recv, f32[1024,256]{1,0:T(8,128)S(1)} %copy-done, f32[128,8,128]{2,1,0:T(8,128)S(1)} %get-tuple-element.22.refs_0_), custom_call_target="tpu_custom_call" | custom-call | flops 201326592 | bytes 4194304 | tf_op jit(solution)/shard_map/pallas_call | solution.py:45
  19.3 6.9 %all-to-all-start = ((f32[16,64,128]{2,1,0:T(8,128)}), f32[16,64,128]{2,1,0:T(8,128)S(1)}, u32[]{:S(2)}, u32[]{:S(2)}) async-start(f32[16,64,128]{2,1,0:T(8,128)} %bitcast.4), calls=%async_computation | async-start | bytes 1048576 | tf_op jit(solution)/shard_map/all_to_all | solution.py:239
  26.2 3.7 %collective-permute-start.5 = (f32[256,512]{1,0:T(8,128)}, f32[256,512]{1,0:T(8,128)S(1)}, u32[]{:S(2)}, u32[]{:S(2)}) collective-permute-start(f32[256,512]{1,0:T(8,128)} %get-tuple-element.25), channel_id=1, source_target_pairs={{0,4},{2,6},{4,0},{6,2},{1,5},{3,7},{5,1},{7,3},{8,12},{10,14},{12... | collective-permute-start | bytes 1572872 | tf_op jit(solution)/shard_map/ppermute | solution.py:235
  30.6 1.9 %collective-permute-start.7 = (f32[256,512]{1,0:T(8,128)S(1)}, f32[256,512]{1,0:T(8,128)S(1)}, u32[]{:S(2)}, u32[]{:S(2)}) collective-permute-start(f32[256,512]{1,0:T(8,128)S(1)} %get-tuple-element.27), channel_id=1, source_target_pairs={{0,6},{2,0},{4,2},{6,4},{1,7},{3,1},{5,3},{7,5},{8,14},{10,8},{12,... | collective-permute-start | bytes 1572872 | tf_op jit(solution)/shard_map/ppermute | solution.py:235
  32.6 4.3 %all-to-all-done.v = f32[16,64,128]{2,1,0:T(8,128)S(1)} async-done(((f32[16,64,128]{2,1,0:T(8,128)}), f32[16,64,128]{2,1,0:T(8,128)S(1)}, u32[]{:S(2)}, u32[]{:S(2)}) %all-to-all-start) | async-done | bytes 524320 | tf_op jit(solution)/shard_map/all_to_all | solution.py:239
  36.9 1.7 %collective-permute-start.2 = (f32[64,128]{1,0:T(8,128)S(1)}, f32[64,128]{1,0:T(8,128)S(1)}, u32[]{:S(2)}, u32[]{:S(2)}) collective-permute-start(f32[64,128]{1,0:T(8,128)S(1)} %shard_map.61.refs_0_), channel_id=1, source_target_pairs={{0,2},{2,4},{4,6},{6,0},{1,3},{3,5},{5,7},{7,1},{8,10},{10,12},{12... | collective-permute-start | bytes 98312 | tf_op jit(solution)/shard_map/ppermute | solution.py:235
  38.6 3.3 %collective-permute-start.3 = (f32[64,128]{1,0:T(8,128)S(1)}, f32[64,128]{1,0:T(8,128)S(1)}, u32[]{:S(2)}, u32[]{:S(2)}) collective-permute-start(f32[64,128]{1,0:T(8,128)S(1)} %shard_map.61.refs_0_), channel_id=1, source_target_pairs={{0,4},{2,6},{4,0},{6,2},{1,5},{3,7},{5,1},{7,3},{8,12},{10,14},{12... | collective-permute-start | bytes 98312 | tf_op jit(solution)/shard_map/ppermute | solution.py:235
  41.9 12.9 %collective-permute-done.2.refs_1_ = f32[64,128]{1,0:T(8,128)S(1)} collective-permute-done((f32[64,128]{1,0:T(8,128)S(1)}, f32[64,128]{1,0:T(8,128)S(1)}, u32[]{:S(2)}, u32[]{:S(2)}) %collective-permute-start.2) | collective-permute-done | bytes 32800 | tf_op jit(solution)/shard_map/ppermute | solution.py:235
  54.8 2.8 %collective-permute-done.4.refs_3_ = f32[64,128]{1,0:T(8,128)S(1)} collective-permute-done((f32[64,128]{1,0:T(8,128)S(1)}, f32[64,128]{1,0:T(8,128)S(1)}, u32[]{:S(2)}, u32[]{:S(2)}) %collective-permute-start.4) | collective-permute-done | bytes 32800 | tf_op jit(solution)/shard_map/ppermute | solution.py:235
  58.4 6.6 %all-to-all-start.1 = ((f32[16,64,128]{2,1,0:T(8,128)}), f32[16,64,128]{2,1,0:T(8,128)S(1)}, u32[]{:S(2)}, u32[]{:S(2)}) async-start(f32[16,64,128]{2,1,0:T(8,128)} %shard_map.62), calls=%async_computation.1 | async-start | bytes 1048576 | tf_op jit(solution)/shard_map/all_to_all | solution.py:239
  65.1 2.9 %collective-permute-start.8 = (f32[128,512]{1,0:T(8,128)S(1)}, f32[128,512]{1,0:T(8,128)S(1)}, u32[]{:S(2)}, u32[]{:S(2)}) collective-permute-start(f32[128,512]{1,0:T(8,128)S(1)} %get-tuple-element.29), channel_id=1, source_target_pairs={{0,64},{64,0},{1,65},{65,1},{2,66},{66,2},{3,67},{67,3},{4,68},{68... | collective-permute-start | bytes 786440 | tf_op jit(solution)/shard_map/ppermute | solution.py:235
  68.1 10.4 %collective-permute-done.8.kb = f32[128,512]{1,0:T(8,128)S(1)} collective-permute-done((f32[128,512]{1,0:T(8,128)S(1)}, f32[128,512]{1,0:T(8,128)S(1)}, u32[]{:S(2)}, u32[]{:S(2)}) %collective-permute-start.8) | collective-permute-done | bytes 262176 | tf_op jit(solution)/shard_map/ppermute | solution.py:235
  78.9 2.6 %collective-permute-start.9 = (f32[128,256]{1,0:T(8,128)S(1)}, f32[128,256]{1,0:T(8,128)S(1)}, u32[]{:S(2)}, u32[]{:S(2)}) collective-permute-start(f32[128,256]{1,0:T(8,128)S(1)} %get-tuple-element.30.zp), channel_id=1, source_target_pairs={{0,1},{1,0},{2,3},{3,2},{4,5},{5,4},{6,7},{7,6},{8,9},{9,8},{10,11... | collective-permute-start | bytes 393224 | tf_op jit(solution)/shard_map/ppermute | solution.py:235
  83.4 19.8 %all_to_all.20.refs_0_ = f32[64,16,128]{2,1,0:T(8,128)S(1)} all-to-all(f32[64,16,128]{2,1,0:T(8,128)S(1)} %bitcast.11), channel_id=1, replica_groups=mesh['yhi'=2,'ylo'=2,'x'=4,'z'=4,'core'=2] {'yhi','ylo','x','z'}, dimensions={0} | all-to-all | bytes 1048576 | tf_op jit(solution)/shard_map/all_to_all | solution.py:239
  104.1 4.7 %all-to-all-start.3 = ((f32[64,16,128]{2,1,0:T(8,128)}), f32[64,16,128]{2,1,0:T(8,128)S(1)}, u32[]{:S(2)}, u32[]{:S(2)}) async-start(f32[64,16,128]{2,1,0:T(8,128)} %shard_map.69), calls=%async_computation.3 | async-start | bytes 1048576 | tf_op jit(solution)/shard_map/all_to_all | solution.py:239
  108.8 2.7 %collective-permute-start.10 = (f32[64,256]{1,0:T(8,128)S(1)}, f32[64,256]{1,0:T(8,128)S(1)}, u32[]{:S(2)}, u32[]{:S(2)}) collective-permute-start(f32[64,256]{1,0:T(8,128)S(1)} %get-tuple-element.32.refs_0_), channel_id=1, source_target_pairs={{0,64},{64,0},{1,65},{65,1},{2,66},{66,2},{3,67},{67,3},{4,68},{68... | collective-permute-start | bytes 196616 | tf_op jit(solution)/shard_map/ppermute | solution.py:235
  111.5 4.9 %collective-permute-done.10.refs_1_ = f32[64,256]{1,0:T(8,128)S(1)} collective-permute-done((f32[64,256]{1,0:T(8,128)S(1)}, f32[64,256]{1,0:T(8,128)S(1)}, u32[]{:S(2)}, u32[]{:S(2)}) %collective-permute-start.10) | collective-permute-done | bytes 65568 | tf_op jit(solution)/shard_map/ppermute | solution.py:235
  117.6 1.8 %collective-permute-start.12 = (f32[128,256]{1,0:T(8,128)S(1)}, f32[128,256]{1,0:T(8,128)S(1)}, u32[]{:S(2)}, u32[]{:S(2)}) collective-permute-start(f32[128,256]{1,0:T(8,128)S(1)} %shard_map.66.refs_0_), channel_id=1, source_target_pairs={{0,4},{2,6},{4,0},{6,2},{1,5},{3,7},{5,1},{7,3},{8,12},{10,14},{12... | collective-permute-start | bytes 393224 | tf_op jit(solution)/shard_map/ppermute | solution.py:235
  120.7 1.7 %collective-permute-done.11.refs_1_ = f32[128,256]{1,0:T(8,128)S(1)} collective-permute-done((f32[128,256]{1,0:T(8,128)S(1)}, f32[128,256]{1,0:T(8,128)S(1)}, u32[]{:S(2)}, u32[]{:S(2)}) %collective-permute-start.11) | collective-permute-done | bytes 131104 | tf_op jit(solution)/shard_map/ppermute | solution.py:235
  123.8 5.4 %collective-permute-start.14 = (f32[512,256]{1,0:T(8,128)S(1)}, f32[512,256]{1,0:T(8,128)S(1)}, u32[]{:S(2)}, u32[]{:S(2)}) collective-permute-start(f32[512,256]{1,0:T(8,128)S(1)} %shard_map.67.mine), channel_id=1, source_target_pairs={{0,1},{1,0},{2,3},{3,2},{4,5},{5,4},{6,7},{7,6},{8,9},{9,8},{10,11... | collective-permute-start | bytes 1572872 | tf_op jit(solution)/shard_map/ppermute | solution.py:235
  132.4 1.6 %shard_map.70 = f32[256,1024]{1,0:T(8,128)} custom-call(s32[3]{0:T(128)S(1)} %pad_add_fusion.where, f32[128,8,128]{2,1,0:T(8,128)S(1)} %bitcast.9, f32[128,8,128]{2,1,0:T(8,128)S(1)} %collective-permute-done.15.other), custom_call_target="tpu_custom_call" | custom-call | tf_op jit(solution)/shard_map/pallas_call | solution.py:45
  (32 shorter events, 13.8 us)
Async XLA Ops:
  9.4 6.1 %copy-start = (f32[1024,256]{1,0:T(8,128)S(1)}, f32[1024,256]{1,0:T(8,128)}, u32[]{:S(2)}) copy-start(f32[1024,256]{1,0:T(8,128)} %rf.3) | copy-start | bytes 3145732
  9.4 6.1 %collective-permute-start.1 = (f32[768,512]{1,0:T(8,128)S(1)}, f32[768,512]{1,0:T(8,128)S(1)}, u32[]{:S(2)}, u32[]{:S(2)}) collective-permute-start(f32[768,512]{1,0:T(8,128)S(1)} %get-tuple-element.21), channel_id=1, source_target_pairs={{0,1},{1,0},{2,3},{3,2},{4,5},{5,4},{6,7},{7,6},{8,9},{9,8},{10,11... | collective-permute-start | bytes 4718600 | tf_op jit(solution)/shard_map/ppermute | solution.py:235
  15.4 2.1 %collective-permute-start = (f32[256,512]{1,0:T(8,128)S(1)}, f32[256,512]{1,0:T(8,128)S(1)}, u32[]{:S(2)}, u32[]{:S(2)}) collective-permute-start(f32[256,512]{1,0:T(8,128)S(1)} %get-tuple-element.19), channel_id=1, source_target_pairs={{0,1},{1,0},{2,3},{3,2},{4,5},{5,4},{6,7},{7,6},{8,9},{9,8},{10,11... | collective-permute-start | bytes 1572872 | tf_op jit(solution)/shard_map/ppermute | solution.py:235
  19.3 17.5 %all-to-all-start = ((f32[16,64,128]{2,1,0:T(8,128)}), f32[16,64,128]{2,1,0:T(8,128)S(1)}, u32[]{:S(2)}, u32[]{:S(2)}) async-start(f32[16,64,128]{2,1,0:T(8,128)} %bitcast.4), calls=%async_computation | async-start | bytes 1048576 | tf_op jit(solution)/shard_map/all_to_all | solution.py:239
  26.2 38.8 %collective-permute-start.5 = (f32[256,512]{1,0:T(8,128)}, f32[256,512]{1,0:T(8,128)S(1)}, u32[]{:S(2)}, u32[]{:S(2)}) collective-permute-start(f32[256,512]{1,0:T(8,128)} %get-tuple-element.25), channel_id=1, source_target_pairs={{0,4},{2,6},{4,0},{6,2},{1,5},{3,7},{5,1},{7,3},{8,12},{10,14},{12... | collective-permute-start | bytes 1572872 | tf_op jit(solution)/shard_map/ppermute | solution.py:235
  29.9 35.1 %collective-permute-start.6 = (f32[256,512]{1,0:T(8,128)}, f32[256,512]{1,0:T(8,128)S(1)}, u32[]{:S(2)}, u32[]{:S(2)}) collective-permute-start(f32[256,512]{1,0:T(8,128)} %get-tuple-element.26), channel_id=1, source_target_pairs={{0,2},{2,4},{4,6},{6,0},{1,3},{3,5},{5,7},{7,1},{8,10},{10,12},{12... | collective-permute-start | bytes 1572872 | tf_op jit(solution)/shard_map/ppermute | solution.py:235
  30.6 34.4 %collective-permute-start.7 = (f32[256,512]{1,0:T(8,128)S(1)}, f32[256,512]{1,0:T(8,128)S(1)}, u32[]{:S(2)}, u32[]{:S(2)}) collective-permute-start(f32[256,512]{1,0:T(8,128)S(1)} %get-tuple-element.27), channel_id=1, source_target_pairs={{0,6},{2,0},{4,2},{6,4},{1,7},{3,1},{5,3},{7,5},{8,14},{10,8},{12,... | collective-permute-start | bytes 1572872 | tf_op jit(solution)/shard_map/ppermute | solution.py:235
  36.9 17.9 %collective-permute-start.2 = (f32[64,128]{1,0:T(8,128)S(1)}, f32[64,128]{1,0:T(8,128)S(1)}, u32[]{:S(2)}, u32[]{:S(2)}) collective-permute-start(f32[64,128]{1,0:T(8,128)S(1)} %shard_map.61.refs_0_), channel_id=1, source_target_pairs={{0,2},{2,4},{4,6},{6,0},{1,3},{3,5},{5,7},{7,1},{8,10},{10,12},{12... | collective-permute-start | bytes 98312 | tf_op jit(solution)/shard_map/ppermute | solution.py:235
  38.6 16.2 %collective-permute-start.3 = (f32[64,128]{1,0:T(8,128)S(1)}, f32[64,128]{1,0:T(8,128)S(1)}, u32[]{:S(2)}, u32[]{:S(2)}) collective-permute-start(f32[64,128]{1,0:T(8,128)S(1)} %shard_map.61.refs_0_), channel_id=1, source_target_pairs={{0,4},{2,6},{4,0},{6,2},{1,5},{3,7},{5,1},{7,3},{8,12},{10,14},{12... | collective-permute-start | bytes 98312 | tf_op jit(solution)/shard_map/ppermute | solution.py:235
  54.8 2.8 %collective-permute-start.4 = (f32[64,128]{1,0:T(8,128)S(1)}, f32[64,128]{1,0:T(8,128)S(1)}, u32[]{:S(2)}, u32[]{:S(2)}) collective-permute-start(f32[64,128]{1,0:T(8,128)S(1)} %shard_map.61.refs_0_), channel_id=1, source_target_pairs={{0,6},{2,0},{4,2},{6,4},{1,7},{3,1},{5,3},{7,5},{8,14},{10,8},{12,... | collective-permute-start | bytes 98312 | tf_op jit(solution)/shard_map/ppermute | solution.py:235
  58.4 20.1 %all-to-all-start.1 = ((f32[16,64,128]{2,1,0:T(8,128)}), f32[16,64,128]{2,1,0:T(8,128)S(1)}, u32[]{:S(2)}, u32[]{:S(2)}) async-start(f32[16,64,128]{2,1,0:T(8,128)} %shard_map.62), calls=%async_computation.1 | async-start | bytes 1048576 | tf_op jit(solution)/shard_map/all_to_all | solution.py:239
  65.1 13.3 %collective-permute-start.8 = (f32[128,512]{1,0:T(8,128)S(1)}, f32[128,512]{1,0:T(8,128)S(1)}, u32[]{:S(2)}, u32[]{:S(2)}) collective-permute-start(f32[128,512]{1,0:T(8,128)S(1)} %get-tuple-element.29), channel_id=1, source_target_pairs={{0,64},{64,0},{1,65},{65,1},{2,66},{66,2},{3,67},{67,3},{4,68},{68... | collective-permute-start | bytes 786440 | tf_op jit(solution)/shard_map/ppermute | solution.py:235
  78.9 3.6 %collective-permute-start.9 = (f32[128,256]{1,0:T(8,128)S(1)}, f32[128,256]{1,0:T(8,128)S(1)}, u32[]{:S(2)}, u32[]{:S(2)}) collective-permute-start(f32[128,256]{1,0:T(8,128)S(1)} %get-tuple-element.30.zp), channel_id=1, source_target_pairs={{0,1},{1,0},{2,3},{3,2},{4,5},{5,4},{6,7},{7,6},{8,9},{9,8},{10,11... | collective-permute-start | bytes 393224 | tf_op jit(solution)/shard_map/ppermute | solution.py:235
  104.1 25.2 %all-to-all-start.3 = ((f32[64,16,128]{2,1,0:T(8,128)}), f32[64,16,128]{2,1,0:T(8,128)S(1)}, u32[]{:S(2)}, u32[]{:S(2)}) async-start(f32[64,16,128]{2,1,0:T(8,128)} %shard_map.69), calls=%async_computation.3 | async-start | bytes 1048576 | tf_op jit(solution)/shard_map/all_to_all | solution.py:239
  108.8 7.6 %collective-permute-start.10 = (f32[64,256]{1,0:T(8,128)S(1)}, f32[64,256]{1,0:T(8,128)S(1)}, u32[]{:S(2)}, u32[]{:S(2)}) collective-permute-start(f32[64,256]{1,0:T(8,128)S(1)} %get-tuple-element.32.refs_0_), channel_id=1, source_target_pairs={{0,64},{64,0},{1,65},{65,1},{2,66},{66,2},{3,67},{67,3},{4,68},{68... | collective-permute-start | bytes 196616 | tf_op jit(solution)/shard_map/ppermute | solution.py:235
  116.4 6.0 %collective-permute-start.11 = (f32[128,256]{1,0:T(8,128)S(1)}, f32[128,256]{1,0:T(8,128)S(1)}, u32[]{:S(2)}, u32[]{:S(2)}) collective-permute-start(f32[128,256]{1,0:T(8,128)S(1)} %shard_map.66.refs_0_), channel_id=1, source_target_pairs={{0,2},{2,4},{4,6},{6,0},{1,3},{3,5},{5,7},{7,1},{8,10},{10,12},{12... | collective-permute-start | bytes 393224 | tf_op jit(solution)/shard_map/ppermute | solution.py:235
  117.6 6.2 %collective-permute-start.12 = (f32[128,256]{1,0:T(8,128)S(1)}, f32[128,256]{1,0:T(8,128)S(1)}, u32[]{:S(2)}, u32[]{:S(2)}) collective-permute-start(f32[128,256]{1,0:T(8,128)S(1)} %shard_map.66.refs_0_), channel_id=1, source_target_pairs={{0,4},{2,6},{4,0},{6,2},{1,5},{3,7},{5,1},{7,3},{8,12},{10,14},{12... | collective-permute-start | bytes 393224 | tf_op jit(solution)/shard_map/ppermute | solution.py:235
  119.4 4.4 %collective-permute-start.13 = (f32[128,256]{1,0:T(8,128)S(1)}, f32[128,256]{1,0:T(8,128)S(1)}, u32[]{:S(2)}, u32[]{:S(2)}) collective-permute-start(f32[128,256]{1,0:T(8,128)S(1)} %shard_map.66.refs_0_), channel_id=1, source_target_pairs={{0,6},{2,0},{4,2},{6,4},{1,7},{3,1},{5,3},{7,5},{8,14},{10,8},{12,... | collective-permute-start | bytes 393224 | tf_op jit(solution)/shard_map/ppermute | solution.py:235
  123.8 7.0 %collective-permute-start.14 = (f32[512,256]{1,0:T(8,128)S(1)}, f32[512,256]{1,0:T(8,128)S(1)}, u32[]{:S(2)}, u32[]{:S(2)}) collective-permute-start(f32[512,256]{1,0:T(8,128)S(1)} %shard_map.67.mine), channel_id=1, source_target_pairs={{0,1},{1,0},{2,3},{3,2},{4,5},{5,4},{6,7},{7,6},{8,9},{9,8},{10,11... | collective-permute-start | bytes 1572872 | tf_op jit(solution)/shard_map/ppermute | solution.py:235
  129.3 3.1 %collective-permute-start.15 = (f32[128,8,128]{2,1,0:T(8,128)S(1)}, f32[128,8,128]{2,1,0:T(8,128)S(1)}, u32[]{:S(2)}, u32[]{:S(2)}) collective-permute-start(f32[128,8,128]{2,1,0:T(8,128)S(1)} %bitcast.8), channel_id=1, source_target_pairs={{0,1},{1,0},{2,3},{3,2},{4,5},{5,4},{6,7},{7,6},{8,9},{9,8},{10,11... | collective-permute-start | bytes 1572872 | tf_op jit(solution)/shard_map/ppermute | solution.py:235

commit v3 on v2

v3 whole, which is shorter than its diff:
```python
import functools

import jax
import jax.numpy as jnp
from jax import lax
from jax.experimental import pallas as pl
from jax.experimental.pallas import tpu as pltpu
from jax.sharding import Mesh, PartitionSpec as P


R = 8192
RC = 256
RL = 4

AXES = ("yhi", "ylo", "x", "z", "core")
PLANE = AXES[:3]
CHIPS = AXES[:4]
SUB = 64
BLOCK = 256
HALF = RL * RC // 2
COLS = HALF // 128
f32 = jnp.float32
bf16 = jnp.bfloat16
SMEM = pl.BlockSpec(memory_space=pltpu.SMEM)
VMEM = pl.BlockSpec(memory_space=pltpu.VMEM)
MIB = 1 << 20


def parts_of(v):
    hi = v.astype(bf16)
    return hi, (v - hi.astype(f32)).astype(bf16)


def dot3(a, b, dims):
    ah, al = parts_of(a)
    bh, bl = parts_of(b)

    def dot(p, q):
        return lax.dot_general(p, q, (dims, ((), ())), preferred_element_type=f32)

    return dot(ah, bh) + (dot(ah, bl) + dot(al, bh))


def call(kernel, outs, ops, smem=0, scratch=(), vmem=16, cost=None):
    return pl.pallas_call(
        kernel,
        out_shape=outs,
        in_specs=[SMEM] * smem + [VMEM] * (len(ops) - smem),
        out_specs=jax.tree.map(lambda _: VMEM, outs),
        scratch_shapes=list(scratch),
        compiler_params=pltpu.CompilerParams(vmem_limit_bytes=vmem * MIB),
        cost_estimate=cost,
    )(*ops)


def shape(*dims):
    return jax.ShapeDtypeStruct(dims, f32)


def half_block(i):
    away = (2, 1, 3, 0)[i // 2]
    return ((lax.axis_index("z") + away) % 4) * 2 + (lax.axis_index("yhi") + 1 - i % 2) % 2


def mix_columns(lf, d, subs, send, keep):
    layers = d.shape[1]
    theirs = (1 - lax.axis_index("core")) * (RL // 2)
    step = 16
    for s in subs:
        for r in range(0, SUB, step):
            v = [d[s, l, r : r + step, :] for l in range(layers)]
            for base, out in ((theirs, send), (RL // 2 - theirs, keep)):
                for j in range(RL // 2):
                    acc = v[0] * lf[base + j, 0]
                    for l in range(1, layers):
                        acc = acc + v[l] * lf[base + j, l]
                    out[s * SUB + r : s * SUB + r + step, j * RC : (j + 1) * RC] = acc


def contract_kernel(lf, w, c, send, keep, ahead, c_copy, wbuf, d, sems):
    layers, _, cols = w.shape
    count, last = wbuf.shape[0], ahead.shape[0]
    per = BLOCK // 2 // SUB

    def copy(s):
        row = half_block(s // per) * (BLOCK // 2) + s % per * SUB
        rows = pl.ds(pl.multiple_of(row, SUB), SUB)
        target = wbuf.at[s] if s < count else ahead.at[s - count]
        return pltpu.make_async_copy(w.at[:, rows, :], target, sems.at[s])

    fetch = pltpu.make_async_copy(c, c_copy, sems.at[count + last])
    fetch.start()
    for s in range(count + last):
        copy(s).start()
    fetch.wait()
    at = 0
    for size in (1, 3) + (4,) * (count // 4 - 1):
        subs = range(at, at + size)
        for s in subs:
            copy(s).wait()
        for s in subs:
            part = wbuf[s].reshape(layers * SUB, cols)
            d[s] = jnp.dot(part, c_copy[...], preferred_element_type=f32).reshape(layers, SUB, RC)
        mix_columns(lf, d, subs, send, keep)
        at += size
    for s in range(count, count + last):
        copy(s).wait()


def contract(lf, w, c):
    layers, rows, cols = w.shape
    count = (rows - BLOCK) // SUB
    last = BLOCK // SUB
    out = shape(rows - BLOCK, HALF)
    hbm = pl.BlockSpec(memory_space=pl.ANY)
    return pl.pallas_call(
        contract_kernel,
        out_shape=(
            out,
            out,
            jax.ShapeDtypeStruct((last, layers, SUB, cols), bf16),
            jax.ShapeDtypeStruct(c.shape, bf16),
        ),
        in_specs=[SMEM, hbm, hbm],
        out_specs=(VMEM,) * 4,
        scratch_shapes=[
            pltpu.VMEM((count, layers, SUB, cols), bf16),
            pltpu.VMEM((count, layers, SUB, RC), f32),
            pltpu.SemaphoreType.DMA((count + last + 1,)),
        ],
        compiler_params=pltpu.CompilerParams(vmem_limit_bytes=40 * MIB),
        cost_estimate=pl.CostEstimate(
            flops=2 * layers * (rows - BLOCK) * cols * RC,
            bytes_accessed=2 * layers * rows * cols,
            transcendentals=0,
        ),
        name="contract",
    )(lf, w, c)


def contract_last_kernel(lf, w, c, send, keep, d):
    last, layers, _, cols = w.shape
    for s in range(last):
        part = w[s].reshape(layers * SUB, cols)
        d[s] = jnp.dot(part, c[...], preferred_element_type=f32).reshape(layers, SUB, RC)
    mix_columns(lf, d, range(last), send, keep)


def contract_last(lf, w, c):
    last, layers, _, cols = w.shape
    return call(
        contract_last_kernel,
        [shape(BLOCK, HALF)] * 2,
        [lf, w, c],
        smem=1,
        scratch=[pltpu.VMEM((last, layers, SUB, RC), f32)],
        cost=pl.CostEstimate(
            flops=2 * layers * BLOCK * cols * RC, bytes_accessed=MIB, transcendentals=0
        ),
    )


def cross_kernel(first, count, keep, recv, rf, *refs):
    prior = refs[0] if len(refs) > 2 * count + 1 else None
    blocks, ct = refs[-2 * count - 1 : -1], refs[-1]
    half = BLOCK // 2
    total = None
    for n in range(count):
        v = keep[n * BLOCK : (n + 1) * BLOCK] + recv[n * BLOCK : (n + 1) * BLOCK]
        blocks[2 * n][...] = v[:half]
        blocks[2 * n + 1][...] = v[half:]
        f = jnp.concatenate(
            [
                rf[pl.ds(pl.multiple_of(half_block(2 * (first + n) + h) * half, half), half), :]
                for h in range(2)
            ],
            axis=0,
        )
        term = dot3(f, v, ((0,), (0,)))
        total = term if total is None else total + term
    for a in range(RC // 8):
        for b in range(COLS):
            t = total[8 * a : 8 * a + 8, 128 * b : 128 * b + 128]
            if prior is not None:
                t = t + prior[a * COLS + b]
            ct[a * COLS + b] = t


def cross_part(keep, recv, rf, first, count, prior):
    ops = [keep, recv, rf] + ([] if prior is None else [prior])
    return call(
        functools.partial(cross_kernel, first, count),
        [shape(BLOCK // 2, HALF)] * (2 * count) + [shape(RC * HALF // 1024, 8, 128)],
        ops,
        vmem=20,
        cost=pl.CostEstimate(
            flops=6 * count * BLOCK * RC * HALF, bytes_accessed=4 * MIB, transcendentals=0
        ),
    )


def rows_kernel(ct, ka, kb, zp, u, full):
    for a in range(RC // 8):
        for b in range(COLS):
            full[8 * a : 8 * a + 8, 128 * b : 128 * b + 128] = ct[a * COLS + b]
    v = ka[...] + kb[...]
    u[...] = v
    zp[...] = dot3(v, full[...], ((1,), (1,)))


def core_kernel(zp, zr, u, z, ct):
    width_scale = 1.0 / jnp.sqrt(f32(RL * RC))
    row_scale = 1.0 / jnp.sqrt(f32(R))
    rows = (zp[...] + zr[...]) * width_scale
    half = rows.shape[0] // 2
    mine = pl.ds(pl.multiple_of(lax.axis_index("core") * half, half), half)
    z[...] = (zp[mine] + zr[mine]) * width_scale
    core = dot3(rows, u[...], ((0,), (0,))) * row_scale
    for a in range(RC // 8):
        for b in range(COLS):
            ct[a * COLS + b] = core[8 * a : 8 * a + 8, 128 * b : 128 * b + 128]


def finish_core_kernel(mine, other, out):
    core = lax.axis_index("core")
    for ref, at in ((mine, core), (other, 1 - core)):
        for b in range(COLS):
            lane = pl.ds(pl.multiple_of(at * HALF + 128 * b, 128), 128)
            for a in range(RC // 8):
                out[8 * a : 8 * a + 8, lane] = ref[a * COLS + b]


def finish_rows_kernel(mine, other, out):
    z, yhi, core = (lax.axis_index(a) for a in ("z", "yhi", "core"))
    quarter = BLOCK // 4
    for ref, at in ((mine, core), (other, 1 - core)):
        for k in range(4):
            base = ((z + 4 - k) % 4) * BLOCK + at * quarter
            for n in range(2):
                row = base + (yhi + n) % 2 * (BLOCK // 2)
                rows = pl.ds(pl.multiple_of(row, quarter), quarter)
                i = (2 * k + n) * quarter
                out[rows, :] = ref[i : i + quarter, :]


def relay_kernel(a, b, c, d, ab, cd):
    ab[...] = a[...] + b[...]
    cd[...] = c[...] + d[...]


def block_kernel(a0, a1, a2, b0, b1, b2, away, keep):
    away[...] = (a0[...] + a1[...]) + a2[...]
    keep[...] = (b0[...] + b1[...]) + b2[...]


def gathered_kernel(v, out):
    total = v[0]
    for i in range(1, v.shape[0]):
        total = total + v[i]
    out[...] = total


def spread_kernel(*refs):
    out = refs[-1]
    if len(refs) == 2:
        v = refs[0][0]
        for i in range(1, out.shape[0]):
            v = v + refs[0][i]
    else:
        s, s1, s2, s3 = (ref[...] for ref in refs[:-1])
        v = (s + s2) + (s1 + s3)
    for i in range(out.shape[0]):
        out[i] = v


def join_kernel(*refs):
    out = refs[-1]
    rows = refs[0].shape[0]
    for i, ref in enumerate(refs[:-1]):
        out[i * rows : (i + 1) * rows] = ref[...]


def shift(v, axis, size, by):
    return lax.ppermute(v, axis, [(i, (i + by) % size) for i in range(size)])


def exchange(v, axes):
    return lax.all_to_all(v, axes, 0, 0, tiled=True)


def sum_over_planes(tiles):
    n = lax.axis_size(PLANE)
    v = exchange(tiles.reshape(n, -1, 128), PLANE)
    s = call(gathered_kernel, shape(*v.shape[1:]), [v])
    s1, s2, s3 = (shift(s, "z", 4, k) for k in (1, 2, 3))
    b = call(spread_kernel, shape(*v.shape), [s, s1, s2, s3])
    return exchange(b, PLANE).reshape(tiles.shape)


def sum_over_chips(tiles):
    n = lax.axis_size(CHIPS)
    v = exchange(tiles.reshape(n, -1, 128), CHIPS)
    b = call(spread_kernel, shape(*v.shape), [v])
    return exchange(b, CHIPS).reshape(tiles.shape)


def body(weights, col_factor, layer_factor, row_factor):
    weights, col_factor = (pltpu.with_memory_space_constraint(v, pltpu.HBM) for v in (weights, col_factor))
    lf = pltpu.with_memory_space_constraint(layer_factor.T, pltpu.HBM)

    send1, keep1, ahead, factor = contract(lf, weights, col_factor)
    recv1 = shift(send1, "core", 2, 1)
    send2, keep2 = contract_last(lf, ahead, factor)
    recv2 = shift(send2, "core", 2, 1)
    v2a, v2b, v1a, v1b, v3a, v3b, ct = cross_part(keep1, recv1, row_factor, 0, 3, None)
    p1 = shift(v2a, "z", 4, 1)
    p2 = shift(v2b, "z", 4, 3)
    p3 = shift(v1b, "z", 4, 1)
    p4 = shift(v3a, "z", 4, 3)
    v0a, v0b, ct = cross_part(keep2, recv2, row_factor, 3, 1, ct)
    cross = sum_over_planes(ct)
    rows = BLOCK // 2
    s1, s3 = call(relay_kernel, [shape(rows, HALF)] * 2, [v1a, p1, v3b, p2])
    p5 = shift(s1, "z", 4, 1)
    p6 = shift(s3, "z", 4, 3)

    away, ka = call(block_kernel, [shape(rows, HALF)] * 2, [v0a, p5, p4, v0b, p3, p6])
    kb = shift(away, "yhi", 2, 1)

    zp, u = call(
        rows_kernel,
        [shape(rows, RC), shape(rows, HALF)],
        [cross, ka, kb],
        scratch=[pltpu.VMEM((RC, HALF), f32)],
    )
    zr = shift(zp, "core", 2, 1)
    z, ct = call(core_kernel, [shape(rows // 2, RC), shape(*ct.shape)], [zp, zr, u])

    zy = shift(z, "yhi", 2, 1)
    both = call(join_kernel, shape(rows, RC), [z, zy])
    gathered = [both] + [shift(both, "z", 4, k) for k in (1, 2, 3)]
    four = call(join_kernel, shape(4 * rows, RC), gathered)
    other = shift(four, "core", 2, 1)
    row_update = call(finish_rows_kernel, shape(8 * rows, RC), [four, other])

    mine = sum_over_chips(ct)
    other = shift(mine, "core", 2, 1)
    core_out = call(finish_core_kernel, shape(RC, 2 * HALF), [mine, other])
    return row_update, core_out


def solution(mesh):
    fine = Mesh(mesh.devices.reshape(2, 2, 4, 4, 2), AXES)
    return jax.shard_map(
        body,
        mesh=fine,
        in_specs=(
            P("yhi", ("ylo", "x"), ("z", "core")),
            P(("z", "core"), None),
            P("yhi", None),
            P(("ylo", "x"), None),
        ),
        out_specs=(P(("ylo", "x"), None), P()),
        check_vma=False,
    )
```

time: 134 us -> 125 us (0.933)
  Pallas kernels: 23.5 us -> 18.3 us
  starting transfers between devices: 49.1 us -> 46.3 us
    pallas_call x2 -> x1, Pallas kernels: 13.2 us -> 8.03 us  [contract(): pl.pallas_call(contract_kernel, out_shape=(out, out, jax.ShapeDtypeStruct...]
    ppermute x16 -> x19, waiting for transfers between devices: 36.5 us -> 33.7 us  [shift(): return lax.ppermute(v, axis, [(i, (i + by) % size) for i in range(size)])]
    all_to_all x3, waiting for transfers between devices: 4.28 us -> 7.02 us  [exchange(): return lax.all_to_all(v, axes, 0, 0, tiled=True)]
    all_to_all x3, starting transfers between devices: 18.1 us -> 15.5 us  [exchange(): return lax.all_to_all(v, axes, 0, 0, tiled=True)]
    ppermute x16 -> x19, starting transfers between devices: 31 us -> 30.7 us  [shift(): return lax.ppermute(v, axis, [(i, (i + by) % size) for i in range(size)])]
    pallas_call x12 -> x14, Pallas kernels: 10.3 us -> 10.2 us  [call(): pl.pallas_call(kernel, out_shape=outs, in_specs=[SMEM] * smem + [VMEM] *...]
  transfers between devices with their start and end apart: 19 -> 22, of which waited for: 9 -> 11; matrix products, arithmetic and copies ran while one was open for 0% -> 0% of each run, Pallas kernels for 7% -> 5%
where the time goes in v3:
time: 125 us
  starting transfers between devices  46.3 us (37%)
  waiting for transfers between devices  40.7 us (33%)
  blocking collectives  18.7 us (15%)
  Pallas kernels  18.3 us (15%)
    ppermute x19, waiting for transfers between devices, shift(): return lax.ppermute(v, axis, [(i, (i + by) % size) for i in range(size)])  33.7 us
    ppermute x19, starting transfers between devices, shift(): return lax.ppermute(v, axis, [(i, (i + by) % size) for i in range(size)])  30.7 us
    all_to_all x1, blocking collectives, exchange(): return lax.all_to_all(v, axes, 0, 0, tiled=True)  18.7 us
    all_to_all x3, starting transfers between devices, exchange(): return lax.all_to_all(v, axes, 0, 0, tiled=True)  15.5 us
    pallas_call x14, Pallas kernels, call(): pl.pallas_call(kernel, out_shape=outs, in_specs=[SMEM] * smem + [VMEM] *...  10.2 us
    pallas_call x1, Pallas kernels, contract(): pl.pallas_call(contract_kernel, out_shape=(out, out, jax.ShapeDtypeStruct...  8.03 us
    all_to_all x3, waiting for transfers between devices, exchange(): return lax.all_to_all(v, axes, 0, 0, tiled=True)  7.02 us
  transfers between devices with their start and end apart: 22, of which 11 were waited for; matrix products, arithmetic and copies ran while one was open for 0% of the time, Pallas kernels for 5%

profile of v3, /device:TPU:1, one launch (start us, length us, event | category | flops | bytes accessed | tf_op | source)
XLA Modules:
  0.0 124.7 jit_solution(2896566615815400137)
XLA Ops:
  0.6 8.0 %contract.1 = (f32[768,512]{1,0:T(8,128)S(1)}, f32[768,512]{1,0:T(8,128)S(1)}, bf16[4,8,64,1024]{3,2,1,0:T(8,128)(2,1)S(1)}, bf16[1024,256]{1,0:T(8,128)(2,1)S(1)}) custom-call(f32[4,8]{1,0:T(4,128)} %bitcast.9, bf16[8,1024,1024]{2,1,0:T(8,128)(2,1)} %w.1, bf16[1024,256]{1,0:T(8,128)(2,1)} %c.1), custom_call_target="tpu_custom_call" | custom-call | flops 3221225472 | bytes 16777216 | tf_op jit(solution)/shard_map/contract/pallas_call | solution.py:116
  8.7 1.5 %collective-permute-start.1 = (f32[768,512]{1,0:T(8,128)S(1)}, f32[768,512]{1,0:T(8,128)S(1)}, u32[]{:S(2)}, u32[]{:S(2)}) collective-permute-start(f32[768,512]{1,0:T(8,128)S(1)} %get-tuple-element.31), channel_id=1, source_target_pairs={{0,1},{1,0},{2,3},{3,2},{4,5},{5,4},{6,7},{7,6},{8,9},{9,8},{10,11... | collective-permute-start | bytes 4718600 | tf_op jit(solution)/shard_map/ppermute | solution.py:284
  10.1 2.5 %shard_map.59 = (f32[256,512]{1,0:T(8,128)S(1)}, f32[256,512]{1,0:T(8,128)S(1)}) custom-call(f32[4,8]{1,0:T(4,128)} %bitcast.10, bf16[4,8,64,1024]{3,2,1,0:T(8,128)(2,1)S(1)} %get-tuple-element.26.w, bf16[1024,256]{1,0:T(8,128)(2,1)S(1)} %get-tuple-element.27.c), custom_call_target="tpu_custom_call" | custom-call | flops 1073741824 | bytes 1048576 | tf_op jit(solution)/shard_map/pallas_call | solution.py:45
  15.9 6.9 %all-to-all-start = ((f32[16,64,128]{2,1,0:T(8,128)}), f32[16,64,128]{2,1,0:T(8,128)S(1)}, u32[]{:S(2)}, u32[]{:S(2)}) async-start(f32[16,64,128]{2,1,0:T(8,128)} %bitcast.1), calls=%async_computation | async-start | bytes 1048576 | tf_op jit(solution)/shard_map/all_to_all | solution.py:288
  22.7 1.7 %collective-permute-start.5 = (f32[128,512]{1,0:T(8,128)S(1)}, f32[128,512]{1,0:T(8,128)S(1)}, u32[]{:S(2)}, u32[]{:S(2)}) collective-permute-start(f32[128,512]{1,0:T(8,128)S(1)} %get-tuple-element.36), channel_id=1, source_target_pairs={{0,2},{2,4},{4,6},{6,0},{1,3},{3,5},{5,7},{7,1},{8,10},{10,12},{12... | collective-permute-start | bytes 786440 | tf_op jit(solution)/shard_map/ppermute | solution.py:284
  24.4 2.2 %collective-permute-start.6 = (f32[128,512]{1,0:T(8,128)S(1)}, f32[128,512]{1,0:T(8,128)S(1)}, u32[]{:S(2)}, u32[]{:S(2)}) collective-permute-start(f32[128,512]{1,0:T(8,128)S(1)} %get-tuple-element.38), channel_id=1, source_target_pairs={{0,6},{2,0},{4,2},{6,4},{1,7},{3,1},{5,3},{7,5},{8,14},{10,8},{12,... | collective-permute-start | bytes 786440 | tf_op jit(solution)/shard_map/ppermute | solution.py:284
  26.6 7.0 %all-to-all-done.v = f32[16,64,128]{2,1,0:T(8,128)S(1)} async-done(((f32[16,64,128]{2,1,0:T(8,128)}), f32[16,64,128]{2,1,0:T(8,128)S(1)}, u32[]{:S(2)}, u32[]{:S(2)}) %all-to-all-start) | async-done | bytes 524320 | tf_op jit(solution)/shard_map/all_to_all | solution.py:288
  33.7 3.8 %collective-permute-start.4 = (f32[64,128]{1,0:T(8,128)S(1)}, f32[64,128]{1,0:T(8,128)S(1)}, u32[]{:S(2)}, u32[]{:S(2)}) collective-permute-start(f32[64,128]{1,0:T(8,128)S(1)} %shard_map.62.refs_0_), channel_id=1, source_target_pairs={{0,6},{2,0},{4,2},{6,4},{1,7},{3,1},{5,3},{7,5},{8,14},{10,8},{12,... | collective-permute-start | bytes 98312 | tf_op jit(solution)/shard_map/ppermute | solution.py:284
  40.9 1.5 %collective-permute-start.10 = (f32[128,512]{1,0:T(8,128)S(1)}, f32[128,512]{1,0:T(8,128)S(1)}, u32[]{:S(2)}, u32[]{:S(2)}) collective-permute-start(f32[128,512]{1,0:T(8,128)S(1)} %get-tuple-element.43), channel_id=1, source_target_pairs={{0,6},{2,0},{4,2},{6,4},{1,7},{3,1},{5,3},{7,5},{8,14},{10,8},{12,... | collective-permute-start | bytes 786440 | tf_op jit(solution)/shard_map/ppermute | solution.py:284
  42.5 9.6 %collective-permute-done.2.refs_1_ = f32[64,128]{1,0:T(8,128)S(1)} collective-permute-done((f32[64,128]{1,0:T(8,128)S(1)}, f32[64,128]{1,0:T(8,128)S(1)}, u32[]{:S(2)}, u32[]{:S(2)}) %collective-permute-start.2) | collective-permute-done | bytes 32800 | tf_op jit(solution)/shard_map/ppermute | solution.py:284
  53.0 4.0 %all-to-all-start.1 = ((f32[16,64,128]{2,1,0:T(8,128)}), f32[16,64,128]{2,1,0:T(8,128)S(1)}, u32[]{:S(2)}, u32[]{:S(2)}) async-start(f32[16,64,128]{2,1,0:T(8,128)} %shard_map.63), calls=%async_computation.1 | async-start | bytes 1048576 | tf_op jit(solution)/shard_map/all_to_all | solution.py:288
  57.1 3.1 %collective-permute-start.11 = (f32[128,512]{1,0:T(8,128)S(1)}, f32[128,512]{1,0:T(8,128)S(1)}, u32[]{:S(2)}, u32[]{:S(2)}) collective-permute-start(f32[128,512]{1,0:T(8,128)S(1)} %get-tuple-element.45), channel_id=1, source_target_pairs={{0,64},{64,0},{1,65},{65,1},{2,66},{66,2},{3,67},{67,3},{4,68},{68... | collective-permute-start | bytes 786440 | tf_op jit(solution)/shard_map/ppermute | solution.py:284
  60.2 10.2 %collective-permute-done.11.kb = f32[128,512]{1,0:T(8,128)S(1)} collective-permute-done((f32[128,512]{1,0:T(8,128)S(1)}, f32[128,512]{1,0:T(8,128)S(1)}, u32[]{:S(2)}, u32[]{:S(2)}) %collective-permute-start.11) | collective-permute-done | bytes 262176 | tf_op jit(solution)/shard_map/ppermute | solution.py:284
  70.8 2.6 %collective-permute-start.12 = (f32[128,256]{1,0:T(8,128)S(1)}, f32[128,256]{1,0:T(8,128)S(1)}, u32[]{:S(2)}, u32[]{:S(2)}) collective-permute-start(f32[128,256]{1,0:T(8,128)S(1)} %get-tuple-element.46.zp), channel_id=1, source_target_pairs={{0,1},{1,0},{2,3},{3,2},{4,5},{5,4},{6,7},{7,6},{8,9},{9,8},{10,11... | collective-permute-start | bytes 393224 | tf_op jit(solution)/shard_map/ppermute | solution.py:284
  74.8 18.7 %all_to_all.20.refs_0_ = f32[64,16,128]{2,1,0:T(8,128)S(1)} all-to-all(f32[64,16,128]{2,1,0:T(8,128)S(1)} %bitcast.8), channel_id=1, replica_groups=mesh['yhi'=2,'ylo'=2,'x'=4,'z'=4,'core'=2] {'yhi','ylo','x','z'}, dimensions={0} | all-to-all | bytes 1048576 | tf_op jit(solution)/shard_map/all_to_all | solution.py:288
  94.4 4.7 %all-to-all-start.3 = ((f32[64,16,128]{2,1,0:T(8,128)}), f32[64,16,128]{2,1,0:T(8,128)S(1)}, u32[]{:S(2)}, u32[]{:S(2)}) async-start(f32[64,16,128]{2,1,0:T(8,128)} %shard_map.71), calls=%async_computation.3 | async-start | bytes 1048576 | tf_op jit(solution)/shard_map/all_to_all | solution.py:288
  99.1 2.7 %collective-permute-start.13 = (f32[64,256]{1,0:T(8,128)S(1)}, f32[64,256]{1,0:T(8,128)S(1)}, u32[]{:S(2)}, u32[]{:S(2)}) collective-permute-start(f32[64,256]{1,0:T(8,128)S(1)} %get-tuple-element.48.refs_0_), channel_id=1, source_target_pairs={{0,64},{64,0},{1,65},{65,1},{2,66},{66,2},{3,67},{67,3},{4,68},{68... | collective-permute-start | bytes 196616 | tf_op jit(solution)/shard_map/ppermute | solution.py:284
  101.8 4.9 %collective-permute-done.13.refs_1_ = f32[64,256]{1,0:T(8,128)S(1)} collective-permute-done((f32[64,256]{1,0:T(8,128)S(1)}, f32[64,256]{1,0:T(8,128)S(1)}, u32[]{:S(2)}, u32[]{:S(2)}) %collective-permute-start.13) | collective-permute-done | bytes 65568 | tf_op jit(solution)/shard_map/ppermute | solution.py:284
  106.7 1.8 %collective-permute-start.16 = (f32[128,256]{1,0:T(8,128)S(1)}, f32[128,256]{1,0:T(8,128)S(1)}, u32[]{:S(2)}, u32[]{:S(2)}) collective-permute-start(f32[128,256]{1,0:T(8,128)S(1)} %shard_map.68.refs_0_), channel_id=1, source_target_pairs={{0,6},{2,0},{4,2},{6,4},{1,7},{3,1},{5,3},{7,5},{8,14},{10,8},{12,... | collective-permute-start | bytes 393224 | tf_op jit(solution)/shard_map/ppermute | solution.py:284
  109.8 1.8 %collective-permute-done.16.refs_3_ = f32[128,256]{1,0:T(8,128)S(1)} collective-permute-done((f32[128,256]{1,0:T(8,128)S(1)}, f32[128,256]{1,0:T(8,128)S(1)}, u32[]{:S(2)}, u32[]{:S(2)}) %collective-permute-start.16) | collective-permute-done | bytes 131104 | tf_op jit(solution)/shard_map/ppermute | solution.py:284
  111.5 2.4 %collective-permute-done.15.refs_2_ = f32[128,256]{1,0:T(8,128)S(1)} collective-permute-done((f32[128,256]{1,0:T(8,128)S(1)}, f32[128,256]{1,0:T(8,128)S(1)}, u32[]{:S(2)}, u32[]{:S(2)}) %collective-permute-start.15) | collective-permute-done | bytes 131104 | tf_op jit(solution)/shard_map/ppermute | solution.py:284
  113.9 1.3 %collective-permute-done.14.refs_1_ = f32[128,256]{1,0:T(8,128)S(1)} collective-permute-done((f32[128,256]{1,0:T(8,128)S(1)}, f32[128,256]{1,0:T(8,128)S(1)}, u32[]{:S(2)}, u32[]{:S(2)}) %collective-permute-start.14) | collective-permute-done | bytes 131104 | tf_op jit(solution)/shard_map/ppermute | solution.py:284
  115.3 5.7 %collective-permute-start.17 = (f32[512,256]{1,0:T(8,128)S(1)}, f32[512,256]{1,0:T(8,128)S(1)}, u32[]{:S(2)}, u32[]{:S(2)}) collective-permute-start(f32[512,256]{1,0:T(8,128)S(1)} %shard_map.69.mine), channel_id=1, source_target_pairs={{0,1},{1,0},{2,3},{3,2},{4,5},{5,4},{6,7},{7,6},{8,9},{9,8},{10,11... | collective-permute-start | bytes 1572872 | tf_op jit(solution)/shard_map/ppermute | solution.py:284
  121.1 1.4 %collective-permute-done.17.other = f32[512,256]{1,0:T(8,128)S(1)} collective-permute-done((f32[512,256]{1,0:T(8,128)S(1)}, f32[512,256]{1,0:T(8,128)S(1)}, u32[]{:S(2)}, u32[]{:S(2)}) %collective-permute-start.17) | collective-permute-done | bytes 524320 | tf_op jit(solution)/shard_map/ppermute | solution.py:284
  (38 shorter events, 13.9 us)
Async XLA Ops:
  8.7 4.5 %collective-permute-start.1 = (f32[768,512]{1,0:T(8,128)S(1)}, f32[768,512]{1,0:T(8,128)S(1)}, u32[]{:S(2)}, u32[]{:S(2)}) collective-permute-start(f32[768,512]{1,0:T(8,128)S(1)} %get-tuple-element.31), channel_id=1, source_target_pairs={{0,1},{1,0},{2,3},{3,2},{4,5},{5,4},{6,7},{7,6},{8,9},{9,8},{10,11... | collective-permute-start | bytes 4718600 | tf_op jit(solution)/shard_map/ppermute | solution.py:284
  10.1 3.0 %copy-start = (f32[1024,256]{1,0:T(8,128)S(1)}, f32[1024,256]{1,0:T(8,128)}, u32[]{:S(2)}) copy-start(f32[1024,256]{1,0:T(8,128)} %rf.3) | copy-start | bytes 3145732
  12.6 2.0 %collective-permute-start = (f32[256,512]{1,0:T(8,128)S(1)}, f32[256,512]{1,0:T(8,128)S(1)}, u32[]{:S(2)}, u32[]{:S(2)}) collective-permute-start(f32[256,512]{1,0:T(8,128)S(1)} %get-tuple-element.29), channel_id=1, source_target_pairs={{0,1},{1,0},{2,3},{3,2},{4,5},{5,4},{6,7},{7,6},{8,9},{9,8},{10,11... | collective-permute-start | bytes 1572872 | tf_op jit(solution)/shard_map/ppermute | solution.py:284
  15.9 17.8 %all-to-all-start = ((f32[16,64,128]{2,1,0:T(8,128)}), f32[16,64,128]{2,1,0:T(8,128)S(1)}, u32[]{:S(2)}, u32[]{:S(2)}) async-start(f32[16,64,128]{2,1,0:T(8,128)} %bitcast.1), calls=%async_computation | async-start | bytes 1048576 | tf_op jit(solution)/shard_map/all_to_all | solution.py:288
  22.7 15.1 %collective-permute-start.5 = (f32[128,512]{1,0:T(8,128)S(1)}, f32[128,512]{1,0:T(8,128)S(1)}, u32[]{:S(2)}, u32[]{:S(2)}) collective-permute-start(f32[128,512]{1,0:T(8,128)S(1)} %get-tuple-element.36), channel_id=1, source_target_pairs={{0,2},{2,4},{4,6},{6,0},{1,3},{3,5},{5,7},{7,1},{8,10},{10,12},{12... | collective-permute-start | bytes 786440 | tf_op jit(solution)/shard_map/ppermute | solution.py:284
  24.4 14.6 %collective-permute-start.6 = (f32[128,512]{1,0:T(8,128)S(1)}, f32[128,512]{1,0:T(8,128)S(1)}, u32[]{:S(2)}, u32[]{:S(2)}) collective-permute-start(f32[128,512]{1,0:T(8,128)S(1)} %get-tuple-element.38), channel_id=1, source_target_pairs={{0,6},{2,0},{4,2},{6,4},{1,7},{3,1},{5,3},{7,5},{8,14},{10,8},{12,... | collective-permute-start | bytes 786440 | tf_op jit(solution)/shard_map/ppermute | solution.py:284
  33.7 7.2 %collective-permute-start.4 = (f32[64,128]{1,0:T(8,128)S(1)}, f32[64,128]{1,0:T(8,128)S(1)}, u32[]{:S(2)}, u32[]{:S(2)}) collective-permute-start(f32[64,128]{1,0:T(8,128)S(1)} %shard_map.62.refs_0_), channel_id=1, source_target_pairs={{0,6},{2,0},{4,2},{6,4},{1,7},{3,1},{5,3},{7,5},{8,14},{10,8},{12,... | collective-permute-start | bytes 98312 | tf_op jit(solution)/shard_map/ppermute | solution.py:284
  37.5 4.9 %collective-permute-start.3 = (f32[64,128]{1,0:T(8,128)S(1)}, f32[64,128]{1,0:T(8,128)S(1)}, u32[]{:S(2)}, u32[]{:S(2)}) collective-permute-start(f32[64,128]{1,0:T(8,128)S(1)} %shard_map.62.refs_0_), channel_id=1, source_target_pairs={{0,4},{2,6},{4,0},{6,2},{1,5},{3,7},{5,1},{7,3},{8,12},{10,14},{12... | collective-permute-start | bytes 98312 | tf_op jit(solution)/shard_map/ppermute | solution.py:284
  37.5 19.4 %collective-permute-start.8 = (f32[128,512]{1,0:T(8,128)S(1)}, f32[128,512]{1,0:T(8,128)S(1)}, u32[]{:S(2)}, u32[]{:S(2)}) collective-permute-start(f32[128,512]{1,0:T(8,128)S(1)} %get-tuple-element.40), channel_id=1, source_target_pairs={{0,6},{2,0},{4,2},{6,4},{1,7},{3,1},{5,3},{7,5},{8,14},{10,8},{12,... | collective-permute-start | bytes 786440 | tf_op jit(solution)/shard_map/ppermute | solution.py:284
  37.9 19.1 %collective-permute-start.9 = (f32[128,512]{1,0:T(8,128)S(1)}, f32[128,512]{1,0:T(8,128)S(1)}, u32[]{:S(2)}, u32[]{:S(2)}) collective-permute-start(f32[128,512]{1,0:T(8,128)S(1)} %get-tuple-element.42), channel_id=1, source_target_pairs={{0,2},{2,4},{4,6},{6,0},{1,3},{3,5},{5,7},{7,1},{8,10},{10,12},{12... | collective-permute-start | bytes 786440 | tf_op jit(solution)/shard_map/ppermute | solution.py:284
  39.8 17.2 %collective-permute-start.7 = (f32[128,512]{1,0:T(8,128)}, f32[128,512]{1,0:T(8,128)S(1)}, u32[]{:S(2)}, u32[]{:S(2)}) collective-permute-start(f32[128,512]{1,0:T(8,128)} %get-tuple-element.39), channel_id=1, source_target_pairs={{0,2},{2,4},{4,6},{6,0},{1,3},{3,5},{5,7},{7,1},{8,10},{10,12},{12... | collective-permute-start | bytes 786440 | tf_op jit(solution)/shard_map/ppermute | solution.py:284
  40.9 16.1 %collective-permute-start.10 = (f32[128,512]{1,0:T(8,128)S(1)}, f32[128,512]{1,0:T(8,128)S(1)}, u32[]{:S(2)}, u32[]{:S(2)}) collective-permute-start(f32[128,512]{1,0:T(8,128)S(1)} %get-tuple-element.43), channel_id=1, source_target_pairs={{0,6},{2,0},{4,2},{6,4},{1,7},{3,1},{5,3},{7,5},{8,14},{10,8},{12,... | collective-permute-start | bytes 786440 | tf_op jit(solution)/shard_map/ppermute | solution.py:284
  42.4 9.7 %collective-permute-start.2 = (f32[64,128]{1,0:T(8,128)S(1)}, f32[64,128]{1,0:T(8,128)S(1)}, u32[]{:S(2)}, u32[]{:S(2)}) collective-permute-start(f32[64,128]{1,0:T(8,128)S(1)} %shard_map.62.refs_0_), channel_id=1, source_target_pairs={{0,2},{2,4},{4,6},{6,0},{1,3},{3,5},{5,7},{7,1},{8,10},{10,12},{12... | collective-permute-start | bytes 98312 | tf_op jit(solution)/shard_map/ppermute | solution.py:284
  53.0 17.4 %all-to-all-start.1 = ((f32[16,64,128]{2,1,0:T(8,128)}), f32[16,64,128]{2,1,0:T(8,128)S(1)}, u32[]{:S(2)}, u32[]{:S(2)}) async-start(f32[16,64,128]{2,1,0:T(8,128)} %shard_map.63), calls=%async_computation.1 | async-start | bytes 1048576 | tf_op jit(solution)/shard_map/all_to_all | solution.py:288
  57.1 13.3 %collective-permute-start.11 = (f32[128,512]{1,0:T(8,128)S(1)}, f32[128,512]{1,0:T(8,128)S(1)}, u32[]{:S(2)}, u32[]{:S(2)}) collective-permute-start(f32[128,512]{1,0:T(8,128)S(1)} %get-tuple-element.45), channel_id=1, source_target_pairs={{0,64},{64,0},{1,65},{65,1},{2,66},{66,2},{3,67},{67,3},{4,68},{68... | collective-permute-start | bytes 786440 | tf_op jit(solution)/shard_map/ppermute | solution.py:284
  70.8 3.6 %collective-permute-start.12 = (f32[128,256]{1,0:T(8,128)S(1)}, f32[128,256]{1,0:T(8,128)S(1)}, u32[]{:S(2)}, u32[]{:S(2)}) collective-permute-start(f32[128,256]{1,0:T(8,128)S(1)} %get-tuple-element.46.zp), channel_id=1, source_target_pairs={{0,1},{1,0},{2,3},{3,2},{4,5},{5,4},{6,7},{7,6},{8,9},{9,8},{10,11... | collective-permute-start | bytes 393224 | tf_op jit(solution)/shard_map/ppermute | solution.py:284
  94.4 26.6 %all-to-all-start.3 = ((f32[64,16,128]{2,1,0:T(8,128)}), f32[64,16,128]{2,1,0:T(8,128)S(1)}, u32[]{:S(2)}, u32[]{:S(2)}) async-start(f32[64,16,128]{2,1,0:T(8,128)} %shard_map.71), calls=%async_computation.3 | async-start | bytes 1048576 | tf_op jit(solution)/shard_map/all_to_all | solution.py:288
  99.1 7.6 %collective-permute-start.13 = (f32[64,256]{1,0:T(8,128)S(1)}, f32[64,256]{1,0:T(8,128)S(1)}, u32[]{:S(2)}, u32[]{:S(2)}) collective-permute-start(f32[64,256]{1,0:T(8,128)S(1)} %get-tuple-element.48.refs_0_), channel_id=1, source_target_pairs={{0,64},{64,0},{1,65},{65,1},{2,66},{66,2},{3,67},{67,3},{4,68},{68... | collective-permute-start | bytes 196616 | tf_op jit(solution)/shard_map/ppermute | solution.py:284
  106.7 4.9 %collective-permute-start.16 = (f32[128,256]{1,0:T(8,128)S(1)}, f32[128,256]{1,0:T(8,128)S(1)}, u32[]{:S(2)}, u32[]{:S(2)}) collective-permute-start(f32[128,256]{1,0:T(8,128)S(1)} %shard_map.68.refs_0_), channel_id=1, source_target_pairs={{0,6},{2,0},{4,2},{6,4},{1,7},{3,1},{5,3},{7,5},{8,14},{10,8},{12,... | collective-permute-start | bytes 393224 | tf_op jit(solution)/shard_map/ppermute | solution.py:284
  108.5 5.5 %collective-permute-start.15 = (f32[128,256]{1,0:T(8,128)S(1)}, f32[128,256]{1,0:T(8,128)S(1)}, u32[]{:S(2)}, u32[]{:S(2)}) collective-permute-start(f32[128,256]{1,0:T(8,128)S(1)} %shard_map.68.refs_0_), channel_id=1, source_target_pairs={{0,4},{2,6},{4,0},{6,2},{1,5},{3,7},{5,1},{7,3},{8,12},{10,14},{12... | collective-permute-start | bytes 393224 | tf_op jit(solution)/shard_map/ppermute | solution.py:284
  109.7 5.6 %collective-permute-start.14 = (f32[128,256]{1,0:T(8,128)S(1)}, f32[128,256]{1,0:T(8,128)S(1)}, u32[]{:S(2)}, u32[]{:S(2)}) collective-permute-start(f32[128,256]{1,0:T(8,128)S(1)} %shard_map.68.refs_0_), channel_id=1, source_target_pairs={{0,2},{2,4},{4,6},{6,0},{1,3},{3,5},{5,7},{7,1},{8,10},{10,12},{12... | collective-permute-start | bytes 393224 | tf_op jit(solution)/shard_map/ppermute | solution.py:284
  115.3 7.2 %collective-permute-start.17 = (f32[512,256]{1,0:T(8,128)S(1)}, f32[512,256]{1,0:T(8,128)S(1)}, u32[]{:S(2)}, u32[]{:S(2)}) collective-permute-start(f32[512,256]{1,0:T(8,128)S(1)} %shard_map.69.mine), channel_id=1, source_target_pairs={{0,1},{1,0},{2,3},{3,2},{4,5},{5,4},{6,7},{7,6},{8,9},{9,8},{10,11... | collective-permute-start | bytes 1572872 | tf_op jit(solution)/shard_map/ppermute | solution.py:284
  121.0 2.6 %collective-permute-start.18 = (f32[128,8,128]{2,1,0:T(8,128)S(1)}, f32[128,8,128]{2,1,0:T(8,128)S(1)}, u32[]{:S(2)}, u32[]{:S(2)}) collective-permute-start(f32[128,8,128]{2,1,0:T(8,128)S(1)} %bitcast.6), channel_id=1, source_target_pairs={{0,1},{1,0},{2,3},{3,2},{4,5},{5,4},{6,7},{7,6},{8,9},{9,8},{10,11... | collective-permute-start | bytes 1572872 | tf_op jit(solution)/shard_map/ppermute | solution.py:284

commit v4 on v3

--- a/solution.py
+++ b/solution.py
@@ -160,15 +160,16 @@
     )
 
 
-def cross_kernel(first, count, keep, recv, rf, *refs):
-    prior = refs[0] if len(refs) > 2 * count + 1 else None
-    blocks, ct = refs[-2 * count - 1 : -1], refs[-1]
+def cross_kernel(first, places, keep, recv, rf, *refs):
+    blocks = len({place[0] for place in places})
+    prior = refs[0] if len(refs) > blocks + 1 else None
+    outs, ct = refs[-blocks - 1 : -1], refs[-1]
     half = BLOCK // 2
     total = None
-    for n in range(count):
+    for n in range(len(places) // 2):
         v = keep[n * BLOCK : (n + 1) * BLOCK] + recv[n * BLOCK : (n + 1) * BLOCK]
-        blocks[2 * n][...] = v[:half]
-        blocks[2 * n + 1][...] = v[half:]
+        for h, (i, at) in enumerate(places[2 * n : 2 * n + 2]):
+            outs[i][at * half : (at + 1) * half] = v[h * half : (h + 1) * half]
         f = jnp.concatenate(
             [
                 rf[pl.ds(pl.multiple_of(half_block(2 * (first + n) + h) * half, half), half), :]
@@ -186,15 +187,16 @@
             ct[a * COLS + b] = t
 
 
-def cross_part(keep, recv, rf, first, count, prior):
+def cross_part(keep, recv, rf, first, places, prior):
     ops = [keep, recv, rf] + ([] if prior is None else [prior])
+    sizes = [sum(p[0] == i for p in places) for i in range(len({p[0] for p in places}))]
     return call(
-        functools.partial(cross_kernel, first, count),
-        [shape(BLOCK // 2, HALF)] * (2 * count) + [shape(RC * HALF // 1024, 8, 128)],
+        functools.partial(cross_kernel, first, places),
+        [shape(n * BLOCK // 2, HALF) for n in sizes] + [shape(RC * HALF // 1024, 8, 128)],
         ops,
         vmem=20,
         cost=pl.CostEstimate(
-            flops=6 * count * BLOCK * RC * HALF, bytes_accessed=4 * MIB, transcendentals=0
+            flops=3 * len(places) * BLOCK * RC * HALF, bytes_accessed=4 * MIB, transcendentals=0
         ),
     )
 
@@ -243,14 +245,16 @@
                 out[rows, :] = ref[i : i + quarter, :]
 
 
-def relay_kernel(a, b, c, d, ab, cd):
-    ab[...] = a[...] + b[...]
-    cd[...] = c[...] + d[...]
-
-
-def block_kernel(a0, a1, a2, b0, b1, b2, away, keep):
-    away[...] = (a0[...] + a1[...]) + a2[...]
-    keep[...] = (b0[...] + b1[...]) + b2[...]
+def relay_kernel(a, b, below, above, ab, cd):
+    half = BLOCK // 2
+    ab[...] = a[...] + below[:half]
+    cd[...] = b[...] + above[:half]
+
+
+def block_kernel(a, b, below, above, a2, b2, away, keep):
+    half = BLOCK // 2
+    away[...] = (a[...] + a2[...]) + above[half:]
+    keep[...] = (b[...] + b2[...]) + below[half:]
 
 
 def gathered_kernel(v, out):
@@ -312,19 +316,19 @@
     recv1 = shift(send1, "core", 2, 1)
     send2, keep2 = contract_last(lf, ahead, factor)
     recv2 = shift(send2, "core", 2, 1)
-    v2a, v2b, v1a, v1b, v3a, v3b, ct = cross_part(keep1, recv1, row_factor, 0, 3, None)
-    p1 = shift(v2a, "z", 4, 1)
-    p2 = shift(v2b, "z", 4, 3)
-    p3 = shift(v1b, "z", 4, 1)
-    p4 = shift(v3a, "z", 4, 3)
-    v0a, v0b, ct = cross_part(keep2, recv2, row_factor, 3, 1, ct)
+    up, down, v1a, v3b, ct = cross_part(
+        keep1, recv1, row_factor, 0, ((0, 0), (1, 0), (2, 0), (0, 1), (1, 1), (3, 0)), None
+    )
+    p1 = shift(up, "z", 4, 1)
+    p2 = shift(down, "z", 4, 3)
+    v0a, v0b, ct = cross_part(keep2, recv2, row_factor, 3, ((0, 0), (1, 0)), ct)
     cross = sum_over_planes(ct)
     rows = BLOCK // 2
-    s1, s3 = call(relay_kernel, [shape(rows, HALF)] * 2, [v1a, p1, v3b, p2])
+    s1, s3 = call(relay_kernel, [shape(rows, HALF)] * 2, [v1a, v3b, p1, p2])
     p5 = shift(s1, "z", 4, 1)
     p6 = shift(s3, "z", 4, 3)
 
-    away, ka = call(block_kernel, [shape(rows, HALF)] * 2, [v0a, p5, p4, v0b, p3, p6])
+    away, ka = call(block_kernel, [shape(rows, HALF)] * 2, [v0a, v0b, p1, p2, p5, p6])
     kb = shift(away, "yhi", 2, 1)
 
     zp, u = call(

time: 125 us -> 119 us (0.952)
  blocking collectives: 18.7 us -> 36.5 us
  waiting for transfers between devices: 40.7 us -> 27.7 us
  starting transfers between devices: 46.3 us -> 36.1 us
  Pallas kernels: 18.3 us -> 16.8 us
    all_to_all x1 -> x2, blocking collectives: 18.7 us -> 36.5 us  [exchange(): return lax.all_to_all(v, axes, 0, 0, tiled=True)]
    ppermute x19 -> x17, waiting for transfers between devices: 33.7 us -> 21.4 us  [shift(): return lax.ppermute(v, axis, [(i, (i + by) % size) for i in range(size)])]
    all_to_all x3 -> x2, starting transfers between devices: 15.5 us -> 8.26 us  [exchange(): return lax.all_to_all(v, axes, 0, 0, tiled=True)]
    ppermute x19 -> x17, starting transfers between devices: 30.7 us -> 27.9 us  [shift(): return lax.ppermute(v, axis, [(i, (i + by) % size) for i in range(size)])]
    pallas_call x14, Pallas kernels: 10.2 us -> 8.73 us  [call(): pl.pallas_call(kernel, out_shape=outs, in_specs=[SMEM] * smem + [VMEM] *...]
    all_to_all x3 -> x2, waiting for transfers between devices: 7.02 us -> 6.3 us  [exchange(): return lax.all_to_all(v, axes, 0, 0, tiled=True)]
  transfers between devices with their start and end apart: 22 -> 19, of which waited for: 11 -> 11; matrix products, arithmetic and copies ran while one was open for 0% -> 0% of each run, Pallas kernels for 5% -> 5%
where the time goes in v4:
time: 119 us; the launch traced here: 118 us
  blocking collectives  36.5 us (31%)
  starting transfers between devices  36.1 us (30%)
  waiting for transfers between devices  27.7 us (23%)
  Pallas kernels  16.8 us (14%)
    all_to_all x2, blocking collectives, exchange(): return lax.all_to_all(v, axes, 0, 0, tiled=True)  36.5 us
    ppermute x17, starting transfers between devices, shift(): return lax.ppermute(v, axis, [(i, (i + by) % size) for i in range(size)])  27.9 us
    ppermute x17, waiting for transfers between devices, shift(): return lax.ppermute(v, axis, [(i, (i + by) % size) for i in range(size)])  21.4 us
    pallas_call x14, Pallas kernels, call(): pl.pallas_call(kernel, out_shape=outs, in_specs=[SMEM] * smem + [VMEM] *...  8.73 us
    all_to_all x2, starting transfers between devices, exchange(): return lax.all_to_all(v, axes, 0, 0, tiled=True)  8.26 us
    pallas_call x1, Pallas kernels, contract(): pl.pallas_call(contract_kernel, out_shape=(out, out, jax.ShapeDtypeStruct...  8.03 us
    all_to_all x2, waiting for transfers between devices, exchange(): return lax.all_to_all(v, axes, 0, 0, tiled=True)  6.3 us
  transfers between devices with their start and end apart: 19, of which 11 were waited for; matrix products, arithmetic and copies ran while one was open for 0% of the time, Pallas kernels for 5%

profile of v4, /device:TPU:1, one launch (start us, length us, event | category | flops | bytes accessed | tf_op | source)
XLA Modules:
  0.0 117.9 jit_solution(7708827967174446967)
XLA Ops:
  0.6 8.0 %contract.1 = (f32[768,512]{1,0:T(8,128)S(1)}, f32[768,512]{1,0:T(8,128)S(1)}, bf16[4,8,64,1024]{3,2,1,0:T(8,128)(2,1)S(1)}, bf16[1024,256]{1,0:T(8,128)(2,1)S(1)}) custom-call(f32[4,8]{1,0:T(4,128)} %bitcast.10, bf16[8,1024,1024]{2,1,0:T(8,128)(2,1)} %w.1, bf16[1024,256]{1,0:T(8,128)(2,1)} %c.1), custom_call_target="tpu_custom_call" | custom-call | flops 3221225472 | bytes 16777216 | tf_op jit(solution)/shard_map/contract/pallas_call | solution.py:116
  8.7 1.5 %collective-permute-start.1 = (f32[768,512]{1,0:T(8,128)S(1)}, f32[768,512]{1,0:T(8,128)S(1)}, u32[]{:S(2)}, u32[]{:S(2)}) collective-permute-start(f32[768,512]{1,0:T(8,128)S(1)} %get-tuple-element.29), channel_id=1, source_target_pairs={{0,1},{1,0},{2,3},{3,2},{4,5},{5,4},{6,7},{7,6},{8,9},{9,8},{10,11... | collective-permute-start | bytes 4718600 | tf_op jit(solution)/shard_map/ppermute | solution.py:288
  10.1 2.5 %shard_map.59 = (f32[256,512]{1,0:T(8,128)S(1)}, f32[256,512]{1,0:T(8,128)S(1)}) custom-call(f32[4,8]{1,0:T(4,128)} %bitcast.11, bf16[4,8,64,1024]{3,2,1,0:T(8,128)(2,1)S(1)} %get-tuple-element.24.w, bf16[1024,256]{1,0:T(8,128)(2,1)S(1)} %get-tuple-element.25.c), custom_call_target="tpu_custom_call" | custom-call | flops 1073741824 | bytes 1048576 | tf_op jit(solution)/shard_map/pallas_call | solution.py:45
  14.1 1.8 %collective-permute-start.5 = (f32[256,512]{1,0:T(8,128)S(1)}, f32[256,512]{1,0:T(8,128)S(1)}, u32[]{:S(2)}, u32[]{:S(2)}) collective-permute-start(f32[256,512]{1,0:T(8,128)S(1)} %get-tuple-element.34), channel_id=1, source_target_pairs={{0,2},{2,4},{4,6},{6,0},{1,3},{3,5},{5,7},{7,1},{8,10},{10,12},{12... | collective-permute-start | bytes 1572872 | tf_op jit(solution)/shard_map/ppermute | solution.py:288
  15.9 2.2 %collective-permute-start.6 = (f32[256,512]{1,0:T(8,128)S(1)}, f32[256,512]{1,0:T(8,128)S(1)}, u32[]{:S(2)}, u32[]{:S(2)}) collective-permute-start(f32[256,512]{1,0:T(8,128)S(1)} %get-tuple-element.35), channel_id=1, source_target_pairs={{0,6},{2,0},{4,2},{6,4},{1,7},{3,1},{5,3},{7,5},{8,14},{10,8},{12,... | collective-permute-start | bytes 1572872 | tf_op jit(solution)/shard_map/ppermute | solution.py:288
  18.5 17.0 %all_to_all.20.v = f32[16,64,128]{2,1,0:T(8,128)S(1)} all-to-all(f32[16,64,128]{2,1,0:T(8,128)S(1)} %bitcast.8), channel_id=1, replica_groups=mesh['yhi'=2,'ylo'=2,'x'=4,'z'=4,'core'=2] {'yhi','ylo','x'}, dimensions={0} | all-to-all | bytes 1048576 | tf_op jit(solution)/shard_map/all_to_all | solution.py:292
  35.6 1.5 %collective-permute-start.4 = (f32[64,128]{1,0:T(8,128)S(1)}, f32[64,128]{1,0:T(8,128)S(1)}, u32[]{:S(2)}, u32[]{:S(2)}) collective-permute-start(f32[64,128]{1,0:T(8,128)S(1)} %shard_map.62.refs_0_), channel_id=1, source_target_pairs={{0,6},{2,0},{4,2},{6,4},{1,7},{3,1},{5,3},{7,5},{8,14},{10,8},{12,... | collective-permute-start | bytes 98312 | tf_op jit(solution)/shard_map/ppermute | solution.py:288
  37.2 2.6 %collective-permute-start.8 = (f32[128,512]{1,0:T(8,128)S(1)}, f32[128,512]{1,0:T(8,128)S(1)}, u32[]{:S(2)}, u32[]{:S(2)}) collective-permute-start(f32[128,512]{1,0:T(8,128)S(1)} %get-tuple-element.39), channel_id=1, source_target_pairs={{0,6},{2,0},{4,2},{6,4},{1,7},{3,1},{5,3},{7,5},{8,14},{10,8},{12,... | collective-permute-start | bytes 786440 | tf_op jit(solution)/shard_map/ppermute | solution.py:288
  40.4 4.0 %collective-permute-done.3.refs_2_ = f32[64,128]{1,0:T(8,128)S(1)} collective-permute-done((f32[64,128]{1,0:T(8,128)S(1)}, f32[64,128]{1,0:T(8,128)S(1)}, u32[]{:S(2)}, u32[]{:S(2)}) %collective-permute-start.3) | collective-permute-done | bytes 32800 | tf_op jit(solution)/shard_map/ppermute | solution.py:288
  45.8 3.6 %all-to-all-start.1 = ((f32[16,64,128]{2,1,0:T(8,128)}), f32[16,64,128]{2,1,0:T(8,128)S(1)}, u32[]{:S(2)}, u32[]{:S(2)}) async-start(f32[16,64,128]{2,1,0:T(8,128)} %shard_map.63), calls=%async_computation.1 | async-start | bytes 1048576 | tf_op jit(solution)/shard_map/all_to_all | solution.py:292
  49.5 2.9 %collective-permute-start.9 = (f32[128,512]{1,0:T(8,128)S(1)}, f32[128,512]{1,0:T(8,128)S(1)}, u32[]{:S(2)}, u32[]{:S(2)}) collective-permute-start(f32[128,512]{1,0:T(8,128)S(1)} %get-tuple-element.41), channel_id=1, source_target_pairs={{0,64},{64,0},{1,65},{65,1},{2,66},{66,2},{3,67},{67,3},{4,68},{68... | collective-permute-start | bytes 786440 | tf_op jit(solution)/shard_map/ppermute | solution.py:288
  52.4 6.3 %all-to-all-done.1 = f32[16,64,128]{2,1,0:T(8,128)S(1)} async-done(((f32[16,64,128]{2,1,0:T(8,128)}), f32[16,64,128]{2,1,0:T(8,128)S(1)}, u32[]{:S(2)}, u32[]{:S(2)}) %all-to-all-start.1) | async-done | bytes 524320 | tf_op jit(solution)/shard_map/all_to_all | solution.py:292
  58.7 3.6 %collective-permute-done.9.kb = f32[128,512]{1,0:T(8,128)S(1)} collective-permute-done((f32[128,512]{1,0:T(8,128)S(1)}, f32[128,512]{1,0:T(8,128)S(1)}, u32[]{:S(2)}, u32[]{:S(2)}) %collective-permute-start.9) | collective-permute-done | bytes 262176 | tf_op jit(solution)/shard_map/ppermute | solution.py:288
  62.7 3.1 %collective-permute-start.10 = (f32[128,256]{1,0:T(8,128)S(1)}, f32[128,256]{1,0:T(8,128)S(1)}, u32[]{:S(2)}, u32[]{:S(2)}) collective-permute-start(f32[128,256]{1,0:T(8,128)S(1)} %get-tuple-element.42.zp), channel_id=1, source_target_pairs={{0,1},{1,0},{2,3},{3,2},{4,5},{5,4},{6,7},{7,6},{8,9},{9,8},{10,11... | collective-permute-start | bytes 393224 | tf_op jit(solution)/shard_map/ppermute | solution.py:288
  67.1 19.5 %all_to_all.21.refs_0_ = f32[64,16,128]{2,1,0:T(8,128)S(1)} all-to-all(f32[64,16,128]{2,1,0:T(8,128)S(1)} %bitcast.9), channel_id=1, replica_groups=mesh['yhi'=2,'ylo'=2,'x'=4,'z'=4,'core'=2] {'yhi','ylo','x','z'}, dimensions={0} | all-to-all | bytes 1048576 | tf_op jit(solution)/shard_map/all_to_all | solution.py:292
  87.5 4.7 %all-to-all-start.3 = ((f32[64,16,128]{2,1,0:T(8,128)}), f32[64,16,128]{2,1,0:T(8,128)S(1)}, u32[]{:S(2)}, u32[]{:S(2)}) async-start(f32[64,16,128]{2,1,0:T(8,128)} %shard_map.71), calls=%async_computation.3 | async-start | bytes 1048576 | tf_op jit(solution)/shard_map/all_to_all | solution.py:292
  92.2 2.7 %collective-permute-start.11 = (f32[64,256]{1,0:T(8,128)S(1)}, f32[64,256]{1,0:T(8,128)S(1)}, u32[]{:S(2)}, u32[]{:S(2)}) collective-permute-start(f32[64,256]{1,0:T(8,128)S(1)} %get-tuple-element.44.refs_0_), channel_id=1, source_target_pairs={{0,64},{64,0},{1,65},{65,1},{2,66},{66,2},{3,67},{67,3},{4,68},{68... | collective-permute-start | bytes 196616 | tf_op jit(solution)/shard_map/ppermute | solution.py:288
  94.9 4.9 %collective-permute-done.11.refs_1_ = f32[64,256]{1,0:T(8,128)S(1)} collective-permute-done((f32[64,256]{1,0:T(8,128)S(1)}, f32[64,256]{1,0:T(8,128)S(1)}, u32[]{:S(2)}, u32[]{:S(2)}) %collective-permute-start.11) | collective-permute-done | bytes 65568 | tf_op jit(solution)/shard_map/ppermute | solution.py:288
  99.8 1.8 %collective-permute-start.14 = (f32[128,256]{1,0:T(8,128)S(1)}, f32[128,256]{1,0:T(8,128)S(1)}, u32[]{:S(2)}, u32[]{:S(2)}) collective-permute-start(f32[128,256]{1,0:T(8,128)S(1)} %shard_map.68.refs_0_), channel_id=1, source_target_pairs={{0,6},{2,0},{4,2},{6,4},{1,7},{3,1},{5,3},{7,5},{8,14},{10,8},{12,... | collective-permute-start | bytes 393224 | tf_op jit(solution)/shard_map/ppermute | solution.py:288
  102.9 1.8 %collective-permute-done.14.refs_3_ = f32[128,256]{1,0:T(8,128)S(1)} collective-permute-done((f32[128,256]{1,0:T(8,128)S(1)}, f32[128,256]{1,0:T(8,128)S(1)}, u32[]{:S(2)}, u32[]{:S(2)}) %collective-permute-start.14) | collective-permute-done | bytes 131104 | tf_op jit(solution)/shard_map/ppermute | solution.py:288
  104.7 2.4 %collective-permute-done.13.refs_2_ = f32[128,256]{1,0:T(8,128)S(1)} collective-permute-done((f32[128,256]{1,0:T(8,128)S(1)}, f32[128,256]{1,0:T(8,128)S(1)}, u32[]{:S(2)}, u32[]{:S(2)}) %collective-permute-start.13) | collective-permute-done | bytes 131104 | tf_op jit(solution)/shard_map/ppermute | solution.py:288
  107.1 1.3 %collective-permute-done.12.refs_1_ = f32[128,256]{1,0:T(8,128)S(1)} collective-permute-done((f32[128,256]{1,0:T(8,128)S(1)}, f32[128,256]{1,0:T(8,128)S(1)}, u32[]{:S(2)}, u32[]{:S(2)}) %collective-permute-start.12) | collective-permute-done | bytes 131104 | tf_op jit(solution)/shard_map/ppermute | solution.py:288
  108.5 5.7 %collective-permute-start.15 = (f32[512,256]{1,0:T(8,128)S(1)}, f32[512,256]{1,0:T(8,128)S(1)}, u32[]{:S(2)}, u32[]{:S(2)}) collective-permute-start(f32[512,256]{1,0:T(8,128)S(1)} %shard_map.69.mine), channel_id=1, source_target_pairs={{0,1},{1,0},{2,3},{3,2},{4,5},{5,4},{6,7},{7,6},{8,9},{9,8},{10,11... | collective-permute-start | bytes 1572872 | tf_op jit(solution)/shard_map/ppermute | solution.py:288
  114.3 1.4 %collective-permute-done.15.other = f32[512,256]{1,0:T(8,128)S(1)} collective-permute-done((f32[512,256]{1,0:T(8,128)S(1)}, f32[512,256]{1,0:T(8,128)S(1)}, u32[]{:S(2)}, u32[]{:S(2)}) %collective-permute-start.15) | collective-permute-done | bytes 524320 | tf_op jit(solution)/shard_map/ppermute | solution.py:288
  (33 shorter events, 10.4 us)
Async XLA Ops:
  8.7 4.5 %collective-permute-start.1 = (f32[768,512]{1,0:T(8,128)S(1)}, f32[768,512]{1,0:T(8,128)S(1)}, u32[]{:S(2)}, u32[]{:S(2)}) collective-permute-start(f32[768,512]{1,0:T(8,128)S(1)} %get-tuple-element.29), channel_id=1, source_target_pairs={{0,1},{1,0},{2,3},{3,2},{4,5},{5,4},{6,7},{7,6},{8,9},{9,8},{10,11... | collective-permute-start | bytes 4718600 | tf_op jit(solution)/shard_map/ppermute | solution.py:288
  10.1 3.0 %copy-start = (f32[1024,256]{1,0:T(8,128)S(1)}, f32[1024,256]{1,0:T(8,128)}, u32[]{:S(2)}) copy-start(f32[1024,256]{1,0:T(8,128)} %rf.3) | copy-start | bytes 3145732
  12.6 5.4 %collective-permute-start = (f32[256,512]{1,0:T(8,128)S(1)}, f32[256,512]{1,0:T(8,128)S(1)}, u32[]{:S(2)}, u32[]{:S(2)}) collective-permute-start(f32[256,512]{1,0:T(8,128)S(1)} %get-tuple-element.27), channel_id=1, source_target_pairs={{0,1},{1,0},{2,3},{3,2},{4,5},{5,4},{6,7},{7,6},{8,9},{9,8},{10,11... | collective-permute-start | bytes 1572872 | tf_op jit(solution)/shard_map/ppermute | solution.py:288
  14.1 23.0 %collective-permute-start.5 = (f32[256,512]{1,0:T(8,128)S(1)}, f32[256,512]{1,0:T(8,128)S(1)}, u32[]{:S(2)}, u32[]{:S(2)}) collective-permute-start(f32[256,512]{1,0:T(8,128)S(1)} %get-tuple-element.34), channel_id=1, source_target_pairs={{0,2},{2,4},{4,6},{6,0},{1,3},{3,5},{5,7},{7,1},{8,10},{10,12},{12... | collective-permute-start | bytes 1572872 | tf_op jit(solution)/shard_map/ppermute | solution.py:288
  15.9 21.2 %collective-permute-start.6 = (f32[256,512]{1,0:T(8,128)S(1)}, f32[256,512]{1,0:T(8,128)S(1)}, u32[]{:S(2)}, u32[]{:S(2)}) collective-permute-start(f32[256,512]{1,0:T(8,128)S(1)} %get-tuple-element.35), channel_id=1, source_target_pairs={{0,6},{2,0},{4,2},{6,4},{1,7},{3,1},{5,3},{7,5},{8,14},{10,8},{12,... | collective-permute-start | bytes 1572872 | tf_op jit(solution)/shard_map/ppermute | solution.py:288
  35.6 4.9 %collective-permute-start.4 = (f32[64,128]{1,0:T(8,128)S(1)}, f32[64,128]{1,0:T(8,128)S(1)}, u32[]{:S(2)}, u32[]{:S(2)}) collective-permute-start(f32[64,128]{1,0:T(8,128)S(1)} %shard_map.62.refs_0_), channel_id=1, source_target_pairs={{0,6},{2,0},{4,2},{6,4},{1,7},{3,1},{5,3},{7,5},{8,14},{10,8},{12,... | collective-permute-start | bytes 98312 | tf_op jit(solution)/shard_map/ppermute | solution.py:288
  37.1 12.3 %collective-permute-start.7 = (f32[128,512]{1,0:T(8,128)S(1)}, f32[128,512]{1,0:T(8,128)S(1)}, u32[]{:S(2)}, u32[]{:S(2)}) collective-permute-start(f32[128,512]{1,0:T(8,128)S(1)} %get-tuple-element.38), channel_id=1, source_target_pairs={{0,2},{2,4},{4,6},{6,0},{1,3},{3,5},{5,7},{7,1},{8,10},{10,12},{12... | collective-permute-start | bytes 786440 | tf_op jit(solution)/shard_map/ppermute | solution.py:288
  37.2 12.2 %collective-permute-start.8 = (f32[128,512]{1,0:T(8,128)S(1)}, f32[128,512]{1,0:T(8,128)S(1)}, u32[]{:S(2)}, u32[]{:S(2)}) collective-permute-start(f32[128,512]{1,0:T(8,128)S(1)} %get-tuple-element.39), channel_id=1, source_target_pairs={{0,6},{2,0},{4,2},{6,4},{1,7},{3,1},{5,3},{7,5},{8,14},{10,8},{12,... | collective-permute-start | bytes 786440 | tf_op jit(solution)/shard_map/ppermute | solution.py:288
  39.8 4.6 %collective-permute-start.3 = (f32[64,128]{1,0:T(8,128)S(1)}, f32[64,128]{1,0:T(8,128)S(1)}, u32[]{:S(2)}, u32[]{:S(2)}) collective-permute-start(f32[64,128]{1,0:T(8,128)S(1)} %shard_map.62.refs_0_), channel_id=1, source_target_pairs={{0,4},{2,6},{4,0},{6,2},{1,5},{3,7},{5,1},{7,3},{8,12},{10,14},{12... | collective-permute-start | bytes 98312 | tf_op jit(solution)/shard_map/ppermute | solution.py:288
  39.8 5.1 %collective-permute-start.2 = (f32[64,128]{1,0:T(8,128)S(1)}, f32[64,128]{1,0:T(8,128)S(1)}, u32[]{:S(2)}, u32[]{:S(2)}) collective-permute-start(f32[64,128]{1,0:T(8,128)S(1)} %shard_map.62.refs_0_), channel_id=1, source_target_pairs={{0,2},{2,4},{4,6},{6,0},{1,3},{3,5},{5,7},{7,1},{8,10},{10,12},{12... | collective-permute-start | bytes 98312 | tf_op jit(solution)/shard_map/ppermute | solution.py:288
  45.8 12.9 %all-to-all-start.1 = ((f32[16,64,128]{2,1,0:T(8,128)}), f32[16,64,128]{2,1,0:T(8,128)S(1)}, u32[]{:S(2)}, u32[]{:S(2)}) async-start(f32[16,64,128]{2,1,0:T(8,128)} %shard_map.63), calls=%async_computation.1 | async-start | bytes 1048576 | tf_op jit(solution)/shard_map/all_to_all | solution.py:292
  49.5 12.8 %collective-permute-start.9 = (f32[128,512]{1,0:T(8,128)S(1)}, f32[128,512]{1,0:T(8,128)S(1)}, u32[]{:S(2)}, u32[]{:S(2)}) collective-permute-start(f32[128,512]{1,0:T(8,128)S(1)} %get-tuple-element.41), channel_id=1, source_target_pairs={{0,64},{64,0},{1,65},{65,1},{2,66},{66,2},{3,67},{67,3},{4,68},{68... | collective-permute-start | bytes 786440 | tf_op jit(solution)/shard_map/ppermute | solution.py:288
  62.7 4.0 %collective-permute-start.10 = (f32[128,256]{1,0:T(8,128)S(1)}, f32[128,256]{1,0:T(8,128)S(1)}, u32[]{:S(2)}, u32[]{:S(2)}) collective-permute-start(f32[128,256]{1,0:T(8,128)S(1)} %get-tuple-element.42.zp), channel_id=1, source_target_pairs={{0,1},{1,0},{2,3},{3,2},{4,5},{5,4},{6,7},{7,6},{8,9},{9,8},{10,11... | collective-permute-start | bytes 393224 | tf_op jit(solution)/shard_map/ppermute | solution.py:288
  87.5 26.6 %all-to-all-start.3 = ((f32[64,16,128]{2,1,0:T(8,128)}), f32[64,16,128]{2,1,0:T(8,128)S(1)}, u32[]{:S(2)}, u32[]{:S(2)}) async-start(f32[64,16,128]{2,1,0:T(8,128)} %shard_map.71), calls=%async_computation.3 | async-start | bytes 1048576 | tf_op jit(solution)/shard_map/all_to_all | solution.py:292
  92.2 7.6 %collective-permute-start.11 = (f32[64,256]{1,0:T(8,128)S(1)}, f32[64,256]{1,0:T(8,128)S(1)}, u32[]{:S(2)}, u32[]{:S(2)}) collective-permute-start(f32[64,256]{1,0:T(8,128)S(1)} %get-tuple-element.44.refs_0_), channel_id=1, source_target_pairs={{0,64},{64,0},{1,65},{65,1},{2,66},{66,2},{3,67},{67,3},{4,68},{68... | collective-permute-start | bytes 196616 | tf_op jit(solution)/shard_map/ppermute | solution.py:288
  99.8 4.9 %collective-permute-start.14 = (f32[128,256]{1,0:T(8,128)S(1)}, f32[128,256]{1,0:T(8,128)S(1)}, u32[]{:S(2)}, u32[]{:S(2)}) collective-permute-start(f32[128,256]{1,0:T(8,128)S(1)} %shard_map.68.refs_0_), channel_id=1, source_target_pairs={{0,6},{2,0},{4,2},{6,4},{1,7},{3,1},{5,3},{7,5},{8,14},{10,8},{12,... | collective-permute-start | bytes 393224 | tf_op jit(solution)/shard_map/ppermute | solution.py:288
  101.6 5.5 %collective-permute-start.13 = (f32[128,256]{1,0:T(8,128)S(1)}, f32[128,256]{1,0:T(8,128)S(1)}, u32[]{:S(2)}, u32[]{:S(2)}) collective-permute-start(f32[128,256]{1,0:T(8,128)S(1)} %shard_map.68.refs_0_), channel_id=1, source_target_pairs={{0,4},{2,6},{4,0},{6,2},{1,5},{3,7},{5,1},{7,3},{8,12},{10,14},{12... | collective-permute-start | bytes 393224 | tf_op jit(solution)/shard_map/ppermute | solution.py:288
  102.8 5.6 %collective-permute-start.12 = (f32[128,256]{1,0:T(8,128)S(1)}, f32[128,256]{1,0:T(8,128)S(1)}, u32[]{:S(2)}, u32[]{:S(2)}) collective-permute-start(f32[128,256]{1,0:T(8,128)S(1)} %shard_map.68.refs_0_), channel_id=1, source_target_pairs={{0,2},{2,4},{4,6},{6,0},{1,3},{3,5},{5,7},{7,1},{8,10},{10,12},{12... | collective-permute-start | bytes 393224 | tf_op jit(solution)/shard_map/ppermute | solution.py:288
  108.5 7.2 %collective-permute-start.15 = (f32[512,256]{1,0:T(8,128)S(1)}, f32[512,256]{1,0:T(8,128)S(1)}, u32[]{:S(2)}, u32[]{:S(2)}) collective-permute-start(f32[512,256]{1,0:T(8,128)S(1)} %shard_map.69.mine), channel_id=1, source_target_pairs={{0,1},{1,0},{2,3},{3,2},{4,5},{5,4},{6,7},{7,6},{8,9},{9,8},{10,11... | collective-permute-start | bytes 1572872 | tf_op jit(solution)/shard_map/ppermute | solution.py:288
  114.2 2.6 %collective-permute-start.16 = (f32[128,8,128]{2,1,0:T(8,128)S(1)}, f32[128,8,128]{2,1,0:T(8,128)S(1)}, u32[]{:S(2)}, u32[]{:S(2)}) collective-permute-start(f32[128,8,128]{2,1,0:T(8,128)S(1)} %bitcast.6), channel_id=1, source_target_pairs={{0,1},{1,0},{2,3},{3,2},{4,5},{5,4},{6,7},{7,6},{8,9},{9,8},{10,11... | collective-permute-start | bytes 1572872 | tf_op jit(solution)/shard_map/ppermute | solution.py:288

commit v5 on v4

--- a/solution.py
+++ b/solution.py
@@ -14,7 +14,6 @@
 
 AXES = ("yhi", "ylo", "x", "z", "core")
 PLANE = AXES[:3]
-CHIPS = AXES[:4]
 SUB = 64
 BLOCK = 256
 HALF = RL * RC // 2
@@ -301,13 +300,6 @@
     return exchange(b, PLANE).reshape(tiles.shape)
 
 
-def sum_over_chips(tiles):
-    n = lax.axis_size(CHIPS)
-    v = exchange(tiles.reshape(n, -1, 128), CHIPS)
-    b = call(spread_kernel, shape(*v.shape), [v])
-    return exchange(b, CHIPS).reshape(tiles.shape)
-
-
 def body(weights, col_factor, layer_factor, row_factor):
     weights, col_factor = (pltpu.with_memory_space_constraint(v, pltpu.HBM) for v in (weights, col_factor))
     lf = pltpu.with_memory_space_constraint(layer_factor.T, pltpu.HBM)
@@ -347,7 +339,7 @@
     other = shift(four, "core", 2, 1)
     row_update = call(finish_rows_kernel, shape(8 * rows, RC), [four, other])
 
-    mine = sum_over_chips(ct)
+    mine = sum_over_planes(ct)
     other = shift(mine, "core", 2, 1)
     core_out = call(finish_core_kernel, shape(RC, 2 * HALF), [mine, other])
     return row_update, core_out

time: 119 us -> 118 us (level)
  blocking collectives: 36.5 us -> 32.9 us
  waiting for transfers between devices: 27.7 us -> 30 us
    all_to_all x2, blocking collectives: 36.5 us -> 32.9 us  [exchange(): return lax.all_to_all(v, axes, 0, 0, tiled=True)]
    ppermute x17 -> x20, waiting for transfers between devices: 21.4 us -> 23.7 us  [shift(): return lax.ppermute(v, axis, [(i, (i + by) % size) for i in range(size)])]
    ppermute x17 -> x20, starting transfers between devices: 27.9 us -> 30.1 us  [shift(): return lax.ppermute(v, axis, [(i, (i + by) % size) for i in range(size)])]
    pallas_call x14 -> x15, Pallas kernels: 8.73 us -> 8.72 us  [call(): pl.pallas_call(kernel, out_shape=outs, in_specs=[SMEM] * smem + [VMEM] *...]
  transfers between devices with their start and end apart: 19 -> 22, of which waited for: 11 -> 14; matrix products, arithmetic and copies ran while one was open for 0% -> 0% of each run, Pallas kernels for 5% -> 5%
where the time goes in v5:
time: 118 us
  starting transfers between devices  37.2 us (32%)
  blocking collectives  32.9 us (28%)
  waiting for transfers between devices  30 us (25%)
  Pallas kernels  16.8 us (14%)
    all_to_all x2, blocking collectives, exchange(): return lax.all_to_all(v, axes, 0, 0, tiled=True)  32.9 us
    ppermute x20, starting transfers between devices, shift(): return lax.ppermute(v, axis, [(i, (i + by) % size) for i in range(size)])  30.1 us
    ppermute x20, waiting for transfers between devices, shift(): return lax.ppermute(v, axis, [(i, (i + by) % size) for i in range(size)])  23.7 us
    pallas_call x15, Pallas kernels, call(): pl.pallas_call(kernel, out_shape=outs, in_specs=[SMEM] * smem + [VMEM] *...  8.72 us
    pallas_call x1, Pallas kernels, contract(): pl.pallas_call(contract_kernel, out_shape=(out, out, jax.ShapeDtypeStruct...  8.03 us
    all_to_all x2, starting transfers between devices, exchange(): return lax.all_to_all(v, axes, 0, 0, tiled=True)  7.15 us
    all_to_all x2, waiting for transfers between devices, exchange(): return lax.all_to_all(v, axes, 0, 0, tiled=True)  6.3 us
  transfers between devices with their start and end apart: 22, of which 14 were waited for; matrix products, arithmetic and copies ran while one was open for 0% of the time, Pallas kernels for 5%

profile of v5, /device:TPU:1, one launch (start us, length us, event | category | flops | bytes accessed | tf_op | source)
XLA Modules:
  0.0 117.6 jit_solution(16260472089246998951)
XLA Ops:
  0.6 8.0 %contract.1 = (f32[768,512]{1,0:T(8,128)S(1)}, f32[768,512]{1,0:T(8,128)S(1)}, bf16[4,8,64,1024]{3,2,1,0:T(8,128)(2,1)S(1)}, bf16[1024,256]{1,0:T(8,128)(2,1)S(1)}) custom-call(f32[4,8]{1,0:T(4,128)} %bitcast.10, bf16[8,1024,1024]{2,1,0:T(8,128)(2,1)} %w.1, bf16[1024,256]{1,0:T(8,128)(2,1)} %c.1), custom_call_target="tpu_custom_call" | custom-call | flops 3221225472 | bytes 16777216 | tf_op jit(solution)/shard_map/contract/pallas_call | solution.py:115
  8.7 1.5 %collective-permute-start.1 = (f32[768,512]{1,0:T(8,128)S(1)}, f32[768,512]{1,0:T(8,128)S(1)}, u32[]{:S(2)}, u32[]{:S(2)}) collective-permute-start(f32[768,512]{1,0:T(8,128)S(1)} %get-tuple-element.29), channel_id=1, source_target_pairs={{0,1},{1,0},{2,3},{3,2},{4,5},{5,4},{6,7},{7,6},{8,9},{9,8},{10,11... | collective-permute-start | bytes 4718600 | tf_op jit(solution)/shard_map/ppermute | solution.py:287
  10.1 2.5 %shard_map.59 = (f32[256,512]{1,0:T(8,128)S(1)}, f32[256,512]{1,0:T(8,128)S(1)}) custom-call(f32[4,8]{1,0:T(4,128)} %bitcast.11, bf16[4,8,64,1024]{3,2,1,0:T(8,128)(2,1)S(1)} %get-tuple-element.24.w, bf16[1024,256]{1,0:T(8,128)(2,1)S(1)} %get-tuple-element.25.c), custom_call_target="tpu_custom_call" | custom-call | flops 1073741824 | bytes 1048576 | tf_op jit(solution)/shard_map/pallas_call | solution.py:44
  14.1 1.8 %collective-permute-start.5 = (f32[256,512]{1,0:T(8,128)S(1)}, f32[256,512]{1,0:T(8,128)S(1)}, u32[]{:S(2)}, u32[]{:S(2)}) collective-permute-start(f32[256,512]{1,0:T(8,128)S(1)} %get-tuple-element.34), channel_id=1, source_target_pairs={{0,2},{2,4},{4,6},{6,0},{1,3},{3,5},{5,7},{7,1},{8,10},{10,12},{12... | collective-permute-start | bytes 1572872 | tf_op jit(solution)/shard_map/ppermute | solution.py:287
  15.9 2.2 %collective-permute-start.6 = (f32[256,512]{1,0:T(8,128)S(1)}, f32[256,512]{1,0:T(8,128)S(1)}, u32[]{:S(2)}, u32[]{:S(2)}) collective-permute-start(f32[256,512]{1,0:T(8,128)S(1)} %get-tuple-element.35), channel_id=1, source_target_pairs={{0,6},{2,0},{4,2},{6,4},{1,7},{3,1},{5,3},{7,5},{8,14},{10,8},{12,... | collective-permute-start | bytes 1572872 | tf_op jit(solution)/shard_map/ppermute | solution.py:287
  18.5 17.0 %all_to_all.20.v = f32[16,64,128]{2,1,0:T(8,128)S(1)} all-to-all(f32[16,64,128]{2,1,0:T(8,128)S(1)} %bitcast.8), channel_id=1, replica_groups=mesh['yhi'=2,'ylo'=2,'x'=4,'z'=4,'core'=2] {'yhi','ylo','x'}, dimensions={0} | all-to-all | bytes 1048576 | tf_op jit(solution)/shard_map/all_to_all | solution.py:291
  35.6 1.5 %collective-permute-start.4 = (f32[64,128]{1,0:T(8,128)S(1)}, f32[64,128]{1,0:T(8,128)S(1)}, u32[]{:S(2)}, u32[]{:S(2)}) collective-permute-start(f32[64,128]{1,0:T(8,128)S(1)} %shard_map.62.refs_0_), channel_id=1, source_target_pairs={{0,6},{2,0},{4,2},{6,4},{1,7},{3,1},{5,3},{7,5},{8,14},{10,8},{12,... | collective-permute-start | bytes 98312 | tf_op jit(solution)/shard_map/ppermute | solution.py:287
  37.2 2.6 %collective-permute-start.8 = (f32[128,512]{1,0:T(8,128)S(1)}, f32[128,512]{1,0:T(8,128)S(1)}, u32[]{:S(2)}, u32[]{:S(2)}) collective-permute-start(f32[128,512]{1,0:T(8,128)S(1)} %get-tuple-element.39), channel_id=1, source_target_pairs={{0,6},{2,0},{4,2},{6,4},{1,7},{3,1},{5,3},{7,5},{8,14},{10,8},{12,... | collective-permute-start | bytes 786440 | tf_op jit(solution)/shard_map/ppermute | solution.py:287
  40.4 4.0 %collective-permute-done.3.refs_2_ = f32[64,128]{1,0:T(8,128)S(1)} collective-permute-done((f32[64,128]{1,0:T(8,128)S(1)}, f32[64,128]{1,0:T(8,128)S(1)}, u32[]{:S(2)}, u32[]{:S(2)}) %collective-permute-start.3) | collective-permute-done | bytes 32800 | tf_op jit(solution)/shard_map/ppermute | solution.py:287
  45.8 3.6 %all-to-all-start.1 = ((f32[16,64,128]{2,1,0:T(8,128)}), f32[16,64,128]{2,1,0:T(8,128)S(1)}, u32[]{:S(2)}, u32[]{:S(2)}) async-start(f32[16,64,128]{2,1,0:T(8,128)} %shard_map.63), calls=%async_computation.1 | async-start | bytes 1048576 | tf_op jit(solution)/shard_map/all_to_all | solution.py:291
  49.5 2.9 %collective-permute-start.9 = (f32[128,512]{1,0:T(8,128)S(1)}, f32[128,512]{1,0:T(8,128)S(1)}, u32[]{:S(2)}, u32[]{:S(2)}) collective-permute-start(f32[128,512]{1,0:T(8,128)S(1)} %get-tuple-element.41), channel_id=1, source_target_pairs={{0,64},{64,0},{1,65},{65,1},{2,66},{66,2},{3,67},{67,3},{4,68},{68... | collective-permute-start | bytes 786440 | tf_op jit(solution)/shard_map/ppermute | solution.py:287
  52.4 6.3 %all-to-all-done.1 = f32[16,64,128]{2,1,0:T(8,128)S(1)} async-done(((f32[16,64,128]{2,1,0:T(8,128)}), f32[16,64,128]{2,1,0:T(8,128)S(1)}, u32[]{:S(2)}, u32[]{:S(2)}) %all-to-all-start.1) | async-done | bytes 524320 | tf_op jit(solution)/shard_map/all_to_all | solution.py:291
  58.7 3.6 %collective-permute-done.9.kb = f32[128,512]{1,0:T(8,128)S(1)} collective-permute-done((f32[128,512]{1,0:T(8,128)S(1)}, f32[128,512]{1,0:T(8,128)S(1)}, u32[]{:S(2)}, u32[]{:S(2)}) %collective-permute-start.9) | collective-permute-done | bytes 262176 | tf_op jit(solution)/shard_map/ppermute | solution.py:287
  62.7 3.1 %collective-permute-start.10 = (f32[128,256]{1,0:T(8,128)S(1)}, f32[128,256]{1,0:T(8,128)S(1)}, u32[]{:S(2)}, u32[]{:S(2)}) collective-permute-start(f32[128,256]{1,0:T(8,128)S(1)} %get-tuple-element.42.zp), channel_id=1, source_target_pairs={{0,1},{1,0},{2,3},{3,2},{4,5},{5,4},{6,7},{7,6},{8,9},{9,8},{10,11... | collective-permute-start | bytes 393224 | tf_op jit(solution)/shard_map/ppermute | solution.py:287
  67.1 15.9 %all_to_all.21.v = f32[16,64,128]{2,1,0:T(8,128)S(1)} all-to-all(f32[16,64,128]{2,1,0:T(8,128)S(1)} %bitcast.9), channel_id=1, replica_groups=mesh['yhi'=2,'ylo'=2,'x'=4,'z'=4,'core'=2] {'yhi','ylo','x'}, dimensions={0} | all-to-all | bytes 1048576 | tf_op jit(solution)/shard_map/all_to_all | solution.py:291
  83.1 1.3 %collective-permute-start.18 = (f32[64,128]{1,0:T(8,128)S(1)}, f32[64,128]{1,0:T(8,128)S(1)}, u32[]{:S(2)}, u32[]{:S(2)}) collective-permute-start(f32[64,128]{1,0:T(8,128)S(1)} %shard_map.71.refs_0_), channel_id=1, source_target_pairs={{0,6},{2,0},{4,2},{6,4},{1,7},{3,1},{5,3},{7,5},{8,14},{10,8},{12,... | collective-permute-start | bytes 98312 | tf_op jit(solution)/shard_map/ppermute | solution.py:287
  86.0 2.7 %collective-permute-done.17.refs_2_ = f32[64,128]{1,0:T(8,128)S(1)} collective-permute-done((f32[64,128]{1,0:T(8,128)S(1)}, f32[64,128]{1,0:T(8,128)S(1)}, u32[]{:S(2)}, u32[]{:S(2)}) %collective-permute-start.17) | collective-permute-done | bytes 32800 | tf_op jit(solution)/shard_map/ppermute | solution.py:287
  89.9 3.6 %all-to-all-start.3 = ((f32[16,64,128]{2,1,0:T(8,128)}), f32[16,64,128]{2,1,0:T(8,128)S(1)}, u32[]{:S(2)}, u32[]{:S(2)}) async-start(f32[16,64,128]{2,1,0:T(8,128)} %shard_map.72), calls=%async_computation.3 | async-start | bytes 1048576 | tf_op jit(solution)/shard_map/all_to_all | solution.py:291
  93.5 2.8 %collective-permute-start.11 = (f32[64,256]{1,0:T(8,128)S(1)}, f32[64,256]{1,0:T(8,128)S(1)}, u32[]{:S(2)}, u32[]{:S(2)}) collective-permute-start(f32[64,256]{1,0:T(8,128)S(1)} %get-tuple-element.44.refs_0_), channel_id=1, source_target_pairs={{0,64},{64,0},{1,65},{65,1},{2,66},{66,2},{3,67},{67,3},{4,68},{68... | collective-permute-start | bytes 196616 | tf_op jit(solution)/shard_map/ppermute | solution.py:287
  96.3 3.0 %collective-permute-done.11.refs_1_ = f32[64,256]{1,0:T(8,128)S(1)} collective-permute-done((f32[64,256]{1,0:T(8,128)S(1)}, f32[64,256]{1,0:T(8,128)S(1)}, u32[]{:S(2)}, u32[]{:S(2)}) %collective-permute-start.11) | collective-permute-done | bytes 65568 | tf_op jit(solution)/shard_map/ppermute | solution.py:287
  101.4 2.1 %collective-permute-done.14.refs_3_ = f32[128,256]{1,0:T(8,128)S(1)} collective-permute-done((f32[128,256]{1,0:T(8,128)S(1)}, f32[128,256]{1,0:T(8,128)S(1)}, u32[]{:S(2)}, u32[]{:S(2)}) %collective-permute-start.14) | collective-permute-done | bytes 131104 | tf_op jit(solution)/shard_map/ppermute | solution.py:287
  103.5 2.6 %collective-permute-done.13.refs_2_ = f32[128,256]{1,0:T(8,128)S(1)} collective-permute-done((f32[128,256]{1,0:T(8,128)S(1)}, f32[128,256]{1,0:T(8,128)S(1)}, u32[]{:S(2)}, u32[]{:S(2)}) %collective-permute-start.13) | collective-permute-done | bytes 131104 | tf_op jit(solution)/shard_map/ppermute | solution.py:287
  107.2 6.7 %collective-permute-start.15 = (f32[512,256]{1,0:T(8,128)S(1)}, f32[512,256]{1,0:T(8,128)S(1)}, u32[]{:S(2)}, u32[]{:S(2)}) collective-permute-start(f32[512,256]{1,0:T(8,128)S(1)} %shard_map.69.mine), channel_id=1, source_target_pairs={{0,1},{1,0},{2,3},{3,2},{4,5},{5,4},{6,7},{7,6},{8,9},{9,8},{10,11... | collective-permute-start | bytes 1572872 | tf_op jit(solution)/shard_map/ppermute | solution.py:287
  114.0 1.4 %collective-permute-done.15.other = f32[512,256]{1,0:T(8,128)S(1)} collective-permute-done((f32[512,256]{1,0:T(8,128)S(1)}, f32[512,256]{1,0:T(8,128)S(1)}, u32[]{:S(2)}, u32[]{:S(2)}) %collective-permute-start.15) | collective-permute-done | bytes 524320 | tf_op jit(solution)/shard_map/ppermute | solution.py:287
  (40 shorter events, 14.1 us)
Async XLA Ops:
  8.7 4.5 %collective-permute-start.1 = (f32[768,512]{1,0:T(8,128)S(1)}, f32[768,512]{1,0:T(8,128)S(1)}, u32[]{:S(2)}, u32[]{:S(2)}) collective-permute-start(f32[768,512]{1,0:T(8,128)S(1)} %get-tuple-element.29), channel_id=1, source_target_pairs={{0,1},{1,0},{2,3},{3,2},{4,5},{5,4},{6,7},{7,6},{8,9},{9,8},{10,11... | collective-permute-start | bytes 4718600 | tf_op jit(solution)/shard_map/ppermute | solution.py:287
  10.1 3.0 %copy-start = (f32[1024,256]{1,0:T(8,128)S(1)}, f32[1024,256]{1,0:T(8,128)}, u32[]{:S(2)}) copy-start(f32[1024,256]{1,0:T(8,128)} %rf.3) | copy-start | bytes 3145732
  12.6 5.4 %collective-permute-start = (f32[256,512]{1,0:T(8,128)S(1)}, f32[256,512]{1,0:T(8,128)S(1)}, u32[]{:S(2)}, u32[]{:S(2)}) collective-permute-start(f32[256,512]{1,0:T(8,128)S(1)} %get-tuple-element.27), channel_id=1, source_target_pairs={{0,1},{1,0},{2,3},{3,2},{4,5},{5,4},{6,7},{7,6},{8,9},{9,8},{10,11... | collective-permute-start | bytes 1572872 | tf_op jit(solution)/shard_map/ppermute | solution.py:287
  14.1 23.0 %collective-permute-start.5 = (f32[256,512]{1,0:T(8,128)S(1)}, f32[256,512]{1,0:T(8,128)S(1)}, u32[]{:S(2)}, u32[]{:S(2)}) collective-permute-start(f32[256,512]{1,0:T(8,128)S(1)} %get-tuple-element.34), channel_id=1, source_target_pairs={{0,2},{2,4},{4,6},{6,0},{1,3},{3,5},{5,7},{7,1},{8,10},{10,12},{12... | collective-permute-start | bytes 1572872 | tf_op jit(solution)/shard_map/ppermute | solution.py:287
  15.9 21.2 %collective-permute-start.6 = (f32[256,512]{1,0:T(8,128)S(1)}, f32[256,512]{1,0:T(8,128)S(1)}, u32[]{:S(2)}, u32[]{:S(2)}) collective-permute-start(f32[256,512]{1,0:T(8,128)S(1)} %get-tuple-element.35), channel_id=1, source_target_pairs={{0,6},{2,0},{4,2},{6,4},{1,7},{3,1},{5,3},{7,5},{8,14},{10,8},{12,... | collective-permute-start | bytes 1572872 | tf_op jit(solution)/shard_map/ppermute | solution.py:287
  35.6 4.9 %collective-permute-start.4 = (f32[64,128]{1,0:T(8,128)S(1)}, f32[64,128]{1,0:T(8,128)S(1)}, u32[]{:S(2)}, u32[]{:S(2)}) collective-permute-start(f32[64,128]{1,0:T(8,128)S(1)} %shard_map.62.refs_0_), channel_id=1, source_target_pairs={{0,6},{2,0},{4,2},{6,4},{1,7},{3,1},{5,3},{7,5},{8,14},{10,8},{12,... | collective-permute-start | bytes 98312 | tf_op jit(solution)/shard_map/ppermute | solution.py:287
  37.1 12.3 %collective-permute-start.7 = (f32[128,512]{1,0:T(8,128)S(1)}, f32[128,512]{1,0:T(8,128)S(1)}, u32[]{:S(2)}, u32[]{:S(2)}) collective-permute-start(f32[128,512]{1,0:T(8,128)S(1)} %get-tuple-element.38), channel_id=1, source_target_pairs={{0,2},{2,4},{4,6},{6,0},{1,3},{3,5},{5,7},{7,1},{8,10},{10,12},{12... | collective-permute-start | bytes 786440 | tf_op jit(solution)/shard_map/ppermute | solution.py:287
  37.2 12.2 %collective-permute-start.8 = (f32[128,512]{1,0:T(8,128)S(1)}, f32[128,512]{1,0:T(8,128)S(1)}, u32[]{:S(2)}, u32[]{:S(2)}) collective-permute-start(f32[128,512]{1,0:T(8,128)S(1)} %get-tuple-element.39), channel_id=1, source_target_pairs={{0,6},{2,0},{4,2},{6,4},{1,7},{3,1},{5,3},{7,5},{8,14},{10,8},{12,... | collective-permute-start | bytes 786440 | tf_op jit(solution)/shard_map/ppermute | solution.py:287
  39.8 4.6 %collective-permute-start.3 = (f32[64,128]{1,0:T(8,128)S(1)}, f32[64,128]{1,0:T(8,128)S(1)}, u32[]{:S(2)}, u32[]{:S(2)}) collective-permute-start(f32[64,128]{1,0:T(8,128)S(1)} %shard_map.62.refs_0_), channel_id=1, source_target_pairs={{0,4},{2,6},{4,0},{6,2},{1,5},{3,7},{5,1},{7,3},{8,12},{10,14},{12... | collective-permute-start | bytes 98312 | tf_op jit(solution)/shard_map/ppermute | solution.py:287
  39.8 5.1 %collective-permute-start.2 = (f32[64,128]{1,0:T(8,128)S(1)}, f32[64,128]{1,0:T(8,128)S(1)}, u32[]{:S(2)}, u32[]{:S(2)}) collective-permute-start(f32[64,128]{1,0:T(8,128)S(1)} %shard_map.62.refs_0_), channel_id=1, source_target_pairs={{0,2},{2,4},{4,6},{6,0},{1,3},{3,5},{5,7},{7,1},{8,10},{10,12},{12... | collective-permute-start | bytes 98312 | tf_op jit(solution)/shard_map/ppermute | solution.py:287
  45.8 12.9 %all-to-all-start.1 = ((f32[16,64,128]{2,1,0:T(8,128)}), f32[16,64,128]{2,1,0:T(8,128)S(1)}, u32[]{:S(2)}, u32[]{:S(2)}) async-start(f32[16,64,128]{2,1,0:T(8,128)} %shard_map.63), calls=%async_computation.1 | async-start | bytes 1048576 | tf_op jit(solution)/shard_map/all_to_all | solution.py:291
  49.5 12.8 %collective-permute-start.9 = (f32[128,512]{1,0:T(8,128)S(1)}, f32[128,512]{1,0:T(8,128)S(1)}, u32[]{:S(2)}, u32[]{:S(2)}) collective-permute-start(f32[128,512]{1,0:T(8,128)S(1)} %get-tuple-element.41), channel_id=1, source_target_pairs={{0,64},{64,0},{1,65},{65,1},{2,66},{66,2},{3,67},{67,3},{4,68},{68... | collective-permute-start | bytes 786440 | tf_op jit(solution)/shard_map/ppermute | solution.py:287
  62.7 4.0 %collective-permute-start.10 = (f32[128,256]{1,0:T(8,128)S(1)}, f32[128,256]{1,0:T(8,128)S(1)}, u32[]{:S(2)}, u32[]{:S(2)}) collective-permute-start(f32[128,256]{1,0:T(8,128)S(1)} %get-tuple-element.42.zp), channel_id=1, source_target_pairs={{0,1},{1,0},{2,3},{3,2},{4,5},{5,4},{6,7},{7,6},{8,9},{9,8},{10,11... | collective-permute-start | bytes 393224 | tf_op jit(solution)/shard_map/ppermute | solution.py:287
  83.1 2.8 %collective-permute-start.18 = (f32[64,128]{1,0:T(8,128)S(1)}, f32[64,128]{1,0:T(8,128)S(1)}, u32[]{:S(2)}, u32[]{:S(2)}) collective-permute-start(f32[64,128]{1,0:T(8,128)S(1)} %shard_map.71.refs_0_), channel_id=1, source_target_pairs={{0,6},{2,0},{4,2},{6,4},{1,7},{3,1},{5,3},{7,5},{8,14},{10,8},{12,... | collective-permute-start | bytes 98312 | tf_op jit(solution)/shard_map/ppermute | solution.py:287
  84.4 4.3 %collective-permute-start.17 = (f32[64,128]{1,0:T(8,128)S(1)}, f32[64,128]{1,0:T(8,128)S(1)}, u32[]{:S(2)}, u32[]{:S(2)}) collective-permute-start(f32[64,128]{1,0:T(8,128)S(1)} %shard_map.71.refs_0_), channel_id=1, source_target_pairs={{0,4},{2,6},{4,0},{6,2},{1,5},{3,7},{5,1},{7,3},{8,12},{10,14},{12... | collective-permute-start | bytes 98312 | tf_op jit(solution)/shard_map/ppermute | solution.py:287
  85.1 4.0 %collective-permute-start.16 = (f32[64,128]{1,0:T(8,128)S(1)}, f32[64,128]{1,0:T(8,128)S(1)}, u32[]{:S(2)}, u32[]{:S(2)}) collective-permute-start(f32[64,128]{1,0:T(8,128)S(1)} %shard_map.71.refs_0_), channel_id=1, source_target_pairs={{0,2},{2,4},{4,6},{6,0},{1,3},{3,5},{5,7},{7,1},{8,10},{10,12},{12... | collective-permute-start | bytes 98312 | tf_op jit(solution)/shard_map/ppermute | solution.py:287
  89.9 24.0 %all-to-all-start.3 = ((f32[16,64,128]{2,1,0:T(8,128)}), f32[16,64,128]{2,1,0:T(8,128)S(1)}, u32[]{:S(2)}, u32[]{:S(2)}) async-start(f32[16,64,128]{2,1,0:T(8,128)} %shard_map.72), calls=%async_computation.3 | async-start | bytes 1048576 | tf_op jit(solution)/shard_map/all_to_all | solution.py:291
  93.5 5.8 %collective-permute-start.11 = (f32[64,256]{1,0:T(8,128)S(1)}, f32[64,256]{1,0:T(8,128)S(1)}, u32[]{:S(2)}, u32[]{:S(2)}) collective-permute-start(f32[64,256]{1,0:T(8,128)S(1)} %get-tuple-element.44.refs_0_), channel_id=1, source_target_pairs={{0,64},{64,0},{1,65},{65,1},{2,66},{66,2},{3,67},{67,3},{4,68},{68... | collective-permute-start | bytes 196616 | tf_op jit(solution)/shard_map/ppermute | solution.py:287
  99.3 4.2 %collective-permute-start.14 = (f32[128,256]{1,0:T(8,128)S(1)}, f32[128,256]{1,0:T(8,128)S(1)}, u32[]{:S(2)}, u32[]{:S(2)}) collective-permute-start(f32[128,256]{1,0:T(8,128)S(1)} %shard_map.68.refs_0_), channel_id=1, source_target_pairs={{0,6},{2,0},{4,2},{6,4},{1,7},{3,1},{5,3},{7,5},{8,14},{10,8},{12,... | collective-permute-start | bytes 393224 | tf_op jit(solution)/shard_map/ppermute | solution.py:287
  100.5 5.6 %collective-permute-start.13 = (f32[128,256]{1,0:T(8,128)S(1)}, f32[128,256]{1,0:T(8,128)S(1)}, u32[]{:S(2)}, u32[]{:S(2)}) collective-permute-start(f32[128,256]{1,0:T(8,128)S(1)} %shard_map.68.refs_0_), channel_id=1, source_target_pairs={{0,4},{2,6},{4,0},{6,2},{1,5},{3,7},{5,1},{7,3},{8,12},{10,14},{12... | collective-permute-start | bytes 393224 | tf_op jit(solution)/shard_map/ppermute | solution.py:287
  101.4 5.9 %collective-permute-start.12 = (f32[128,256]{1,0:T(8,128)S(1)}, f32[128,256]{1,0:T(8,128)S(1)}, u32[]{:S(2)}, u32[]{:S(2)}) collective-permute-start(f32[128,256]{1,0:T(8,128)S(1)} %shard_map.68.refs_0_), channel_id=1, source_target_pairs={{0,2},{2,4},{4,6},{6,0},{1,3},{3,5},{5,7},{7,1},{8,10},{10,12},{12... | collective-permute-start | bytes 393224 | tf_op jit(solution)/shard_map/ppermute | solution.py:287
  107.2 8.2 %collective-permute-start.15 = (f32[512,256]{1,0:T(8,128)S(1)}, f32[512,256]{1,0:T(8,128)S(1)}, u32[]{:S(2)}, u32[]{:S(2)}) collective-permute-start(f32[512,256]{1,0:T(8,128)S(1)} %shard_map.69.mine), channel_id=1, source_target_pairs={{0,1},{1,0},{2,3},{3,2},{4,5},{5,4},{6,7},{7,6},{8,9},{9,8},{10,11... | collective-permute-start | bytes 1572872 | tf_op jit(solution)/shard_map/ppermute | solution.py:287
  113.9 2.6 %collective-permute-start.19 = (f32[128,8,128]{2,1,0:T(8,128)S(1)}, f32[128,8,128]{2,1,0:T(8,128)S(1)}, u32[]{:S(2)}, u32[]{:S(2)}) collective-permute-start(f32[128,8,128]{2,1,0:T(8,128)S(1)} %bitcast.6), channel_id=1, source_target_pairs={{0,1},{1,0},{2,3},{3,2},{4,5},{5,4},{6,7},{7,6},{8,9},{9,8},{10,11... | collective-permute-start | bytes 1572872 | tf_op jit(solution)/shard_map/ppermute | solution.py:287

commit v6 on v5

--- a/solution.py
+++ b/solution.py
@@ -240,7 +240,7 @@
             for n in range(2):
                 row = base + (yhi + n) % 2 * (BLOCK // 2)
                 rows = pl.ds(pl.multiple_of(row, quarter), quarter)
-                i = (2 * k + n) * quarter
+                i = (4 * n + k) * quarter
                 out[rows, :] = ref[i : i + quarter, :]
 
 
@@ -332,12 +332,12 @@
     zr = shift(zp, "core", 2, 1)
     z, ct = call(core_kernel, [shape(rows // 2, RC), shape(*ct.shape)], [zp, zr, u])
 
-    zy = shift(z, "yhi", 2, 1)
-    both = call(join_kernel, shape(rows, RC), [z, zy])
-    gathered = [both] + [shift(both, "z", 4, k) for k in (1, 2, 3)]
-    four = call(join_kernel, shape(4 * rows, RC), gathered)
-    other = shift(four, "core", 2, 1)
-    row_update = call(finish_rows_kernel, shape(8 * rows, RC), [four, other])
+    gathered = [z] + [shift(z, "z", 4, k) for k in (1, 2, 3)]
+    four = call(join_kernel, shape(2 * rows, RC), gathered)
+    beyond = shift(four, "yhi", 2, 1)
+    eight = call(join_kernel, shape(4 * rows, RC), [four, beyond])
+    other = shift(eight, "core", 2, 1)
+    row_update = call(finish_rows_kernel, shape(8 * rows, RC), [eight, other])
 
     mine = sum_over_planes(ct)
     other = shift(mine, "core", 2, 1)

time: 118 us -> 117 us (level)
  starting transfers between devices: 37.2 us -> 34.9 us
    ppermute x20, starting transfers between devices: 30.1 us -> 27.8 us  [shift(): return lax.ppermute(v, axis, [(i, (i + by) % size) for i in range(size)])]
where the time goes in v6:
time: 117 us; the launch traced here: 116 us
  starting transfers between devices  34.9 us (30%)
  blocking collectives  32.9 us (28%)
  waiting for transfers between devices  30.9 us (26%)
  Pallas kernels  16.8 us (14%)
    all_to_all x2, blocking collectives, exchange(): return lax.all_to_all(v, axes, 0, 0, tiled=True)  32.9 us
    ppermute x20, starting transfers between devices, shift(): return lax.ppermute(v, axis, [(i, (i + by) % size) for i in range(size)])  27.8 us
    ppermute x20, waiting for transfers between devices, shift(): return lax.ppermute(v, axis, [(i, (i + by) % size) for i in range(size)])  24.6 us
    pallas_call x15, Pallas kernels, call(): pl.pallas_call(kernel, out_shape=outs, in_specs=[SMEM] * smem + [VMEM] *...  8.73 us
    pallas_call x1, Pallas kernels, contract(): pl.pallas_call(contract_kernel, out_shape=(out, out, jax.ShapeDtypeStruct...  8.03 us
    all_to_all x2, starting transfers between devices, exchange(): return lax.all_to_all(v, axes, 0, 0, tiled=True)  7.15 us
    all_to_all x2, waiting for transfers between devices, exchange(): return lax.all_to_all(v, axes, 0, 0, tiled=True)  6.3 us
  transfers between devices with their start and end apart: 22, of which 14 were waited for; matrix products, arithmetic and copies ran while one was open for 0% of the time, Pallas kernels for 5%

profile of v6, /device:TPU:1, one launch (start us, length us, event | category | flops | bytes accessed | tf_op | source)
XLA Modules:
  0.0 116.3 jit_solution(16842021750318049497)
XLA Ops:
  0.6 8.0 %contract.1 = (f32[768,512]{1,0:T(8,128)S(1)}, f32[768,512]{1,0:T(8,128)S(1)}, bf16[4,8,64,1024]{3,2,1,0:T(8,128)(2,1)S(1)}, bf16[1024,256]{1,0:T(8,128)(2,1)S(1)}) custom-call(f32[4,8]{1,0:T(4,128)} %bitcast.10, bf16[8,1024,1024]{2,1,0:T(8,128)(2,1)} %w.1, bf16[1024,256]{1,0:T(8,128)(2,1)} %c.1), custom_call_target="tpu_custom_call" | custom-call | flops 3221225472 | bytes 16777216 | tf_op jit(solution)/shard_map/contract/pallas_call | solution.py:115
  8.7 1.5 %collective-permute-start.1 = (f32[768,512]{1,0:T(8,128)S(1)}, f32[768,512]{1,0:T(8,128)S(1)}, u32[]{:S(2)}, u32[]{:S(2)}) collective-permute-start(f32[768,512]{1,0:T(8,128)S(1)} %get-tuple-element.29), channel_id=1, source_target_pairs={{0,1},{1,0},{2,3},{3,2},{4,5},{5,4},{6,7},{7,6},{8,9},{9,8},{10,11... | collective-permute-start | bytes 4718600 | tf_op jit(solution)/shard_map/ppermute | solution.py:287
  10.1 2.5 %shard_map.59 = (f32[256,512]{1,0:T(8,128)S(1)}, f32[256,512]{1,0:T(8,128)S(1)}) custom-call(f32[4,8]{1,0:T(4,128)} %bitcast.11, bf16[4,8,64,1024]{3,2,1,0:T(8,128)(2,1)S(1)} %get-tuple-element.24.w, bf16[1024,256]{1,0:T(8,128)(2,1)S(1)} %get-tuple-element.25.c), custom_call_target="tpu_custom_call" | custom-call | flops 1073741824 | bytes 1048576 | tf_op jit(solution)/shard_map/pallas_call | solution.py:44
  14.1 1.8 %collective-permute-start.5 = (f32[256,512]{1,0:T(8,128)S(1)}, f32[256,512]{1,0:T(8,128)S(1)}, u32[]{:S(2)}, u32[]{:S(2)}) collective-permute-start(f32[256,512]{1,0:T(8,128)S(1)} %get-tuple-element.34), channel_id=1, source_target_pairs={{0,2},{2,4},{4,6},{6,0},{1,3},{3,5},{5,7},{7,1},{8,10},{10,12},{12... | collective-permute-start | bytes 1572872 | tf_op jit(solution)/shard_map/ppermute | solution.py:287
  15.9 2.2 %collective-permute-start.6 = (f32[256,512]{1,0:T(8,128)S(1)}, f32[256,512]{1,0:T(8,128)S(1)}, u32[]{:S(2)}, u32[]{:S(2)}) collective-permute-start(f32[256,512]{1,0:T(8,128)S(1)} %get-tuple-element.35), channel_id=1, source_target_pairs={{0,6},{2,0},{4,2},{6,4},{1,7},{3,1},{5,3},{7,5},{8,14},{10,8},{12,... | collective-permute-start | bytes 1572872 | tf_op jit(solution)/shard_map/ppermute | solution.py:287
  18.5 17.0 %all_to_all.20.v = f32[16,64,128]{2,1,0:T(8,128)S(1)} all-to-all(f32[16,64,128]{2,1,0:T(8,128)S(1)} %bitcast.8), channel_id=1, replica_groups=mesh['yhi'=2,'ylo'=2,'x'=4,'z'=4,'core'=2] {'yhi','ylo','x'}, dimensions={0} | all-to-all | bytes 1048576 | tf_op jit(solution)/shard_map/all_to_all | solution.py:291
  35.6 1.5 %collective-permute-start.4 = (f32[64,128]{1,0:T(8,128)S(1)}, f32[64,128]{1,0:T(8,128)S(1)}, u32[]{:S(2)}, u32[]{:S(2)}) collective-permute-start(f32[64,128]{1,0:T(8,128)S(1)} %shard_map.62.refs_0_), channel_id=1, source_target_pairs={{0,6},{2,0},{4,2},{6,4},{1,7},{3,1},{5,3},{7,5},{8,14},{10,8},{12,... | collective-permute-start | bytes 98312 | tf_op jit(solution)/shard_map/ppermute | solution.py:287
  37.2 2.6 %collective-permute-start.8 = (f32[128,512]{1,0:T(8,128)S(1)}, f32[128,512]{1,0:T(8,128)S(1)}, u32[]{:S(2)}, u32[]{:S(2)}) collective-permute-start(f32[128,512]{1,0:T(8,128)S(1)} %get-tuple-element.39), channel_id=1, source_target_pairs={{0,6},{2,0},{4,2},{6,4},{1,7},{3,1},{5,3},{7,5},{8,14},{10,8},{12,... | collective-permute-start | bytes 786440 | tf_op jit(solution)/shard_map/ppermute | solution.py:287
  40.4 4.0 %collective-permute-done.3.refs_2_ = f32[64,128]{1,0:T(8,128)S(1)} collective-permute-done((f32[64,128]{1,0:T(8,128)S(1)}, f32[64,128]{1,0:T(8,128)S(1)}, u32[]{:S(2)}, u32[]{:S(2)}) %collective-permute-start.3) | collective-permute-done | bytes 32800 | tf_op jit(solution)/shard_map/ppermute | solution.py:287
  45.8 3.6 %all-to-all-start.1 = ((f32[16,64,128]{2,1,0:T(8,128)}), f32[16,64,128]{2,1,0:T(8,128)S(1)}, u32[]{:S(2)}, u32[]{:S(2)}) async-start(f32[16,64,128]{2,1,0:T(8,128)} %shard_map.63), calls=%async_computation.1 | async-start | bytes 1048576 | tf_op jit(solution)/shard_map/all_to_all | solution.py:291
  49.5 2.9 %collective-permute-start.9 = (f32[128,512]{1,0:T(8,128)S(1)}, f32[128,512]{1,0:T(8,128)S(1)}, u32[]{:S(2)}, u32[]{:S(2)}) collective-permute-start(f32[128,512]{1,0:T(8,128)S(1)} %get-tuple-element.41), channel_id=1, source_target_pairs={{0,64},{64,0},{1,65},{65,1},{2,66},{66,2},{3,67},{67,3},{4,68},{68... | collective-permute-start | bytes 786440 | tf_op jit(solution)/shard_map/ppermute | solution.py:287
  52.4 6.3 %all-to-all-done.1 = f32[16,64,128]{2,1,0:T(8,128)S(1)} async-done(((f32[16,64,128]{2,1,0:T(8,128)}), f32[16,64,128]{2,1,0:T(8,128)S(1)}, u32[]{:S(2)}, u32[]{:S(2)}) %all-to-all-start.1) | async-done | bytes 524320 | tf_op jit(solution)/shard_map/all_to_all | solution.py:291
  58.7 3.6 %collective-permute-done.9.kb = f32[128,512]{1,0:T(8,128)S(1)} collective-permute-done((f32[128,512]{1,0:T(8,128)S(1)}, f32[128,512]{1,0:T(8,128)S(1)}, u32[]{:S(2)}, u32[]{:S(2)}) %collective-permute-start.9) | collective-permute-done | bytes 262176 | tf_op jit(solution)/shard_map/ppermute | solution.py:287
  62.7 3.1 %collective-permute-start.10 = (f32[128,256]{1,0:T(8,128)S(1)}, f32[128,256]{1,0:T(8,128)S(1)}, u32[]{:S(2)}, u32[]{:S(2)}) collective-permute-start(f32[128,256]{1,0:T(8,128)S(1)} %get-tuple-element.42.zp), channel_id=1, source_target_pairs={{0,1},{1,0},{2,3},{3,2},{4,5},{5,4},{6,7},{7,6},{8,9},{9,8},{10,11... | collective-permute-start | bytes 393224 | tf_op jit(solution)/shard_map/ppermute | solution.py:287
  67.1 15.9 %all_to_all.21.v = f32[16,64,128]{2,1,0:T(8,128)S(1)} all-to-all(f32[16,64,128]{2,1,0:T(8,128)S(1)} %bitcast.9), channel_id=1, replica_groups=mesh['yhi'=2,'ylo'=2,'x'=4,'z'=4,'core'=2] {'yhi','ylo','x'}, dimensions={0} | all-to-all | bytes 1048576 | tf_op jit(solution)/shard_map/all_to_all | solution.py:291
  83.1 1.3 %collective-permute-start.18 = (f32[64,128]{1,0:T(8,128)S(1)}, f32[64,128]{1,0:T(8,128)S(1)}, u32[]{:S(2)}, u32[]{:S(2)}) collective-permute-start(f32[64,128]{1,0:T(8,128)S(1)} %shard_map.71.refs_0_), channel_id=1, source_target_pairs={{0,6},{2,0},{4,2},{6,4},{1,7},{3,1},{5,3},{7,5},{8,14},{10,8},{12,... | collective-permute-start | bytes 98312 | tf_op jit(solution)/shard_map/ppermute | solution.py:287
  86.0 2.7 %collective-permute-done.17.refs_2_ = f32[64,128]{1,0:T(8,128)S(1)} collective-permute-done((f32[64,128]{1,0:T(8,128)S(1)}, f32[64,128]{1,0:T(8,128)S(1)}, u32[]{:S(2)}, u32[]{:S(2)}) %collective-permute-start.17) | collective-permute-done | bytes 32800 | tf_op jit(solution)/shard_map/ppermute | solution.py:287
  89.9 3.6 %all-to-all-start.3 = ((f32[16,64,128]{2,1,0:T(8,128)}), f32[16,64,128]{2,1,0:T(8,128)S(1)}, u32[]{:S(2)}, u32[]{:S(2)}) async-start(f32[16,64,128]{2,1,0:T(8,128)} %shard_map.72), calls=%async_computation.3 | async-start | bytes 1048576 | tf_op jit(solution)/shard_map/all_to_all | solution.py:291
  95.5 1.2 collective-permute-done.13.refs_3_
  96.7 2.4 %collective-permute-done.12.refs_2_ = f32[64,256]{1,0:T(8,128)S(1)} collective-permute-done((f32[64,256]{1,0:T(8,128)S(1)}, f32[64,256]{1,0:T(8,128)S(1)}, u32[]{:S(2)}, u32[]{:S(2)}) %collective-permute-start.12) | collective-permute-done | bytes 65568 | tf_op jit(solution)/shard_map/ppermute | solution.py:287
  99.8 2.9 %collective-permute-start.14 = (f32[256,256]{1,0:T(8,128)S(1)}, f32[256,256]{1,0:T(8,128)S(1)}, u32[]{:S(2)}, u32[]{:S(2)}) collective-permute-start(f32[256,256]{1,0:T(8,128)S(1)} %shard_map.68.refs_0_), channel_id=1, source_target_pairs={{0,64},{64,0},{1,65},{65,1},{2,66},{66,2},{3,67},{67,3},{4,68},{68... | collective-permute-start | bytes 786440 | tf_op jit(solution)/shard_map/ppermute | solution.py:287
  102.7 5.6 %collective-permute-done.14.refs_1_ = f32[256,256]{1,0:T(8,128)S(1)} collective-permute-done((f32[256,256]{1,0:T(8,128)S(1)}, f32[256,256]{1,0:T(8,128)S(1)}, u32[]{:S(2)}, u32[]{:S(2)}) %collective-permute-start.14) | collective-permute-done | bytes 262176 | tf_op jit(solution)/shard_map/ppermute | solution.py:287
  108.3 4.3 %collective-permute-start.15 = (f32[512,256]{1,0:T(8,128)S(1)}, f32[512,256]{1,0:T(8,128)S(1)}, u32[]{:S(2)}, u32[]{:S(2)}) collective-permute-start(f32[512,256]{1,0:T(8,128)S(1)} %shard_map.69.mine), channel_id=1, source_target_pairs={{0,1},{1,0},{2,3},{3,2},{4,5},{5,4},{6,7},{7,6},{8,9},{9,8},{10,11... | collective-permute-start | bytes 1572872 | tf_op jit(solution)/shard_map/ppermute | solution.py:287
  112.7 1.4 %collective-permute-done.15.other = f32[512,256]{1,0:T(8,128)S(1)} collective-permute-done((f32[512,256]{1,0:T(8,128)S(1)}, f32[512,256]{1,0:T(8,128)S(1)}, u32[]{:S(2)}, u32[]{:S(2)}) %collective-permute-start.15) | collective-permute-done | bytes 524320 | tf_op jit(solution)/shard_map/ppermute | solution.py:287
  (40 shorter events, 13.7 us)
Async XLA Ops:
  8.7 4.5 %collective-permute-start.1 = (f32[768,512]{1,0:T(8,128)S(1)}, f32[768,512]{1,0:T(8,128)S(1)}, u32[]{:S(2)}, u32[]{:S(2)}) collective-permute-start(f32[768,512]{1,0:T(8,128)S(1)} %get-tuple-element.29), channel_id=1, source_target_pairs={{0,1},{1,0},{2,3},{3,2},{4,5},{5,4},{6,7},{7,6},{8,9},{9,8},{10,11... | collective-permute-start | bytes 4718600 | tf_op jit(solution)/shard_map/ppermute | solution.py:287
  10.1 3.0 %copy-start = (f32[1024,256]{1,0:T(8,128)S(1)}, f32[1024,256]{1,0:T(8,128)}, u32[]{:S(2)}) copy-start(f32[1024,256]{1,0:T(8,128)} %rf.3) | copy-start | bytes 3145732
  12.6 5.4 %collective-permute-start = (f32[256,512]{1,0:T(8,128)S(1)}, f32[256,512]{1,0:T(8,128)S(1)}, u32[]{:S(2)}, u32[]{:S(2)}) collective-permute-start(f32[256,512]{1,0:T(8,128)S(1)} %get-tuple-element.27), channel_id=1, source_target_pairs={{0,1},{1,0},{2,3},{3,2},{4,5},{5,4},{6,7},{7,6},{8,9},{9,8},{10,11... | collective-permute-start | bytes 1572872 | tf_op jit(solution)/shard_map/ppermute | solution.py:287
  14.1 23.0 %collective-permute-start.5 = (f32[256,512]{1,0:T(8,128)S(1)}, f32[256,512]{1,0:T(8,128)S(1)}, u32[]{:S(2)}, u32[]{:S(2)}) collective-permute-start(f32[256,512]{1,0:T(8,128)S(1)} %get-tuple-element.34), channel_id=1, source_target_pairs={{0,2},{2,4},{4,6},{6,0},{1,3},{3,5},{5,7},{7,1},{8,10},{10,12},{12... | collective-permute-start | bytes 1572872 | tf_op jit(solution)/shard_map/ppermute | solution.py:287
  15.9 21.2 %collective-permute-start.6 = (f32[256,512]{1,0:T(8,128)S(1)}, f32[256,512]{1,0:T(8,128)S(1)}, u32[]{:S(2)}, u32[]{:S(2)}) collective-permute-start(f32[256,512]{1,0:T(8,128)S(1)} %get-tuple-element.35), channel_id=1, source_target_pairs={{0,6},{2,0},{4,2},{6,4},{1,7},{3,1},{5,3},{7,5},{8,14},{10,8},{12,... | collective-permute-start | bytes 1572872 | tf_op jit(solution)/shard_map/ppermute | solution.py:287
  35.6 4.9 %collective-permute-start.4 = (f32[64,128]{1,0:T(8,128)S(1)}, f32[64,128]{1,0:T(8,128)S(1)}, u32[]{:S(2)}, u32[]{:S(2)}) collective-permute-start(f32[64,128]{1,0:T(8,128)S(1)} %shard_map.62.refs_0_), channel_id=1, source_target_pairs={{0,6},{2,0},{4,2},{6,4},{1,7},{3,1},{5,3},{7,5},{8,14},{10,8},{12,... | collective-permute-start | bytes 98312 | tf_op jit(solution)/shard_map/ppermute | solution.py:287
  37.1 12.3 %collective-permute-start.7 = (f32[128,512]{1,0:T(8,128)S(1)}, f32[128,512]{1,0:T(8,128)S(1)}, u32[]{:S(2)}, u32[]{:S(2)}) collective-permute-start(f32[128,512]{1,0:T(8,128)S(1)} %get-tuple-element.38), channel_id=1, source_target_pairs={{0,2},{2,4},{4,6},{6,0},{1,3},{3,5},{5,7},{7,1},{8,10},{10,12},{12... | collective-permute-start | bytes 786440 | tf_op jit(solution)/shard_map/ppermute | solution.py:287
  37.2 12.2 %collective-permute-start.8 = (f32[128,512]{1,0:T(8,128)S(1)}, f32[128,512]{1,0:T(8,128)S(1)}, u32[]{:S(2)}, u32[]{:S(2)}) collective-permute-start(f32[128,512]{1,0:T(8,128)S(1)} %get-tuple-element.39), channel_id=1, source_target_pairs={{0,6},{2,0},{4,2},{6,4},{1,7},{3,1},{5,3},{7,5},{8,14},{10,8},{12,... | collective-permute-start | bytes 786440 | tf_op jit(solution)/shard_map/ppermute | solution.py:287
  39.8 4.6 %collective-permute-start.3 = (f32[64,128]{1,0:T(8,128)S(1)}, f32[64,128]{1,0:T(8,128)S(1)}, u32[]{:S(2)}, u32[]{:S(2)}) collective-permute-start(f32[64,128]{1,0:T(8,128)S(1)} %shard_map.62.refs_0_), channel_id=1, source_target_pairs={{0,4},{2,6},{4,0},{6,2},{1,5},{3,7},{5,1},{7,3},{8,12},{10,14},{12... | collective-permute-start | bytes 98312 | tf_op jit(solution)/shard_map/ppermute | solution.py:287
  39.8 5.1 %collective-permute-start.2 = (f32[64,128]{1,0:T(8,128)S(1)}, f32[64,128]{1,0:T(8,128)S(1)}, u32[]{:S(2)}, u32[]{:S(2)}) collective-permute-start(f32[64,128]{1,0:T(8,128)S(1)} %shard_map.62.refs_0_), channel_id=1, source_target_pairs={{0,2},{2,4},{4,6},{6,0},{1,3},{3,5},{5,7},{7,1},{8,10},{10,12},{12... | collective-permute-start | bytes 98312 | tf_op jit(solution)/shard_map/ppermute | solution.py:287
  45.8 12.9 %all-to-all-start.1 = ((f32[16,64,128]{2,1,0:T(8,128)}), f32[16,64,128]{2,1,0:T(8,128)S(1)}, u32[]{:S(2)}, u32[]{:S(2)}) async-start(f32[16,64,128]{2,1,0:T(8,128)} %shard_map.63), calls=%async_computation.1 | async-start | bytes 1048576 | tf_op jit(solution)/shard_map/all_to_all | solution.py:291
  49.5 12.8 %collective-permute-start.9 = (f32[128,512]{1,0:T(8,128)S(1)}, f32[128,512]{1,0:T(8,128)S(1)}, u32[]{:S(2)}, u32[]{:S(2)}) collective-permute-start(f32[128,512]{1,0:T(8,128)S(1)} %get-tuple-element.41), channel_id=1, source_target_pairs={{0,64},{64,0},{1,65},{65,1},{2,66},{66,2},{3,67},{67,3},{4,68},{68... | collective-permute-start | bytes 786440 | tf_op jit(solution)/shard_map/ppermute | solution.py:287
  62.7 4.0 %collective-permute-start.10 = (f32[128,256]{1,0:T(8,128)S(1)}, f32[128,256]{1,0:T(8,128)S(1)}, u32[]{:S(2)}, u32[]{:S(2)}) collective-permute-start(f32[128,256]{1,0:T(8,128)S(1)} %get-tuple-element.42.zp), channel_id=1, source_target_pairs={{0,1},{1,0},{2,3},{3,2},{4,5},{5,4},{6,7},{7,6},{8,9},{9,8},{10,11... | collective-permute-start | bytes 393224 | tf_op jit(solution)/shard_map/ppermute | solution.py:287
  83.1 2.8 %collective-permute-start.18 = (f32[64,128]{1,0:T(8,128)S(1)}, f32[64,128]{1,0:T(8,128)S(1)}, u32[]{:S(2)}, u32[]{:S(2)}) collective-permute-start(f32[64,128]{1,0:T(8,128)S(1)} %shard_map.71.refs_0_), channel_id=1, source_target_pairs={{0,6},{2,0},{4,2},{6,4},{1,7},{3,1},{5,3},{7,5},{8,14},{10,8},{12,... | collective-permute-start | bytes 98312 | tf_op jit(solution)/shard_map/ppermute | solution.py:287
  84.4 4.3 %collective-permute-start.17 = (f32[64,128]{1,0:T(8,128)S(1)}, f32[64,128]{1,0:T(8,128)S(1)}, u32[]{:S(2)}, u32[]{:S(2)}) collective-permute-start(f32[64,128]{1,0:T(8,128)S(1)} %shard_map.71.refs_0_), channel_id=1, source_target_pairs={{0,4},{2,6},{4,0},{6,2},{1,5},{3,7},{5,1},{7,3},{8,12},{10,14},{12... | collective-permute-start | bytes 98312 | tf_op jit(solution)/shard_map/ppermute | solution.py:287
  85.1 4.0 %collective-permute-start.16 = (f32[64,128]{1,0:T(8,128)S(1)}, f32[64,128]{1,0:T(8,128)S(1)}, u32[]{:S(2)}, u32[]{:S(2)}) collective-permute-start(f32[64,128]{1,0:T(8,128)S(1)} %shard_map.71.refs_0_), channel_id=1, source_target_pairs={{0,2},{2,4},{4,6},{6,0},{1,3},{3,5},{5,7},{7,1},{8,10},{10,12},{12... | collective-permute-start | bytes 98312 | tf_op jit(solution)/shard_map/ppermute | solution.py:287
  89.9 22.7 %all-to-all-start.3 = ((f32[16,64,128]{2,1,0:T(8,128)}), f32[16,64,128]{2,1,0:T(8,128)S(1)}, u32[]{:S(2)}, u32[]{:S(2)}) async-start(f32[16,64,128]{2,1,0:T(8,128)} %shard_map.72), calls=%async_computation.3 | async-start | bytes 1048576 | tf_op jit(solution)/shard_map/all_to_all | solution.py:291
  93.5 3.2 %collective-permute-start.13 = (f32[64,256]{1,0:T(8,128)S(1)}, f32[64,256]{1,0:T(8,128)S(1)}, u32[]{:S(2)}, u32[]{:S(2)}) collective-permute-start(f32[64,256]{1,0:T(8,128)S(1)} %get-tuple-element.44.refs_0_), channel_id=1, source_target_pairs={{0,6},{2,0},{4,2},{6,4},{1,7},{3,1},{5,3},{7,5},{8,14},{10,8},{12,... | collective-permute-start | bytes 196616 | tf_op jit(solution)/shard_map/ppermute | solution.py:287
  94.5 4.6 %collective-permute-start.12 = (f32[64,256]{1,0:T(8,128)S(1)}, f32[64,256]{1,0:T(8,128)S(1)}, u32[]{:S(2)}, u32[]{:S(2)}) collective-permute-start(f32[64,256]{1,0:T(8,128)S(1)} %get-tuple-element.44.refs_0_), channel_id=1, source_target_pairs={{0,4},{2,6},{4,0},{6,2},{1,5},{3,7},{5,1},{7,3},{8,12},{10,14},{12... | collective-permute-start | bytes 196616 | tf_op jit(solution)/shard_map/ppermute | solution.py:287
  95.4 4.4 %collective-permute-start.11 = (f32[64,256]{1,0:T(8,128)S(1)}, f32[64,256]{1,0:T(8,128)S(1)}, u32[]{:S(2)}, u32[]{:S(2)}) collective-permute-start(f32[64,256]{1,0:T(8,128)S(1)} %get-tuple-element.44.refs_0_), channel_id=1, source_target_pairs={{0,2},{2,4},{4,6},{6,0},{1,3},{3,5},{5,7},{7,1},{8,10},{10,12},{12... | collective-permute-start | bytes 196616 | tf_op jit(solution)/shard_map/ppermute | solution.py:287
  99.8 8.4 %collective-permute-start.14 = (f32[256,256]{1,0:T(8,128)S(1)}, f32[256,256]{1,0:T(8,128)S(1)}, u32[]{:S(2)}, u32[]{:S(2)}) collective-permute-start(f32[256,256]{1,0:T(8,128)S(1)} %shard_map.68.refs_0_), channel_id=1, source_target_pairs={{0,64},{64,0},{1,65},{65,1},{2,66},{66,2},{3,67},{67,3},{4,68},{68... | collective-permute-start | bytes 786440 | tf_op jit(solution)/shard_map/ppermute | solution.py:287
  108.3 5.8 %collective-permute-start.15 = (f32[512,256]{1,0:T(8,128)S(1)}, f32[512,256]{1,0:T(8,128)S(1)}, u32[]{:S(2)}, u32[]{:S(2)}) collective-permute-start(f32[512,256]{1,0:T(8,128)S(1)} %shard_map.69.mine), channel_id=1, source_target_pairs={{0,1},{1,0},{2,3},{3,2},{4,5},{5,4},{6,7},{7,6},{8,9},{9,8},{10,11... | collective-permute-start | bytes 1572872 | tf_op jit(solution)/shard_map/ppermute | solution.py:287
  112.6 2.6 %collective-permute-start.19 = (f32[128,8,128]{2,1,0:T(8,128)S(1)}, f32[128,8,128]{2,1,0:T(8,128)S(1)}, u32[]{:S(2)}, u32[]{:S(2)}) collective-permute-start(f32[128,8,128]{2,1,0:T(8,128)S(1)} %bitcast.6), channel_id=1, source_target_pairs={{0,1},{1,0},{2,3},{3,2},{4,5},{5,4},{6,7},{7,6},{8,9},{9,8},{10,11... | collective-permute-start | bytes 1572872 | tf_op jit(solution)/shard_map/ppermute | solution.py:287
